TPU v7x, 128 devices: a whole 4x4x4 slice. The times are simulated.
128 devices in a mesh: space: 32 (over z, x, core), rep: 4 (over y).
Axes of the slice: x: 4, y: 4, z: 4, core: 2. Of those that a mesh axis runs over, the one named last changes fastest.
Arguments:
- voxels: bfloat16 [4, 128, 512, 128], P('rep', 'space'), may hold values from -6 to 6
- occupied: int32 [4, 128], P('rep', 'space'), may hold values from 0 to 1, as said below
- neighbours: int32 [4, 128, 6], P('rep', 'space'), may hold values from -1 to 127, as said below
- first_weight: bfloat16 [27, 128, 128], replicated, may hold values from -0.109375 to 0.109375
- second_weight: bfloat16 [27, 128, 128], replicated, may hold values from -0.109375 to 0.109375
- cotangent: bfloat16 [4, 128, 512, 128], P('rep', 'space'), may hold values from -0.01171875 to 0.01171875
Outputs:
- output_field: bfloat16 [4, 128, 512, 128], P('rep', 'space')
- first_grad: float32 [27, 128, 128], replicated
- second_grad: float32 [27, 128, 128], replicated
Inputs may be any that keep to these rules, and one draw needn't show every extreme that they name: In every slab each device of space holds n blocks in its first n slots (occupied 1) and padding after them, n from 1 to 4; in some slab the last device holds 4. `neighbours`: device s of space owns one tile of 2 x 2 x 1 block positions. With h = log2(32) - 1, bit h of s is the tile's third coordinate (the slab is two tiles deep in the third dimension), and below it bit 2k of s is bit k of the tile's first coordinate and bit 2k+1 of s bit k of its second. Entry f names owner * 4 + slot of the occupied block of the same slab across face f (-x, +x, -y, +y, -z, +z), or -1 where there is none or the slot is padding; if a names b across face f, b names a across the opposite face.
All inputs are finite; a program needn't handle non-finite values.
Results may differ from a plain program's by a relative error of at most 0.0031.
Values may be sent and summed in bfloat16 or wider, within the bound.
No kernel may reach another device: no remote copies, remote signals or barrier semaphores. Data moves between devices by JAX's collectives and lax.ppermute only.
A program may use at most 128 MiB of HBM per device.

v0:
```python
import functools

import jax
import jax.numpy as jnp
from jax import lax
from jax.experimental import pallas as pl
from jax.experimental.pallas import tpu as pltpu
from jax.sharding import PartitionSpec as P

BF = jnp.bfloat16
F32 = jnp.float32
VMEM = pl.BlockSpec(memory_space=pltpu.VMEM)
SMEM = pl.BlockSpec(memory_space=pltpu.SMEM)
PARAMS = pltpu.CompilerParams(vmem_limit_bytes=56 << 20)
ROWS = 3456
CHUNK = 56


def tile_of(s):
    return (s & 1) | ((s >> 1) & 2), ((s >> 1) & 1) | ((s >> 2) & 2), s >> 4


def owner_of(a, b, z):
    return (a & 1) | ((b & 1) << 1) | ((a >> 1) << 2) | ((b >> 1) << 3) | (z << 4)


def swaps(kind):
    pairs = []
    for s in range(32):
        a, b, z = tile_of(s)
        if kind == "xe":
            a ^= 1
        elif kind == "ye":
            b ^= 1
        elif kind == "z":
            z ^= 1
        elif kind == "xo":
            if a not in (1, 2):
                continue
            a = 3 - a
        elif kind == "yo":
            if b not in (1, 2):
                continue
            b = 3 - b
        pairs.append((s, owner_of(a, b, z)))
    return pairs


SWAPS = tuple(swaps(kind) for kind in ("xe", "xo", "ye", "yo", "z"))


def exchange(sent):
    return tuple(lax.ppermute(a, "space", pairs) for a, pairs in zip(sent, SWAPS))


def remote_links(links, face, device):
    found = []
    for n in range(4):
        link = links[0, n, face]
        valid = link >= 0
        found.append((link, valid, valid & ((link >> 2) != device)))
    return found


def face_of(x, n, axis, layer):
    if axis == 0:
        return x[n, pl.ds(layer * 64, 64), :]
    if axis == 1:
        return jnp.concatenate([x[n, pl.ds(i * 64 + layer * 8, 8), :] for i in range(8)], axis=0)
    return x[n, pl.ds(layer, 64, stride=8), :]


def pack_faces(fields, links, device, sends):
    bits = (device & 1, (device >> 1) & 1, device >> 4)
    for axis in range(3):
        width = 4 if axis == 2 else 2
        for odd in range(1 if axis == 2 else 2):
            send = sends[2 * axis + odd]
            side = bits[axis] ^ (1 - odd)
            rank = jnp.int32(0)
            for n in range(4):
                link = links[0, n, 2 * axis + side]
                remote = (link >= 0) & ((link >> 2) != device)
                at = rank

                @pl.when(remote)
                def _():
                    for a, x in enumerate(fields):
                        row = pl.multiple_of((a * width + at) * 64, 64)
                        send[pl.ds(row, 64), :] = face_of(x, n, axis, side * 7).astype(BF)

                rank = rank + remote.astype(jnp.int32)


def take_faces(x, links, device, got, field, faces):
    bits = (device & 1, (device >> 1) & 1, device >> 4)
    for axis in range(3):
        width = 4 if axis == 2 else 2
        for side in range(2):
            found = remote_links(links, 2 * axis + side, device)
            for n in range(4):
                link, valid, remote = found[n]
                slot = link & 3
                rank = jnp.int32(0)
                for q in range(4):
                    if q != n:
                        lower = found[q][2] & ((found[q][0] & 3) < slot)
                        rank = rank + lower.astype(jnp.int32)
                rank = jnp.minimum(jnp.where(remote, rank, 0), width - 1)
                row = pl.ds(pl.multiple_of((field * width + rank) * 64, 64), 64)
                if axis == 2:
                    far = got[4][row, :].astype(F32)
                    value = jnp.where(remote, far, 0.0)
                else:
                    even = (bits[axis] ^ side) == 1
                    far = jnp.where(even, got[2 * axis][row, :], got[2 * axis + 1][row, :])
                    near = face_of(x, jnp.where(valid, slot, 0), axis, 0 if side else 7)
                    value = jnp.where(valid, jnp.where(remote, far.astype(F32), near), 0.0)
                faces[axis][n, side] = value


def build(wide, odd, x, faces):
    k_of = lax.broadcasted_iota(jnp.int32, (10, 8, 128), 1)
    at_low, at_high = k_of == 0, k_of == 7
    none = jnp.zeros((1, 8, 128), F32)

    def block(n, carry):
        for i in range(10):
            if i in (0, 9):
                core = faces[0][n, 0 if i == 0 else 1].reshape(8, 8, 128)
                layers = jnp.concatenate((none, core, none), axis=0)
                low, high = jnp.zeros_like(layers), jnp.zeros_like(layers)
            else:
                at = pl.ds((i - 1) * 8, 8)
                core = x[n, pl.ds((i - 1) * 64, 64), :].reshape(8, 8, 128)
                layers = jnp.concatenate(
                    (faces[1][n, 0, at, :][None], core, faces[1][n, 1, at, :][None]), axis=0
                )
                low, high = (
                    jnp.concatenate(
                        (none, jnp.broadcast_to(faces[2][n, side, at, :][:, None, :], (8, 8, 128)), none),
                        axis=0,
                    )
                    for side in range(2)
                )
            before = jnp.where(at_low, low, pltpu.roll(layers, 1, 1))
            after = jnp.where(at_high, high, pltpu.roll(layers, 7, 1))
            for tk, shifted in enumerate((before, layers, after)):
                wide[tk, n, i] = shifted.reshape(80, 128).astype(BF)
                odd[tk, n, i] = shifted[1:9].reshape(64, 128).astype(BF)
        return carry

    lax.fori_loop(0, 4, block, 0)


def tap(wide, odd, n, i, tj, tk):
    if tj == 1:
        return odd[tk, n, i]
    return wide[tk, n, i, pl.ds(8 * tj, 64), :]


def convolve(wide, odd, pair_weights, n):
    columns = []
    for layer in range(4):
        for tj in range(3):
            for tk in range(3):
                columns.append(
                    jnp.concatenate([tap(wide, odd, n, 2 * p + layer, tj, tk) for p in range(4)], axis=0)
                )
    group = jnp.concatenate(columns, axis=1)
    both = jnp.dot(group, pair_weights[...], preferred_element_type=F32)
    rows = []
    for p in range(4):
        for half in range(2):
            rows.append(both[p * 64 : (p + 1) * 64, half * 128 : (half + 1) * 128])
    return jnp.concatenate(rows, axis=0)


def lay_weights(pair_weights, block_of):
    pair_weights[pl.ds(3456, 1152), pl.ds(0, 128)] = jnp.zeros((1152, 128), BF)
    pair_weights[pl.ds(0, 1152), pl.ds(128, 128)] = jnp.zeros((1152, 128), BF)
    for t in range(27):
        block = block_of(t)
        pair_weights[pl.ds(t * 128, 128), pl.ds(0, 128)] = block
        pair_weights[pl.ds((t + 9) * 128, 128), pl.ds(128, 128)] = block


def weight_terms(wide, odd, turned, put):
    for ti in range(3):
        columns = []
        for tj in range(3):
            for tk in range(3):
                columns.append(
                    jnp.concatenate(
                        [tap(wide, odd, n, i + ti, tj, tk) for n in range(4) for i in range(8)], axis=0
                    )
                )
        total = jnp.dot(turned[...], jnp.concatenate(columns, axis=1), preferred_element_type=F32)
        for q in range(9):
            put(9 * ti + q, total[:, q * 128 : (q + 1) * 128])


def load_masked(x, source, occupied):
    for n in range(4):
        keep = occupied[0, n].astype(F32)
        x[n] = source[0, n].astype(F32) * keep


def first_faces_kernel(voxels, cotangent, links, occupied, *rest):
    sends, (x, g) = rest[:5], rest[5:]
    device = lax.axis_index("space")
    load_masked(x, voxels, occupied)
    load_masked(g, cotangent, occupied)
    pack_faces((x, g), links, device, sends)


def hidden_faces_kernel(hidden, links, *rest):
    sends, (x,) = rest[:5], rest[5:]
    device = lax.axis_index("space")
    for n in range(4):
        x[n] = hidden[n].astype(F32)
    pack_faces((x,), links, device, sends)


def main_kernel(
    voxels, cotangent, links, occupied, first_weight, second_weight, g0, g1, g2, g3, g4,
    hidden, terms,
    x, fx, fy, fz, wide, odd, wide_grad, odd_grad, pair_weights, slope, hidden_turned, grad_turned,
):
    device = lax.axis_index("space")
    got = (g0, g1, g2, g3, g4)
    faces = (fx, fy, fz)
    load_masked(x, voxels, occupied)
    take_faces(x, links, device, got, 0, faces)
    build(wide, odd, x, faces)
    lay_weights(pair_weights, lambda t: first_weight[t])

    def forward(n, carry):
        keep = occupied[0, n].astype(F32)
        first = convolve(wide, odd, pair_weights, n)
        sigma = jax.nn.sigmoid(first)
        value = (first * sigma * keep).astype(BF)
        hidden[n] = value
        hidden_turned[:, pl.ds(pl.multiple_of(n * 512, 512), 512)] = value.T
        slope[n] = sigma * (1.0 + first * (1.0 - sigma)) * keep
        return carry

    lax.fori_loop(0, 4, forward, 0)

    load_masked(x, cotangent, occupied)
    take_faces(x, links, device, got, 1, faces)
    build(wide_grad, odd_grad, x, faces)
    lay_weights(pair_weights, lambda t: second_weight[26 - t].T)

    def put_second(t, block):
        terms[pl.ds(ROWS + (26 - t) * 128, 128), :] = block.astype(BF)

    weight_terms(wide_grad, odd_grad, hidden_turned, put_second)

    def backward(n, carry):
        grad = convolve(wide_grad, odd_grad, pair_weights, n) * slope[n]
        grad_turned[:, pl.ds(pl.multiple_of(n * 512, 512), 512)] = grad.astype(BF).T
        return carry

    lax.fori_loop(0, 4, backward, 0)

    def put_first(t, block):
        terms[pl.ds(t * 128, 128), :] = block.T.astype(BF)

    weight_terms(wide, odd, grad_turned, put_first)
    terms[pl.ds(2 * ROWS, 256), :] = jnp.zeros((256, 128), BF)


def last_kernel(
    voxels, hidden, links, occupied, second_weight, g0, g1, g2, g3, g4,
    output,
    x, fx, fy, fz, wide, odd, pair_weights,
):
    device = lax.axis_index("space")
    faces = (fx, fy, fz)
    for n in range(4):
        x[n] = hidden[n].astype(F32)
    take_faces(x, links, device, (g0, g1, g2, g3, g4), 0, faces)
    build(wide, odd, x, faces)
    lay_weights(pair_weights, lambda t: second_weight[t])

    def forward(n, carry):
        keep = occupied[0, n].astype(F32)
        second = convolve(wide, odd, pair_weights, n)
        output[0, n] = ((voxels[0, n].astype(F32) * keep + second) * keep).astype(BF)
        return carry

    lax.fori_loop(0, 4, forward, 0)


def sum_kernel(chunks, spread):
    total = chunks[0].astype(F32)

    def add(p, total):
        return total + chunks[p].astype(F32)

    total = lax.fori_loop(1, 128, add, total, unroll=8).astype(BF)

    def put(p, carry):
        spread[p] = total
        return carry

    lax.fori_loop(0, 128, put, 0, unroll=8)


def send_shapes(fields):
    return tuple(jax.ShapeDtypeStruct((fields * w * 64, 128), BF) for w in (2, 2, 2, 2, 4))


def call(kernel, outs, ins, scratch, flops=0, nbytes=0):
    specs = [SMEM if a.dtype == jnp.int32 else VMEM for a in ins]
    many = isinstance(outs, tuple)
    return pl.pallas_call(
        kernel,
        out_shape=outs,
        in_specs=specs,
        out_specs=tuple(VMEM for _ in outs) if many else VMEM,
        scratch_shapes=scratch,
        compiler_params=PARAMS,
        cost_estimate=pl.CostEstimate(flops=flops, bytes_accessed=nbytes, transcendentals=0),
    )(*ins)


def local(voxels, occupied, neighbours, first_weight, second_weight, cotangent):
    field = pltpu.VMEM((4, 512, 128), F32)
    sides = [pltpu.VMEM((4, 2, 64, 128), F32)] * 3
    padded = [pltpu.VMEM((3, 4, 10, 80, 128), BF), pltpu.VMEM((3, 4, 10, 64, 128), BF)]
    pairs = pltpu.VMEM((4608, 256), BF)
    turned = pltpu.VMEM((128, 2048), BF)

    sent = call(
        first_faces_kernel,
        send_shapes(2),
        (voxels, cotangent, neighbours, occupied),
        [field, field],
        nbytes=2 << 20,
    )
    got = exchange(sent)
    hidden, terms = call(
        main_kernel,
        (jax.ShapeDtypeStruct((4, 512, 128), BF), jax.ShapeDtypeStruct((128 * CHUNK, 128), BF)),
        (voxels, cotangent, neighbours, occupied, first_weight, second_weight) + got,
        [field] + sides + padded + padded + [pairs, field, turned, turned],
        flops=8 << 30,
        nbytes=8 << 20,
    )
    parts = lax.all_to_all(
        terms.reshape(128, CHUNK, 128), ("space", "rep"), split_axis=0, concat_axis=0, tiled=True
    )
    sent = call(hidden_faces_kernel, send_shapes(1), (hidden, neighbours), [field], nbytes=1 << 20)
    got = exchange(sent)
    output = call(
        last_kernel,
        jax.ShapeDtypeStruct((1, 4, 512, 128), BF),
        (voxels, hidden, neighbours, occupied, second_weight) + got,
        [field] + sides + padded + [pairs],
        flops=3 << 30,
        nbytes=4 << 20,
    )
    spread = call(
        sum_kernel, jax.ShapeDtypeStruct((128, CHUNK, 128), BF), (parts,), [], nbytes=4 << 20
    )
    whole = lax.all_to_all(spread, ("space", "rep"), split_axis=0, concat_axis=0, tiled=True)
    whole = whole.reshape(128 * CHUNK, 128)
    first_grad = whole[:ROWS].reshape(27, 128, 128).astype(F32)
    second_grad = whole[ROWS : 2 * ROWS].reshape(27, 128, 128).astype(F32)
    return output, first_grad, second_grad


def solution(mesh):
    placed = (
        P("rep", "space", None, None),
        P("rep", "space"),
        P("rep", "space", None),
        P(),
        P(),
        P("rep", "space", None, None),
    )
    return jax.shard_map(
        local,
        mesh=mesh,
        in_specs=placed,
        out_specs=(P("rep", "space", None, None), P(), P()),
        check_vma=False,
    )
```

profile of v0, /device:TPU:1, one launch (start us, length us, event | category | flops | bytes accessed | tf_op | source)
XLA Modules:
  0.0 114.6 jit_solution(16533044565960825612)
XLA Ops:
  0.6 2.3 %shard_map.85 = (bf16[256,128]{1,0:T(8,128)(2,1)}, bf16[256,128]{1,0:T(8,128)(2,1)}, bf16[256,128]{1,0:T(8,128)(2,1)}, bf16[256,128]{1,0:T(8,128)(2,1)}, bf16[512,128]{1,0:T(8,128)(2,1)}) custom-call(bf16[1,4,512,128]{3,2,1,0:T(8,128)(2,1)} %voxels.5, bf16[1,4,512,128]{3,2,1,0:T(8,128)(2,1)} %cotangent.3, s32[1,4,6]{2,1,0:T(4,128)} %links.7, s32[1,4]{1,0:T(1,128)} %occupied.5), custom_call_target="tpu_custom_call" | custom-call | bytes 2097152 | tf_op jit(solution)/shard_map/pallas_call | solution.py:318
  3.0 4.4 %collective-permute-start.4 = (bf16[512,128]{1,0:T(8,128)(2,1)}, bf16[512,128]{1,0:T(8,128)(2,1)S(1)}, u32[]{:S(2)}, u32[]{:S(2)}) collective-permute-start(bf16[512,128]{1,0:T(8,128)(2,1)} %get-tuple-element.19), channel_id=1, source_target_pairs={{0,64},{4,68},{8,72},{12,76},{16,80},{20,84},{24,88},{28,92},{32,9... | collective-permute-start | bytes 393224 | tf_op jit(solution)/shard_map/ppermute | solution.py:53
  7.4 1.0 collective-permute-start
  8.4 4.5 %collective-permute-start.1 = (bf16[256,128]{1,0:T(8,128)(2,1)}, bf16[256,128]{1,0:T(8,128)(2,1)S(1)}, u32[]{:S(2)}, u32[]{:S(2)}) collective-permute-start(bf16[256,128]{1,0:T(8,128)(2,1)} %get-tuple-element.16), channel_id=1, source_target_pairs={{4,16},{12,24},{16,4},{24,12},{36,48},{44,56},{48,36},{56,44},{68,... | collective-permute-start | bytes 196616 | tf_op jit(solution)/shard_map/ppermute | solution.py:53
  12.9 0.4 collective-permute-start.2
  13.3 0.7 collective-permute-start.3
  13.9 0.0 collective-permute-done.g0
  14.0 0.0 copy-start.2
  14.0 1.7 %collective-permute-done.1.g1 = bf16[256,128]{1,0:T(8,128)(2,1)S(1)} collective-permute-done((bf16[256,128]{1,0:T(8,128)(2,1)}, bf16[256,128]{1,0:T(8,128)(2,1)S(1)}, u32[]{:S(2)}, u32[]{:S(2)}) %collective-permute-start.1) | collective-permute-done | bytes 65568 | tf_op jit(solution)/shard_map/ppermute | solution.py:53
  15.7 0.0 copy-start.3
  15.7 0.9 collective-permute-done.2.g2
  16.6 0.0 copy-start.4
  16.6 0.0 collective-permute-done.3.g3
  16.6 0.0 copy-start.5
  16.6 0.0 collective-permute-done.4.g4
  16.6 0.0 copy-done.2
  16.6 0.0 copy-done.3
  16.6 0.6 copy-done.4
  17.2 0.0 copy-done.5
  17.2 0.0 copy-start
  17.2 0.7 copy-done
  17.9 16.4 %shard_map.86 = (bf16[4,512,128]{2,1,0:T(8,128)(2,1)}, bf16[7168,128]{1,0:T(8,128)(2,1)}) custom-call(bf16[1,4,512,128]{3,2,1,0:T(8,128)(2,1)} %voxels.5, bf16[1,4,512,128]{3,2,1,0:T(8,128)(2,1)} %cotangent.3, s32[1,4,6]{2,1,0:T(4,128)} %links.7, s32[1,4]{1,0:T(1,128)} %occupied.5, bf16[27,128,128]{2,1,0:T(8,128)(2,1)} %first_weight.1, ...), custom_call_target="tpu_custom_call" | custom-call | flops 8589934592 | bytes 8388608 | tf_op jit(solution)/shard_map/pallas_call | solution.py:318
  34.3 38.6 %all_to_all.10.chunks = bf16[128,56,128]{2,1,0:T(8,128)(2,1)} all-to-all(bf16[128,56,128]{2,1,0:T(8,128)(2,1)} %bitcast.9), channel_id=1, replica_groups=mesh['space'=32,'rep'=4] {'space','rep'}, dimensions={0} | all-to-all | bytes 3670016 | tf_op jit(solution)/shard_map/all_to_all | solution.py:352
  72.9 3.3 %shard_map.89 = bf16[128,56,128]{2,1,0:T(8,128)(2,1)} custom-call(bf16[128,56,128]{2,1,0:T(8,128)(2,1)} %all_to_all.10.chunks), custom_call_target="tpu_custom_call" | custom-call | bytes 4194304 | tf_op jit(solution)/shard_map/pallas_call | solution.py:318
  76.1 3.8 %all-to-all-start.1 = ((bf16[128,56,128]{2,1,0:T(8,128)(2,1)}), bf16[128,56,128]{2,1,0:T(8,128)(2,1)S(1)}, u32[]{:S(2)}, u32[]{:S(2)}) async-start(bf16[128,56,128]{2,1,0:T(8,128)(2,1)} %shard_map.89), calls=%async_computation.1 | async-start | bytes 3670016 | tf_op jit(solution)/shard_map/all_to_all | solution.py:368
  80.0 2.0 %shard_map.87 = (bf16[128,128]{1,0:T(8,128)(2,1)}, bf16[128,128]{1,0:T(8,128)(2,1)}, bf16[128,128]{1,0:T(8,128)(2,1)}, bf16[128,128]{1,0:T(8,128)(2,1)}, bf16[256,128]{1,0:T(8,128)(2,1)}) custom-call(bf16[4,512,128]{2,1,0:T(8,128)(2,1)} %get-tuple-element.20.hidden, s32[1,4,6]{2,1,0:T(4,128)} %links.7), custom_call_target="tpu_custom_call" | custom-call | bytes 1048576 | tf_op jit(solution)/shard_map/pallas_call | solution.py:318
  82.0 3.3 %collective-permute-start.9 = (bf16[256,128]{1,0:T(8,128)(2,1)}, bf16[256,128]{1,0:T(8,128)(2,1)S(1)}, u32[]{:S(2)}, u32[]{:S(2)}) collective-permute-start(bf16[256,128]{1,0:T(8,128)(2,1)} %get-tuple-element.25), channel_id=1, source_target_pairs={{0,64},{4,68},{8,72},{12,76},{16,80},{20,84},{24,88},{28,92},{32,9... | collective-permute-start | bytes 196616 | tf_op jit(solution)/shard_map/ppermute | solution.py:53
  85.3 0.7 collective-permute-start.5
  85.9 4.5 %collective-permute-start.6 = (bf16[128,128]{1,0:T(8,128)(2,1)}, bf16[128,128]{1,0:T(8,128)(2,1)S(1)}, u32[]{:S(2)}, u32[]{:S(2)}) collective-permute-start(bf16[128,128]{1,0:T(8,128)(2,1)} %get-tuple-element.22), channel_id=1, source_target_pairs={{4,16},{12,24},{16,4},{24,12},{36,48},{44,56},{48,36},{56,44},{68,... | collective-permute-start | bytes 98312 | tf_op jit(solution)/shard_map/ppermute | solution.py:53
  90.4 0.4 collective-permute-start.7
  90.8 0.7 collective-permute-start.8
  91.5 0.0 collective-permute-done.5.g0
  91.5 0.0 copy-start.6
  91.5 12.2 %collective-permute-done.6.g1 = bf16[128,128]{1,0:T(8,128)(2,1)S(1)} collective-permute-done((bf16[128,128]{1,0:T(8,128)(2,1)}, bf16[128,128]{1,0:T(8,128)(2,1)S(1)}, u32[]{:S(2)}, u32[]{:S(2)}) %collective-permute-start.6) | collective-permute-done | bytes 32800 | tf_op jit(solution)/shard_map/ppermute | solution.py:53
  103.8 0.0 copy-start.7
  103.8 0.0 collective-permute-done.7.g2
  103.8 0.0 copy-start.8
  103.8 0.0 collective-permute-done.8.g3
  103.8 0.0 copy-start.9
  103.8 0.0 collective-permute-done.9.g4
  103.8 0.0 copy-done.6
  103.8 0.6 copy-done.7
  104.4 0.0 copy-done.8
  104.4 0.0 copy-done.9
  104.4 0.0 copy-start.1
  104.4 0.6 copy-done.1
  105.0 6.6 %shard_map.88 = bf16[1,4,512,128]{3,2,1,0:T(8,128)(2,1)} custom-call(bf16[1,4,512,128]{3,2,1,0:T(8,128)(2,1)} %voxels.5, bf16[4,512,128]{2,1,0:T(8,128)(2,1)} %get-tuple-element.20.hidden, s32[1,4,6]{2,1,0:T(4,128)} %links.7, s32[1,4]{1,0:T(1,128)} %occupied.5, bf16[27,128,128]{2,1,0:T(8,128)(2,1)} %second_weight.3, bf16[128,128]{1,0:T(8,128)(2,1)} %copy-done.6, ...), custom_call_target="tpu_custom_call" | custom-call | flops 3221225472 | bytes 4194304 | tf_op jit(solution)/shard_map/pallas_call | solution.py:318
  111.6 0.0 all-to-all-done.1
  111.6 0.1 fusion
  111.8 1.4 %convert.2 = f32[27,128,128]{2,1,0:T(8,128)} convert(bf16[27,128,128]{2,1,0:T(8,128)(2,1)S(1)} %bitcast.8) | non-fusion elementwise | flops 442368 | bytes 2654208 | tf_op jit(solution)/shard_map/convert_element_type | solution.py:370
  113.2 1.4 %convert.3 = f32[27,128,128]{2,1,0:T(8,128)} convert(bf16[27,128,128]{2,1,0:T(8,128)(2,1)S(1)} %bitcast.7) | non-fusion elementwise | flops 442368 | bytes 2654208 | tf_op jit(solution)/shard_map/convert_element_type | solution.py:371
Async XLA Ops:
  3.0 13.6 %collective-permute-start.4 = (bf16[512,128]{1,0:T(8,128)(2,1)}, bf16[512,128]{1,0:T(8,128)(2,1)S(1)}, u32[]{:S(2)}, u32[]{:S(2)}) collective-permute-start(bf16[512,128]{1,0:T(8,128)(2,1)} %get-tuple-element.19), channel_id=1, source_target_pairs={{0,64},{4,68},{8,72},{12,76},{16,80},{20,84},{24,88},{28,92},{32,9... | collective-permute-start | bytes 393224 | tf_op jit(solution)/shard_map/ppermute | solution.py:53
  7.4 6.6 %collective-permute-start = (bf16[256,128]{1,0:T(8,128)(2,1)}, bf16[256,128]{1,0:T(8,128)(2,1)S(1)}, u32[]{:S(2)}, u32[]{:S(2)}) collective-permute-start(bf16[256,128]{1,0:T(8,128)(2,1)} %get-tuple-element.15), channel_id=1, source_target_pairs={{0,4},{4,0},{8,12},{12,8},{16,20},{20,16},{24,28},{28,24},{32,36},... | collective-permute-start | bytes 196616 | tf_op jit(solution)/shard_map/ppermute | solution.py:53
  8.4 7.3 %collective-permute-start.1 = (bf16[256,128]{1,0:T(8,128)(2,1)}, bf16[256,128]{1,0:T(8,128)(2,1)S(1)}, u32[]{:S(2)}, u32[]{:S(2)}) collective-permute-start(bf16[256,128]{1,0:T(8,128)(2,1)} %get-tuple-element.16), channel_id=1, source_target_pairs={{4,16},{12,24},{16,4},{24,12},{36,48},{44,56},{48,36},{56,44},{68,... | collective-permute-start | bytes 196616 | tf_op jit(solution)/shard_map/ppermute | solution.py:53
  12.9 3.7 %collective-permute-start.2 = (bf16[256,128]{1,0:T(8,128)(2,1)}, bf16[256,128]{1,0:T(8,128)(2,1)S(1)}, u32[]{:S(2)}, u32[]{:S(2)}) collective-permute-start(bf16[256,128]{1,0:T(8,128)(2,1)} %get-tuple-element.17), channel_id=1, source_target_pairs={{0,8},{4,12},{8,0},{12,4},{16,24},{20,28},{24,16},{28,20},{32,40},... | collective-permute-start | bytes 196616 | tf_op jit(solution)/shard_map/ppermute | solution.py:53
  13.3 3.3 %collective-permute-start.3 = (bf16[256,128]{1,0:T(8,128)(2,1)}, bf16[256,128]{1,0:T(8,128)(2,1)S(1)}, u32[]{:S(2)}, u32[]{:S(2)}) collective-permute-start(bf16[256,128]{1,0:T(8,128)(2,1)} %get-tuple-element.18), channel_id=1, source_target_pairs={{8,32},{12,36},{24,48},{28,52},{32,8},{36,12},{48,24},{52,28},{72,... | collective-permute-start | bytes 196616 | tf_op jit(solution)/shard_map/ppermute | solution.py:53
  14.0 2.6 %copy-start.2 = (bf16[256,128]{1,0:T(8,128)(2,1)}, bf16[256,128]{1,0:T(8,128)(2,1)S(1)}, u32[]{:S(2)}) copy-start(bf16[256,128]{1,0:T(8,128)(2,1)S(1)} %collective-permute-done.g0) | copy-start | bytes 196612
  15.7 0.9 copy-start.3
  16.6 0.6 copy-start.4
  16.6 0.6 copy-start.5
  17.2 0.7 copy-start
  76.1 35.5 %all-to-all-start.1 = ((bf16[128,56,128]{2,1,0:T(8,128)(2,1)}), bf16[128,56,128]{2,1,0:T(8,128)(2,1)S(1)}, u32[]{:S(2)}, u32[]{:S(2)}) async-start(bf16[128,56,128]{2,1,0:T(8,128)(2,1)} %shard_map.89), calls=%async_computation.1 | async-start | bytes 3670016 | tf_op jit(solution)/shard_map/all_to_all | solution.py:368
  82.0 21.8 %collective-permute-start.9 = (bf16[256,128]{1,0:T(8,128)(2,1)}, bf16[256,128]{1,0:T(8,128)(2,1)S(1)}, u32[]{:S(2)}, u32[]{:S(2)}) collective-permute-start(bf16[256,128]{1,0:T(8,128)(2,1)} %get-tuple-element.25), channel_id=1, source_target_pairs={{0,64},{4,68},{8,72},{12,76},{16,80},{20,84},{24,88},{28,92},{32,9... | collective-permute-start | bytes 196616 | tf_op jit(solution)/shard_map/ppermute | solution.py:53
  85.3 6.2 %collective-permute-start.5 = (bf16[128,128]{1,0:T(8,128)(2,1)}, bf16[128,128]{1,0:T(8,128)(2,1)S(1)}, u32[]{:S(2)}, u32[]{:S(2)}) collective-permute-start(bf16[128,128]{1,0:T(8,128)(2,1)} %get-tuple-element.21), channel_id=1, source_target_pairs={{0,4},{4,0},{8,12},{12,8},{16,20},{20,16},{24,28},{28,24},{32,36},... | collective-permute-start | bytes 98312 | tf_op jit(solution)/shard_map/ppermute | solution.py:53
  85.9 17.8 %collective-permute-start.6 = (bf16[128,128]{1,0:T(8,128)(2,1)}, bf16[128,128]{1,0:T(8,128)(2,1)S(1)}, u32[]{:S(2)}, u32[]{:S(2)}) collective-permute-start(bf16[128,128]{1,0:T(8,128)(2,1)} %get-tuple-element.22), channel_id=1, source_target_pairs={{4,16},{12,24},{16,4},{24,12},{36,48},{44,56},{48,36},{56,44},{68,... | collective-permute-start | bytes 98312 | tf_op jit(solution)/shard_map/ppermute | solution.py:53
  90.4 13.3 %collective-permute-start.7 = (bf16[128,128]{1,0:T(8,128)(2,1)}, bf16[128,128]{1,0:T(8,128)(2,1)S(1)}, u32[]{:S(2)}, u32[]{:S(2)}) collective-permute-start(bf16[128,128]{1,0:T(8,128)(2,1)} %get-tuple-element.23), channel_id=1, source_target_pairs={{0,8},{4,12},{8,0},{12,4},{16,24},{20,28},{24,16},{28,20},{32,40},... | collective-permute-start | bytes 98312 | tf_op jit(solution)/shard_map/ppermute | solution.py:53
  90.8 12.9 %collective-permute-start.8 = (bf16[128,128]{1,0:T(8,128)(2,1)}, bf16[128,128]{1,0:T(8,128)(2,1)S(1)}, u32[]{:S(2)}, u32[]{:S(2)}) collective-permute-start(bf16[128,128]{1,0:T(8,128)(2,1)} %get-tuple-element.24), channel_id=1, source_target_pairs={{8,32},{12,36},{24,48},{28,52},{32,8},{36,12},{48,24},{52,28},{72,... | collective-permute-start | bytes 98312 | tf_op jit(solution)/shard_map/ppermute | solution.py:53
  91.5 12.3 %copy-start.6 = (bf16[128,128]{1,0:T(8,128)(2,1)}, bf16[128,128]{1,0:T(8,128)(2,1)S(1)}, u32[]{:S(2)}) copy-start(bf16[128,128]{1,0:T(8,128)(2,1)S(1)} %collective-permute-done.5.g0) | copy-start | bytes 98308
  103.8 0.6 copy-start.7
  103.8 0.6 copy-start.8
  103.8 0.6 copy-start.9
  104.4 0.6 copy-start.1
where the time goes:
time: 115 us
  blocking collectives  38.6 us (34%)
  Pallas kernels  30.7 us (27%)
  starting transfers between devices  24.3 us (21%)
  waiting for transfers between devices  14.9 us (13%)
  other arithmetic  2.81 us (2%)
  local copies, waits for them, and re-layouts  2.63 us (2%)
    all_to_all x1, blocking collectives, local(): lax.all_to_all(terms.reshape(128, CHUNK, 128), ('space', 'rep'), split_ax...  38.6 us
    pallas_call x5, Pallas kernels, call(): pl.pallas_call(kernel, out_shape=outs, in_specs=specs, out_specs=tuple((V...  30.7 us
    ppermute x10, starting transfers between devices, exchange(): lax.ppermute(a, 'space', pairs)  20.5 us
    ppermute x10, waiting for transfers between devices, exchange(): lax.ppermute(a, 'space', pairs)  14.9 us
    all_to_all x1, starting transfers between devices, local(): lax.all_to_all(spread, ('space', 'rep'), split_axis=0, concat_axis=0, til...  3.82 us
    unnamed x20, local copies, waits for them, and re-layouts  2.51 us
  transfers between devices with their start and end apart: 11, of which 3 were waited for; matrix products, arithmetic and copies ran while one was open for 0% of the time, Pallas kernels for 8%

commit v1 on v0

--- a/solution.py
+++ b/solution.py
@@ -11,7 +11,6 @@
 F32 = jnp.float32
 VMEM = pl.BlockSpec(memory_space=pltpu.VMEM)
 SMEM = pl.BlockSpec(memory_space=pltpu.SMEM)
-PARAMS = pltpu.CompilerParams(vmem_limit_bytes=56 << 20)
 ROWS = 3456
 CHUNK = 56
 
@@ -49,8 +48,13 @@
 SWAPS = tuple(swaps(kind) for kind in ("xe", "xo", "ye", "yo", "z"))
 
 
+SPACE = ("chip", "core")
+PEERS = ("chip", "rep")
+PARTNER = ((0, 1), (1, 0))
+
+
 def exchange(sent):
-    return tuple(lax.ppermute(a, "space", pairs) for a, pairs in zip(sent, SWAPS))
+    return tuple(lax.ppermute(a, SPACE, pairs) for a, pairs in zip(sent, SWAPS))
 
 
 def remote_links(links, face, device):
@@ -208,7 +212,7 @@
 
 def first_faces_kernel(voxels, cotangent, links, occupied, *rest):
     sends, (x, g) = rest[:5], rest[5:]
-    device = lax.axis_index("space")
+    device = lax.axis_index(SPACE)
     load_masked(x, voxels, occupied)
     load_masked(g, cotangent, occupied)
     pack_faces((x, g), links, device, sends)
@@ -216,7 +220,7 @@
 
 def hidden_faces_kernel(hidden, links, *rest):
     sends, (x,) = rest[:5], rest[5:]
-    device = lax.axis_index("space")
+    device = lax.axis_index(SPACE)
     for n in range(4):
         x[n] = hidden[n].astype(F32)
     pack_faces((x,), links, device, sends)
@@ -224,10 +228,10 @@
 
 def main_kernel(
     voxels, cotangent, links, occupied, first_weight, second_weight, g0, g1, g2, g3, g4,
-    hidden, terms,
+    hidden, own_terms, other_terms,
     x, fx, fy, fz, wide, odd, wide_grad, odd_grad, pair_weights, slope, hidden_turned, grad_turned,
 ):
-    device = lax.axis_index("space")
+    device = lax.axis_index(SPACE)
     got = (g0, g1, g2, g3, g4)
     faces = (fx, fy, fz)
     load_masked(x, voxels, occupied)
@@ -252,8 +256,21 @@
     build(wide_grad, odd_grad, x, faces)
     lay_weights(pair_weights, lambda t: second_weight[26 - t].T)
 
+    core = device & 1
+
+    def put(of_core, t, block):
+        rows = pl.ds(t * 128, 128)
+
+        @pl.when(core == of_core)
+        def _():
+            own_terms[rows, :] = block
+
+        @pl.when(core != of_core)
+        def _():
+            other_terms[rows, :] = block
+
     def put_second(t, block):
-        terms[pl.ds(ROWS + (26 - t) * 128, 128), :] = block.astype(BF)
+        put(1, 26 - t, block)
 
     weight_terms(wide_grad, odd_grad, hidden_turned, put_second)
 
@@ -265,10 +282,9 @@
     lax.fori_loop(0, 4, backward, 0)
 
     def put_first(t, block):
-        terms[pl.ds(t * 128, 128), :] = block.T.astype(BF)
+        put(0, t, block.T)
 
     weight_terms(wide, odd, grad_turned, put_first)
-    terms[pl.ds(2 * ROWS, 256), :] = jnp.zeros((256, 128), BF)
 
 
 def last_kernel(
@@ -276,7 +292,7 @@
     output,
     x, fx, fy, fz, wide, odd, pair_weights,
 ):
-    device = lax.axis_index("space")
+    device = lax.axis_index(SPACE)
     faces = (fx, fy, fz)
     for n in range(4):
         x[n] = hidden[n].astype(F32)
@@ -293,27 +309,51 @@
     lax.fori_loop(0, 4, forward, 0)
 
 
-def sum_kernel(chunks, spread):
+def pair_kernel(own, other, terms):
+    terms[pl.ds(0, ROWS), :] = (own[...] + other[...]).astype(BF)
+    terms[pl.ds(ROWS, 64 * CHUNK - ROWS), :] = jnp.zeros((64 * CHUNK - ROWS, 128), BF)
+
+
+def sum_kernel(chunks, *rest):
+    spread = rest[-1]
     total = chunks[0].astype(F32)
 
     def add(p, total):
         return total + chunks[p].astype(F32)
 
-    total = lax.fori_loop(1, 128, add, total, unroll=8).astype(BF)
+    total = lax.fori_loop(1, 64, add, total, unroll=7).astype(BF)
 
     def put(p, carry):
         spread[p] = total
         return carry
 
-    lax.fori_loop(0, 128, put, 0, unroll=8)
+    lax.fori_loop(0, 64, put, 0, unroll=8)
+
+
+def finish_kernel(own, other, first_grad, second_grad):
+    core = lax.axis_index("core")
+
+    def put(mine, theirs):
+        mine[...] = own[pl.ds(0, ROWS), :].astype(F32)
+        theirs[...] = other[pl.ds(0, ROWS), :].astype(F32)
+
+    @pl.when(core == 0)
+    def _():
+        put(first_grad, second_grad)
+
+    @pl.when(core == 1)
+    def _():
+        put(second_grad, first_grad)
 
 
 def send_shapes(fields):
     return tuple(jax.ShapeDtypeStruct((fields * w * 64, 128), BF) for w in (2, 2, 2, 2, 4))
 
 
-def call(kernel, outs, ins, scratch, flops=0, nbytes=0):
+def call(kernel, outs, ins, scratch, limit, flops=0, nbytes=0, unread=0):
     specs = [SMEM if a.dtype == jnp.int32 else VMEM for a in ins]
+    for at in range(len(ins) - unread, len(ins)):
+        specs[at] = pl.BlockSpec(memory_space=pl.ANY)
     many = isinstance(outs, tuple)
     return pl.pallas_call(
         kernel,
@@ -321,7 +361,7 @@
         in_specs=specs,
         out_specs=tuple(VMEM for _ in outs) if many else VMEM,
         scratch_shapes=scratch,
-        compiler_params=PARAMS,
+        compiler_params=pltpu.CompilerParams(vmem_limit_bytes=limit << 20),
         cost_estimate=pl.CostEstimate(flops=flops, bytes_accessed=nbytes, transcendentals=0),
     )(*ins)
 
@@ -338,53 +378,70 @@
         send_shapes(2),
         (voxels, cotangent, neighbours, occupied),
         [field, field],
+        8,
         nbytes=2 << 20,
     )
     got = exchange(sent)
-    hidden, terms = call(
+    terms_shape = jax.ShapeDtypeStruct((ROWS, 128), F32)
+    hidden, own, other = call(
         main_kernel,
-        (jax.ShapeDtypeStruct((4, 512, 128), BF), jax.ShapeDtypeStruct((128 * CHUNK, 128), BF)),
+        (jax.ShapeDtypeStruct((4, 512, 128), BF), terms_shape, terms_shape),
         (voxels, cotangent, neighbours, occupied, first_weight, second_weight) + got,
         [field] + sides + padded + padded + [pairs, field, turned, turned],
+        32,
         flops=8 << 30,
         nbytes=8 << 20,
     )
+    other = lax.ppermute(other, "core", PARTNER)
+    chunks = jax.ShapeDtypeStruct((64 * CHUNK, 128), BF)
+    terms = call(pair_kernel, chunks, (own, other), [], 8, nbytes=4 << 20)
     parts = lax.all_to_all(
-        terms.reshape(128, CHUNK, 128), ("space", "rep"), split_axis=0, concat_axis=0, tiled=True
-    )
-    sent = call(hidden_faces_kernel, send_shapes(1), (hidden, neighbours), [field], nbytes=1 << 20)
+        terms.reshape(64, CHUNK, 128), PEERS, split_axis=0, concat_axis=0, tiled=True
+    )
+    sent = call(hidden_faces_kernel, send_shapes(1), (hidden, neighbours), [field], 6, nbytes=1 << 20)
     got = exchange(sent)
+    spread = call(
+        sum_kernel,
+        jax.ShapeDtypeStruct((64, CHUNK, 128), BF),
+        (parts,) + got,
+        [],
+        6,
+        nbytes=2 << 20,
+        unread=5,
+    )
+    mine = lax.all_to_all(spread, PEERS, split_axis=0, concat_axis=0, tiled=True)
     output = call(
         last_kernel,
         jax.ShapeDtypeStruct((1, 4, 512, 128), BF),
         (voxels, hidden, neighbours, occupied, second_weight) + got,
         [field] + sides + padded + [pairs],
+        20,
         flops=3 << 30,
         nbytes=4 << 20,
     )
-    spread = call(
-        sum_kernel, jax.ShapeDtypeStruct((128, CHUNK, 128), BF), (parts,), [], nbytes=4 << 20
-    )
-    whole = lax.all_to_all(spread, ("space", "rep"), split_axis=0, concat_axis=0, tiled=True)
-    whole = whole.reshape(128 * CHUNK, 128)
-    first_grad = whole[:ROWS].reshape(27, 128, 128).astype(F32)
-    second_grad = whole[ROWS : 2 * ROWS].reshape(27, 128, 128).astype(F32)
-    return output, first_grad, second_grad
+    mine, output = lax.optimization_barrier((mine, output))
+    mine = mine.reshape(64 * CHUNK, 128)
+    theirs = lax.ppermute(mine, "core", PARTNER)
+    first_grad, second_grad = call(
+        finish_kernel, (terms_shape, terms_shape), (mine, theirs), [], 10, nbytes=6 << 20
+    )
+    return output, first_grad.reshape(27, 128, 128), second_grad.reshape(27, 128, 128)
 
 
 def solution(mesh):
+    mesh = jax.sharding.Mesh(mesh.devices.reshape(16, 2, 4), ("chip", "core", "rep"))
     placed = (
-        P("rep", "space", None, None),
-        P("rep", "space"),
-        P("rep", "space", None),
+        P("rep", SPACE, None, None),
+        P("rep", SPACE),
+        P("rep", SPACE, None),
         P(),
         P(),
-        P("rep", "space", None, None),
+        P("rep", SPACE, None, None),
     )
     return jax.shard_map(
         local,
         mesh=mesh,
         in_specs=placed,
-        out_specs=(P("rep", "space", None, None), P(), P()),
+        out_specs=(P("rep", SPACE, None, None), P(), P()),
         check_vma=False,
     )

time: 115 us -> 105 us (0.913)
  blocking collectives: 38.6 us -> 0 us
  starting transfers between devices: 24.3 us -> 42.4 us
  waiting for transfers between devices: 14.9 us -> 23.1 us
  local copies, waits for them, and re-layouts: 2.63 us -> 9.18 us
  other arithmetic: 2.81 us -> 0 us
  Pallas kernels: 30.7 us -> 29.1 us
    all_to_all x1 -> x0, blocking collectives: 38.6 us -> none  [local(): lax.all_to_all(terms.reshape(128, CHUNK, 128), ('space', 'rep'), split_ax...]
    all_to_all x1 -> x2, starting transfers between devices: 3.82 us -> 18.2 us  [the longest x1 11.5 us: local(): lax.all_to_all(terms.reshape(64, CHUNK, 128), PEERS, split_axis=0, concat...]
    all_to_all x1 -> x2, waiting for transfers between devices: 0.01 us -> 11.5 us  [the longest x1 9.49 us: local(): lax.all_to_all(spread, PEERS, split_axis=0, concat_axis=0, tiled=True)]
    unnamed x20 -> x28, local copies, waits for them, and re-layouts: 2.51 us -> 9.18 us
    ppermute x10 -> x12, starting transfers between devices: 20.5 us -> 24.2 us  [the longest x10 20.9 us: exchange(): lax.ppermute(a, SPACE, pairs)]
    ppermute x10 -> x12, waiting for transfers between devices: 14.9 us -> 11.5 us  [the longest x10 5.74 us: exchange(): lax.ppermute(a, SPACE, pairs)]
    convert_element_type x2 -> x0, other arithmetic: 2.81 us -> none  [the longest x1 1.41 us: local(): first_grad = whole[:ROWS].reshape(27, 128, 128).astype(F32)]
    pallas_call x5 -> x7, Pallas kernels: 30.7 us -> 29.1 us  [call(): pl.pallas_call(kernel, out_shape=outs, in_specs=specs, out_specs=tuple((V...]
  transfers between devices with their start and end apart: 11 -> 14, of which waited for: 3 -> 7; matrix products, arithmetic and copies ran while one was open for 0% -> 0% of each run, Pallas kernels for 8% -> 6%
where the time goes in v1:
time: 105 us
  starting transfers between devices  42.4 us (40%)
  Pallas kernels  29.1 us (28%)
  waiting for transfers between devices  23.1 us (22%)
  local copies, waits for them, and re-layouts  9.18 us (9%)
    pallas_call x7, Pallas kernels, call(): pl.pallas_call(kernel, out_shape=outs, in_specs=specs, out_specs=tuple((V...  29.1 us
    ppermute x10, starting transfers between devices, exchange(): lax.ppermute(a, SPACE, pairs)  20.9 us
    all_to_all x1, starting transfers between devices, local(): lax.all_to_all(terms.reshape(64, CHUNK, 128), PEERS, split_axis=0, concat...  11.5 us
    all_to_all x1, waiting for transfers between devices, local(): lax.all_to_all(spread, PEERS, split_axis=0, concat_axis=0, tiled=True)  9.49 us
    unnamed x28, local copies, waits for them, and re-layouts  9.18 us
    all_to_all x1, starting transfers between devices, local(): lax.all_to_all(spread, PEERS, split_axis=0, concat_axis=0, tiled=True)  6.71 us
    ppermute x10, waiting for transfers between devices, exchange(): lax.ppermute(a, SPACE, pairs)  5.74 us
    ppermute x1, waiting for transfers between devices, local(): other = lax.ppermute(other, 'core', PARTNER)  3.68 us
  transfers between devices with their start and end apart: 14, of which 7 were waited for; matrix products, arithmetic and copies ran while one was open for 0% of the time, Pallas kernels for 6%

profile of v1, /device:TPU:1, one launch (start us, length us, event | category | flops | bytes accessed | tf_op | source)
XLA Modules:
  0.0 104.6 jit_solution(452453440576406069)
XLA Ops:
  0.6 0.0 copy-start
  0.6 1.0 copy-done
  1.7 0.0 copy-start.2
  1.7 1.0 copy-done.2
  2.7 0.0 copy-start.5
  2.7 0.7 copy-done.5
  3.4 0.0 copy-start.8
  3.4 0.7 copy-done.8
  4.1 0.9 shard_map.85
  5.0 4.5 %collective-permute-start.4 = (bf16[512,128]{1,0:T(8,128)(2,1)S(1)}, bf16[512,128]{1,0:T(8,128)(2,1)S(1)}, u32[]{:S(2)}, u32[]{:S(2)}) collective-permute-start(bf16[512,128]{1,0:T(8,128)(2,1)S(1)} %get-tuple-element.24), channel_id=1, source_target_pairs={{0,64},{4,68},{8,72},{12,76},{16,80},{20,84},{24,88},{28,92},{32,9... | collective-permute-start | bytes 393224 | tf_op jit(solution)/shard_map/ppermute | solution.py:57
  9.5 1.0 collective-permute-start
  10.5 4.5 %collective-permute-start.1 = (bf16[256,128]{1,0:T(8,128)(2,1)S(1)}, bf16[256,128]{1,0:T(8,128)(2,1)S(1)}, u32[]{:S(2)}, u32[]{:S(2)}) collective-permute-start(bf16[256,128]{1,0:T(8,128)(2,1)S(1)} %get-tuple-element.21), channel_id=1, source_target_pairs={{4,16},{12,24},{16,4},{24,12},{36,48},{44,56},{48,36},{56,44},{68,... | collective-permute-start | bytes 196616 | tf_op jit(solution)/shard_map/ppermute | solution.py:57
  15.0 0.5 collective-permute-start.2
  15.4 0.7 collective-permute-start.3
  16.1 0.0 collective-permute-done.g0
  16.1 1.4 %collective-permute-done.1.g1 = bf16[256,128]{1,0:T(8,128)(2,1)S(1)} collective-permute-done((bf16[256,128]{1,0:T(8,128)(2,1)S(1)}, bf16[256,128]{1,0:T(8,128)(2,1)S(1)}, u32[]{:S(2)}, u32[]{:S(2)}) %collective-permute-start.1) | collective-permute-done | bytes 65568 | tf_op jit(solution)/shard_map/ppermute | solution.py:57
  17.5 0.9 collective-permute-done.2.g2
  18.4 0.0 collective-permute-done.3.g3
  18.4 0.0 collective-permute-done.4.g4
  18.4 0.0 copy-start.1
  18.4 1.0 copy-done.1
  19.5 0.0 copy-start.3
  19.5 1.0 copy-done.3
  20.5 0.0 copy-start.6
  20.5 0.7 copy-done.6
  21.2 0.0 copy-start.9
  21.2 0.7 copy-done.9
  21.9 0.0 copy-start.11
  21.9 1.2 %copy-done.11 = bf16[27,128,128]{2,1,0:T(8,128)(2,1)S(1)} copy-done((bf16[27,128,128]{2,1,0:T(8,128)(2,1)S(1)}, bf16[27,128,128]{2,1,0:T(8,128)(2,1)}, u32[]{:S(2)}) %copy-start.11) | copy-done | bytes 884760
  23.0 0.0 copy-start.12
  23.0 1.2 %copy-done.12 = bf16[27,128,128]{2,1,0:T(8,128)(2,1)S(1)} copy-done((bf16[27,128,128]{2,1,0:T(8,128)(2,1)S(1)}, bf16[27,128,128]{2,1,0:T(8,128)(2,1)}, u32[]{:S(2)}) %copy-start.12) | copy-done | bytes 884760
  24.2 17.3 %shard_map.86 = (bf16[4,512,128]{2,1,0:T(8,128)(2,1)S(1)}, f32[3456,128]{1,0:T(8,128)S(1)}, f32[3456,128]{1,0:T(8,128)S(1)}) custom-call(bf16[1,4,512,128]{3,2,1,0:T(8,128)(2,1)S(1)} %copy-done.3, bf16[1,4,512,128]{3,2,1,0:T(8,128)(2,1)S(1)} %copy-done.1, s32[1,4,6]{2,1,0:T(4,128)S(1)} %copy-done.6, s32[1,4]{1,0:T(1,128)S(1)} %copy-done.9, ...), custom_call_target="tpu_custom_call" | custom-call | flops 8589934592 | bytes 8388608 | tf_op jit(solution)/shard_map/pallas_call | solution.py:358
  41.5 0.1 collective-permute-start.5
  41.6 3.7 %collective-permute-done.5.other = f32[3456,128]{1,0:T(8,128)S(1)} collective-permute-done((f32[3456,128]{1,0:T(8,128)S(1)}, f32[3456,128]{1,0:T(8,128)S(1)}, u32[]{:S(2)}, u32[]{:S(2)}) %collective-permute-start.5) | collective-permute-done | bytes 1769504 | tf_op jit(solution)/shard_map/ppermute | solution.py:395
  45.3 1.2 %shard_map.87 = bf16[3584,128]{1,0:T(8,128)(2,1)} custom-call(f32[3456,128]{1,0:T(8,128)S(1)} %get-tuple-element.25.own, f32[3456,128]{1,0:T(8,128)S(1)} %collective-permute-done.5.other), custom_call_target="tpu_custom_call" | custom-call | bytes 4194304 | tf_op jit(solution)/shard_map/pallas_call | solution.py:358
  46.5 0.0 copy-start.7
  46.5 11.5 %all-to-all-start = ((bf16[64,56,128]{2,1,0:T(8,128)(2,1)}), bf16[64,56,128]{2,1,0:T(8,128)(2,1)S(1)}, u32[]{:S(2)}, u32[]{:S(2)}) async-start(bf16[64,56,128]{2,1,0:T(8,128)(2,1)} %bitcast), calls=%async_computation | async-start | bytes 1835008 | tf_op jit(solution)/shard_map/all_to_all | solution.py:398
  58.1 0.0 copy-done.7
  58.1 0.9 shard_map.88
  58.9 2.9 %collective-permute-start.10 = (bf16[256,128]{1,0:T(8,128)(2,1)S(1)}, bf16[256,128]{1,0:T(8,128)(2,1)S(1)}, u32[]{:S(2)}, u32[]{:S(2)}) collective-permute-start(bf16[256,128]{1,0:T(8,128)(2,1)S(1)} %get-tuple-element.32), channel_id=1, source_target_pairs={{0,64},{4,68},{8,72},{12,76},{16,80},{20,84},{24,88},{28,92},{32,9... | collective-permute-start | bytes 196616 | tf_op jit(solution)/shard_map/ppermute | solution.py:57
  61.8 1.2 %collective-permute-start.6 = (bf16[128,128]{1,0:T(8,128)(2,1)S(1)}, bf16[128,128]{1,0:T(8,128)(2,1)S(1)}, u32[]{:S(2)}, u32[]{:S(2)}) collective-permute-start(bf16[128,128]{1,0:T(8,128)(2,1)S(1)} %get-tuple-element.28), channel_id=1, source_target_pairs={{0,4},{4,0},{8,12},{12,8},{16,20},{20,16},{24,28},{28,24},{32,36},... | collective-permute-start | bytes 98312 | tf_op jit(solution)/shard_map/ppermute | solution.py:57
  63.0 4.5 %collective-permute-start.7 = (bf16[128,128]{1,0:T(8,128)(2,1)S(1)}, bf16[128,128]{1,0:T(8,128)(2,1)S(1)}, u32[]{:S(2)}, u32[]{:S(2)}) collective-permute-start(bf16[128,128]{1,0:T(8,128)(2,1)S(1)} %get-tuple-element.29), channel_id=1, source_target_pairs={{4,16},{12,24},{16,4},{24,12},{36,48},{44,56},{48,36},{56,44},{68,... | collective-permute-start | bytes 98312 | tf_op jit(solution)/shard_map/ppermute | solution.py:57
  67.6 0.4 collective-permute-start.8
  68.0 0.0 copy-start.4
  68.0 0.0 copy-start.10
  68.0 0.0 copy-start.13
  68.0 0.8 collective-permute-start.9
  68.8 0.0 collective-permute-done.6.rest_0_.g0
  68.8 3.4 %collective-permute-done.7.rest_1_.g1 = bf16[128,128]{1,0:T(8,128)(2,1)S(1)} collective-permute-done((bf16[128,128]{1,0:T(8,128)(2,1)S(1)}, bf16[128,128]{1,0:T(8,128)(2,1)S(1)}, u32[]{:S(2)}, u32[]{:S(2)}) %collective-permute-start.7) | collective-permute-done | bytes 32800 | tf_op jit(solution)/shard_map/ppermute | solution.py:57
  72.2 0.0 collective-permute-done.8.rest_2_.g2
  72.2 0.0 collective-permute-done.9.rest_3_.g3
  72.2 0.0 collective-permute-done.10.rest_4_.g4
  72.2 2.0 %all-to-all-done.chunks = bf16[64,56,128]{2,1,0:T(8,128)(2,1)S(1)} async-done(((bf16[64,56,128]{2,1,0:T(8,128)(2,1)}), bf16[64,56,128]{2,1,0:T(8,128)(2,1)S(1)}, u32[]{:S(2)}, u32[]{:S(2)}) %all-to-all-start) | async-done | bytes 917536 | tf_op jit(solution)/shard_map/all_to_all | solution.py:398
  74.3 1.2 %shard_map.89 = bf16[64,56,128]{2,1,0:T(8,128)(2,1)} custom-call(bf16[64,56,128]{2,1,0:T(8,128)(2,1)S(1)} %all-to-all-done.chunks, bf16[128,128]{1,0:T(8,128)(2,1)S(1)} %collective-permute-done.6.rest_0_.g0, bf16[128,128]{1,0:T(8,128)(2,1)S(1)} %collective-permute-done.7.rest_1_.g1, bf16[128,128]{1,0:T(8,128)(2,1)S(1)} %collective-permute-done.8.rest_2_.g2, ...), custom_call_target="tpu_custom_call" | custom-call | bytes 2097152 | tf_op jit(solution)/shard_map/pallas_call | solution.py:358
  75.4 6.7 %all-to-all-start.1 = ((bf16[64,56,128]{2,1,0:T(8,128)(2,1)}), bf16[64,56,128]{2,1,0:T(8,128)(2,1)S(1)}, u32[]{:S(2)}, u32[]{:S(2)}) async-start(bf16[64,56,128]{2,1,0:T(8,128)(2,1)} %shard_map.89), calls=%async_computation.1 | async-start | bytes 1835008 | tf_op jit(solution)/shard_map/all_to_all | solution.py:412
  82.1 0.0 copy-done.4
  82.1 0.0 copy-done.10
  82.2 0.0 copy-done.13
  82.2 5.6 %shard_map.90 = bf16[1,4,512,128]{3,2,1,0:T(8,128)(2,1)} custom-call(bf16[1,4,512,128]{3,2,1,0:T(8,128)(2,1)S(1)} %copy-done.4, bf16[4,512,128]{2,1,0:T(8,128)(2,1)S(1)} %get-tuple-element.27.hidden, s32[1,4,6]{2,1,0:T(4,128)S(1)} %copy-done.7, s32[1,4]{1,0:T(1,128)S(1)} %copy-done.10, bf16[27,128,128]{2,1,0:T(8,128)(2,1)S(1)} %copy-done.13, ...), custom_call_target="tpu_custom_call" | custom-call | flops 3221225472 | bytes 4194304 | tf_op jit(solution)/shard_map/pallas_call | solution.py:358
  87.8 9.5 %all-to-all-done.1 = bf16[64,56,128]{2,1,0:T(8,128)(2,1)S(1)} async-done(((bf16[64,56,128]{2,1,0:T(8,128)(2,1)}), bf16[64,56,128]{2,1,0:T(8,128)(2,1)S(1)}, u32[]{:S(2)}, u32[]{:S(2)}) %all-to-all-start.1) | async-done | bytes 917536 | tf_op jit(solution)/shard_map/all_to_all | solution.py:412
  97.3 3.1 %collective-permute-start.11 = (bf16[3584,128]{1,0:T(8,128)(2,1)S(1)}, bf16[3584,128]{1,0:T(8,128)(2,1)S(1)}, u32[]{:S(2)}, u32[]{:S(2)}) collective-permute-start(bf16[3584,128]{1,0:T(8,128)(2,1)S(1)} %bitcast.4), channel_id=1, source_target_pairs={{0,4},{4,0},{1,5},{5,1},{2,6},{6,2},{3,7},{7,3},{8,12},{12,8},{9,1... | collective-permute-start | bytes 2752520 | tf_op jit(solution)/shard_map/ppermute | solution.py:424
  100.4 2.1 %collective-permute-done.11.other = bf16[3584,128]{1,0:T(8,128)(2,1)S(1)} collective-permute-done((bf16[3584,128]{1,0:T(8,128)(2,1)S(1)}, bf16[3584,128]{1,0:T(8,128)(2,1)S(1)}, u32[]{:S(2)}, u32[]{:S(2)}) %collective-permute-start.11) | collective-permute-done | bytes 917536 | tf_op jit(solution)/shard_map/ppermute | solution.py:424
  102.5 2.0 %shard_map.91 = (f32[3456,128]{1,0:T(8,128)}, f32[3456,128]{1,0:T(8,128)}) custom-call(bf16[3584,128]{1,0:T(8,128)(2,1)S(1)} %bitcast.5, bf16[3584,128]{1,0:T(8,128)(2,1)S(1)} %collective-permute-done.11.other), custom_call_target="tpu_custom_call" | custom-call | bytes 6291456 | tf_op jit(solution)/shard_map/pallas_call | solution.py:358
Async XLA Ops:
  0.6 1.0 copy-start
  1.7 1.0 copy-start.2
  2.7 0.7 copy-start.5
  3.4 0.7 copy-start.8
  5.0 13.4 %collective-permute-start.4 = (bf16[512,128]{1,0:T(8,128)(2,1)S(1)}, bf16[512,128]{1,0:T(8,128)(2,1)S(1)}, u32[]{:S(2)}, u32[]{:S(2)}) collective-permute-start(bf16[512,128]{1,0:T(8,128)(2,1)S(1)} %get-tuple-element.24), channel_id=1, source_target_pairs={{0,64},{4,68},{8,72},{12,76},{16,80},{20,84},{24,88},{28,92},{32,9... | collective-permute-start | bytes 393224 | tf_op jit(solution)/shard_map/ppermute | solution.py:57
  9.5 6.6 %collective-permute-start = (bf16[256,128]{1,0:T(8,128)(2,1)S(1)}, bf16[256,128]{1,0:T(8,128)(2,1)S(1)}, u32[]{:S(2)}, u32[]{:S(2)}) collective-permute-start(bf16[256,128]{1,0:T(8,128)(2,1)S(1)} %get-tuple-element.20), channel_id=1, source_target_pairs={{0,4},{4,0},{8,12},{12,8},{16,20},{20,16},{24,28},{28,24},{32,36},... | collective-permute-start | bytes 196616 | tf_op jit(solution)/shard_map/ppermute | solution.py:57
  10.5 7.1 %collective-permute-start.1 = (bf16[256,128]{1,0:T(8,128)(2,1)S(1)}, bf16[256,128]{1,0:T(8,128)(2,1)S(1)}, u32[]{:S(2)}, u32[]{:S(2)}) collective-permute-start(bf16[256,128]{1,0:T(8,128)(2,1)S(1)} %get-tuple-element.21), channel_id=1, source_target_pairs={{4,16},{12,24},{16,4},{24,12},{36,48},{44,56},{48,36},{56,44},{68,... | collective-permute-start | bytes 196616 | tf_op jit(solution)/shard_map/ppermute | solution.py:57
  15.0 3.4 %collective-permute-start.2 = (bf16[256,128]{1,0:T(8,128)(2,1)S(1)}, bf16[256,128]{1,0:T(8,128)(2,1)S(1)}, u32[]{:S(2)}, u32[]{:S(2)}) collective-permute-start(bf16[256,128]{1,0:T(8,128)(2,1)S(1)} %get-tuple-element.22), channel_id=1, source_target_pairs={{0,8},{4,12},{8,0},{12,4},{16,24},{20,28},{24,16},{28,20},{32,40},... | collective-permute-start | bytes 196616 | tf_op jit(solution)/shard_map/ppermute | solution.py:57
  15.4 3.0 %collective-permute-start.3 = (bf16[256,128]{1,0:T(8,128)(2,1)S(1)}, bf16[256,128]{1,0:T(8,128)(2,1)S(1)}, u32[]{:S(2)}, u32[]{:S(2)}) collective-permute-start(bf16[256,128]{1,0:T(8,128)(2,1)S(1)} %get-tuple-element.23), channel_id=1, source_target_pairs={{8,32},{12,36},{24,48},{28,52},{32,8},{36,12},{48,24},{52,28},{72,... | collective-permute-start | bytes 196616 | tf_op jit(solution)/shard_map/ppermute | solution.py:57
  18.4 1.0 copy-start.1
  19.5 1.0 copy-start.3
  20.5 0.7 copy-start.6
  21.2 0.7 copy-start.9
  21.9 1.2 %copy-start.11 = (bf16[27,128,128]{2,1,0:T(8,128)(2,1)S(1)}, bf16[27,128,128]{2,1,0:T(8,128)(2,1)}, u32[]{:S(2)}) copy-start(bf16[27,128,128]{2,1,0:T(8,128)(2,1)} %first_weight.1) | copy-start | bytes 2654212
  23.0 1.2 %copy-start.12 = (bf16[27,128,128]{2,1,0:T(8,128)(2,1)S(1)}, bf16[27,128,128]{2,1,0:T(8,128)(2,1)}, u32[]{:S(2)}) copy-start(bf16[27,128,128]{2,1,0:T(8,128)(2,1)} %second_weight.3) | copy-start | bytes 2654212
  41.5 3.8 %collective-permute-start.5 = (f32[3456,128]{1,0:T(8,128)S(1)}, f32[3456,128]{1,0:T(8,128)S(1)}, u32[]{:S(2)}, u32[]{:S(2)}) collective-permute-start(f32[3456,128]{1,0:T(8,128)S(1)} %get-tuple-element.26), channel_id=1, source_target_pairs={{0,4},{4,0},{1,5},{5,1},{2,6},{6,2},{3,7},{7,3},{8,12},{12,8},{9,1... | collective-permute-start | bytes 5308424 | tf_op jit(solution)/shard_map/ppermute | solution.py:395
  46.5 11.5 %copy-start.7 = (s32[1,4,6]{2,1,0:T(4,128)S(1)}, s32[1,4,6]{2,1,0:T(4,128)}, u32[]{:S(2)}) copy-start(s32[1,4,6]{2,1,0:T(4,128)} %links.7) | copy-start | bytes 292
  46.5 27.7 %all-to-all-start = ((bf16[64,56,128]{2,1,0:T(8,128)(2,1)}), bf16[64,56,128]{2,1,0:T(8,128)(2,1)S(1)}, u32[]{:S(2)}, u32[]{:S(2)}) async-start(bf16[64,56,128]{2,1,0:T(8,128)(2,1)} %bitcast), calls=%async_computation | async-start | bytes 1835008 | tf_op jit(solution)/shard_map/all_to_all | solution.py:398
  58.9 13.3 %collective-permute-start.10 = (bf16[256,128]{1,0:T(8,128)(2,1)S(1)}, bf16[256,128]{1,0:T(8,128)(2,1)S(1)}, u32[]{:S(2)}, u32[]{:S(2)}) collective-permute-start(bf16[256,128]{1,0:T(8,128)(2,1)S(1)} %get-tuple-element.32), channel_id=1, source_target_pairs={{0,64},{4,68},{8,72},{12,76},{16,80},{20,84},{24,88},{28,92},{32,9... | collective-permute-start | bytes 196616 | tf_op jit(solution)/shard_map/ppermute | solution.py:57
  61.8 7.0 %collective-permute-start.6 = (bf16[128,128]{1,0:T(8,128)(2,1)S(1)}, bf16[128,128]{1,0:T(8,128)(2,1)S(1)}, u32[]{:S(2)}, u32[]{:S(2)}) collective-permute-start(bf16[128,128]{1,0:T(8,128)(2,1)S(1)} %get-tuple-element.28), channel_id=1, source_target_pairs={{0,4},{4,0},{8,12},{12,8},{16,20},{20,16},{24,28},{28,24},{32,36},... | collective-permute-start | bytes 98312 | tf_op jit(solution)/shard_map/ppermute | solution.py:57
  63.0 9.2 %collective-permute-start.7 = (bf16[128,128]{1,0:T(8,128)(2,1)S(1)}, bf16[128,128]{1,0:T(8,128)(2,1)S(1)}, u32[]{:S(2)}, u32[]{:S(2)}) collective-permute-start(bf16[128,128]{1,0:T(8,128)(2,1)S(1)} %get-tuple-element.29), channel_id=1, source_target_pairs={{4,16},{12,24},{16,4},{24,12},{36,48},{44,56},{48,36},{56,44},{68,... | collective-permute-start | bytes 98312 | tf_op jit(solution)/shard_map/ppermute | solution.py:57
  67.6 4.6 %collective-permute-start.8 = (bf16[128,128]{1,0:T(8,128)(2,1)S(1)}, bf16[128,128]{1,0:T(8,128)(2,1)S(1)}, u32[]{:S(2)}, u32[]{:S(2)}) collective-permute-start(bf16[128,128]{1,0:T(8,128)(2,1)S(1)} %get-tuple-element.30), channel_id=1, source_target_pairs={{0,8},{4,12},{8,0},{12,4},{16,24},{20,28},{24,16},{28,20},{32,40},... | collective-permute-start | bytes 98312 | tf_op jit(solution)/shard_map/ppermute | solution.py:57
  68.0 14.2 %copy-start.4 = (bf16[1,4,512,128]{3,2,1,0:T(8,128)(2,1)S(1)}, bf16[1,4,512,128]{3,2,1,0:T(8,128)(2,1)}, u32[]{:S(2)}) copy-start(bf16[1,4,512,128]{3,2,1,0:T(8,128)(2,1)} %voxels.5) | copy-start | bytes 1572868
  68.0 14.2 %copy-start.10 = (s32[1,4]{1,0:T(1,128)S(1)}, s32[1,4]{1,0:T(1,128)}, u32[]{:S(2)}) copy-start(s32[1,4]{1,0:T(1,128)} %occupied.5) | copy-start | bytes 52
  68.0 14.2 %copy-start.13 = (bf16[27,128,128]{2,1,0:T(8,128)(2,1)S(1)}, bf16[27,128,128]{2,1,0:T(8,128)(2,1)}, u32[]{:S(2)}) copy-start(bf16[27,128,128]{2,1,0:T(8,128)(2,1)} %second_weight.3) | copy-start | bytes 2654212
  68.0 4.2 %collective-permute-start.9 = (bf16[128,128]{1,0:T(8,128)(2,1)S(1)}, bf16[128,128]{1,0:T(8,128)(2,1)S(1)}, u32[]{:S(2)}, u32[]{:S(2)}) collective-permute-start(bf16[128,128]{1,0:T(8,128)(2,1)S(1)} %get-tuple-element.31), channel_id=1, source_target_pairs={{8,32},{12,36},{24,48},{28,52},{32,8},{36,12},{48,24},{52,28},{72,... | collective-permute-start | bytes 98312 | tf_op jit(solution)/shard_map/ppermute | solution.py:57
  75.4 21.9 %all-to-all-start.1 = ((bf16[64,56,128]{2,1,0:T(8,128)(2,1)}), bf16[64,56,128]{2,1,0:T(8,128)(2,1)S(1)}, u32[]{:S(2)}, u32[]{:S(2)}) async-start(bf16[64,56,128]{2,1,0:T(8,128)(2,1)} %shard_map.89), calls=%async_computation.1 | async-start | bytes 1835008 | tf_op jit(solution)/shard_map/all_to_all | solution.py:412
  97.3 5.2 %collective-permute-start.11 = (bf16[3584,128]{1,0:T(8,128)(2,1)S(1)}, bf16[3584,128]{1,0:T(8,128)(2,1)S(1)}, u32[]{:S(2)}, u32[]{:S(2)}) collective-permute-start(bf16[3584,128]{1,0:T(8,128)(2,1)S(1)} %bitcast.4), channel_id=1, source_target_pairs={{0,4},{4,0},{1,5},{5,1},{2,6},{6,2},{3,7},{7,3},{8,12},{12,8},{9,1... | collective-permute-start | bytes 2752520 | tf_op jit(solution)/shard_map/ppermute | solution.py:424

commit v2 on v1

--- a/solution.py
+++ b/solution.py
@@ -1,5 +1,3 @@
-import functools
-
 import jax
 import jax.numpy as jnp
 from jax import lax
@@ -7,10 +5,12 @@
 from jax.experimental.pallas import tpu as pltpu
 from jax.sharding import PartitionSpec as P
 
+
 BF = jnp.bfloat16
 F32 = jnp.float32
 VMEM = pl.BlockSpec(memory_space=pltpu.VMEM)
-SMEM = pl.BlockSpec(memory_space=pltpu.SMEM)
+HBM = pl.BlockSpec(memory_space=pltpu.HBM)
+ANY = pl.BlockSpec(memory_space=pl.ANY)
 ROWS = 3456
 CHUNK = 56
 
@@ -54,7 +54,10 @@
 
 
 def exchange(sent):
-    return tuple(lax.ppermute(a, SPACE, pairs) for a, pairs in zip(sent, SWAPS))
+    got = []
+    for way in range(5):
+        got.append(lax.ppermute(sent[way], SPACE, SWAPS[way]))
+    return tuple(got)
 
 
 def remote_links(links, face, device):
@@ -204,39 +207,63 @@
             put(9 * ti + q, total[:, q * 128 : (q + 1) * 128])
 
 
-def load_masked(x, source, occupied):
-    for n in range(4):
-        keep = occupied[0, n].astype(F32)
-        x[n] = source[0, n].astype(F32) * keep
-
-
-def first_faces_kernel(voxels, cotangent, links, occupied, *rest):
-    sends, (x, g) = rest[:5], rest[5:]
+def fetch(sems, *pairs):
+    copies = [pltpu.make_async_copy(a, b, sems.at[q]) for q, (a, b) in enumerate(pairs)]
+    for copy in copies:
+        copy.start()
+    return copies
+
+
+def first_faces_kernel(voxels, cotangent, links_in, occupied_in, *rest):
+    sends, (masked, grad_out), (x, g, raw_x, raw_g, links, occupied, sems) = rest[:5], rest[5:7], rest[7:]
     device = lax.axis_index(SPACE)
-    load_masked(x, voxels, occupied)
-    load_masked(g, cotangent, occupied)
+    copies = fetch(
+        sems, (links_in, links), (occupied_in, occupied), (voxels, raw_x), (cotangent, raw_g)
+    )
+    copies[0].wait()
+    copies[1].wait()
+    for copy, raw, wide, kept in ((copies[2], raw_x, x, masked), (copies[3], raw_g, g, grad_out)):
+        copy.wait()
+        for n in range(4):
+            value = raw[0, n].astype(F32) * occupied[0, n].astype(F32)
+            wide[n] = value
+            kept[n] = value.astype(BF)
     pack_faces((x, g), links, device, sends)
 
 
-def hidden_faces_kernel(hidden, links, *rest):
-    sends, (x,) = rest[:5], rest[5:]
+def hidden_faces_kernel(hidden, links_in, *rest):
+    sends, (x, links, sems) = rest[:5], rest[5:]
     device = lax.axis_index(SPACE)
+    copies = fetch(sems, (links_in, links))
     for n in range(4):
         x[n] = hidden[n].astype(F32)
+    copies[0].wait()
     pack_faces((x,), links, device, sends)
 
 
 def main_kernel(
-    voxels, cotangent, links, occupied, first_weight, second_weight, g0, g1, g2, g3, g4,
+    masked, grad_out, links_in, occupied_in, first_in, second_in, g0, g1, g2, g3, g4,
     hidden, own_terms, other_terms,
     x, fx, fy, fz, wide, odd, wide_grad, odd_grad, pair_weights, slope, hidden_turned, grad_turned,
+    first_weight, second_weight, links, occupied, sems,
 ):
+    copies = fetch(
+        sems,
+        (links_in, links),
+        (occupied_in, occupied),
+        (first_in, first_weight),
+        (second_in, second_weight),
+    )
     device = lax.axis_index(SPACE)
     got = (g0, g1, g2, g3, g4)
     faces = (fx, fy, fz)
-    load_masked(x, voxels, occupied)
+    for n in range(4):
+        x[n] = masked[n].astype(F32)
+    copies[0].wait()
+    copies[1].wait()
     take_faces(x, links, device, got, 0, faces)
     build(wide, odd, x, faces)
+    copies[2].wait()
     lay_weights(pair_weights, lambda t: first_weight[t])
 
     def forward(n, carry):
@@ -251,9 +278,11 @@
 
     lax.fori_loop(0, 4, forward, 0)
 
-    load_masked(x, cotangent, occupied)
+    for n in range(4):
+        x[n] = grad_out[n].astype(F32)
     take_faces(x, links, device, got, 1, faces)
     build(wide_grad, odd_grad, x, faces)
+    copies[3].wait()
     lay_weights(pair_weights, lambda t: second_weight[26 - t].T)
 
     core = device & 1
@@ -288,22 +317,28 @@
 
 
 def last_kernel(
-    voxels, hidden, links, occupied, second_weight, g0, g1, g2, g3, g4,
+    masked, hidden, links_in, occupied_in, second_in, g0, g1, g2, g3, g4,
     output,
-    x, fx, fy, fz, wide, odd, pair_weights,
+    x, fx, fy, fz, wide, odd, pair_weights, second_weight, links, occupied, sems,
 ):
+    copies = fetch(
+        sems, (links_in, links), (occupied_in, occupied), (second_in, second_weight)
+    )
     device = lax.axis_index(SPACE)
     faces = (fx, fy, fz)
     for n in range(4):
         x[n] = hidden[n].astype(F32)
+    copies[0].wait()
+    copies[1].wait()
     take_faces(x, links, device, (g0, g1, g2, g3, g4), 0, faces)
     build(wide, odd, x, faces)
+    copies[2].wait()
     lay_weights(pair_weights, lambda t: second_weight[t])
 
     def forward(n, carry):
         keep = occupied[0, n].astype(F32)
         second = convolve(wide, odd, pair_weights, n)
-        output[0, n] = ((voxels[0, n].astype(F32) * keep + second) * keep).astype(BF)
+        output[0, n] = ((masked[n].astype(F32) + second) * keep).astype(BF)
         return carry
 
     lax.fori_loop(0, 4, forward, 0)
@@ -330,91 +365,120 @@
     lax.fori_loop(0, 64, put, 0, unroll=8)
 
 
-def finish_kernel(own, other, first_grad, second_grad):
+def finish(core_of_first, source, outs, wide, sems):
     core = lax.axis_index("core")
-
-    def put(mine, theirs):
-        mine[...] = own[pl.ds(0, ROWS), :].astype(F32)
-        theirs[...] = other[pl.ds(0, ROWS), :].astype(F32)
-
-    @pl.when(core == 0)
-    def _():
-        put(first_grad, second_grad)
-
-    @pl.when(core == 1)
-    def _():
-        put(second_grad, first_grad)
+    parts = 4
+    rows = ROWS // parts
+    for q in range(parts):
+        at = pl.ds(q * rows, rows)
+        wide[at, :] = source[at, :].astype(F32)
+        for out, there in zip(outs, (core == core_of_first, core != core_of_first)):
+
+            @pl.when(there)
+            def _():
+                pltpu.make_async_copy(wide.at[at], out.at[at], sems.at[q]).start()
+
+    for q in range(parts):
+        at = pl.ds(q * rows, rows)
+        pltpu.make_async_copy(wide.at[at], outs[0].at[at], sems.at[q]).wait()
+
+
+def finish_own_kernel(own, first_grad, second_grad, wide, sems):
+    finish(0, own, (first_grad, second_grad), wide, sems)
+
+
+def finish_other_kernel(other, first_in, second_in, first_grad, second_grad, wide, sems):
+    finish(1, other, (first_grad, second_grad), wide, sems)
 
 
 def send_shapes(fields):
     return tuple(jax.ShapeDtypeStruct((fields * w * 64, 128), BF) for w in (2, 2, 2, 2, 4))
 
 
-def call(kernel, outs, ins, scratch, limit, flops=0, nbytes=0, unread=0):
-    specs = [SMEM if a.dtype == jnp.int32 else VMEM for a in ins]
-    for at in range(len(ins) - unread, len(ins)):
-        specs[at] = pl.BlockSpec(memory_space=pl.ANY)
+def call(kernel, outs, ins, specs, scratch, limit, flops=0, nbytes=0, out_specs=VMEM, aliases={}):
     many = isinstance(outs, tuple)
+    ins = [
+        pltpu.with_memory_space_constraint(a, pltpu.HBM) if spec is HBM else a
+        for a, spec in zip(ins, specs)
+    ]
     return pl.pallas_call(
         kernel,
         out_shape=outs,
         in_specs=specs,
-        out_specs=tuple(VMEM for _ in outs) if many else VMEM,
+        out_specs=tuple(out_specs for _ in outs) if many else out_specs,
         scratch_shapes=scratch,
+        input_output_aliases=aliases,
         compiler_params=pltpu.CompilerParams(vmem_limit_bytes=limit << 20),
         cost_estimate=pl.CostEstimate(flops=flops, bytes_accessed=nbytes, transcendentals=0),
     )(*ins)
 
 
-def local(voxels, occupied, neighbours, first_weight, second_weight, cotangent):
+def step(voxels, occupied, neighbours, first_weight, second_weight, cotangent):
     field = pltpu.VMEM((4, 512, 128), F32)
+    raw = pltpu.VMEM((1, 4, 512, 128), BF)
+    links = pltpu.SMEM((1, 4, 6), jnp.int32)
+    flags = pltpu.SMEM((1, 4), jnp.int32)
+    weights = pltpu.VMEM((27, 128, 128), BF)
     sides = [pltpu.VMEM((4, 2, 64, 128), F32)] * 3
     padded = [pltpu.VMEM((3, 4, 10, 80, 128), BF), pltpu.VMEM((3, 4, 10, 64, 128), BF)]
     pairs = pltpu.VMEM((4608, 256), BF)
     turned = pltpu.VMEM((128, 2048), BF)
-
-    sent = call(
+    sems = pltpu.SemaphoreType.DMA((4,))
+    blocks = jax.ShapeDtypeStruct((4, 512, 128), BF)
+    terms_shape = jax.ShapeDtypeStruct((ROWS, 128), F32)
+
+    *sent, masked, grad_out = call(
         first_faces_kernel,
-        send_shapes(2),
+        send_shapes(2) + (blocks, blocks),
         (voxels, cotangent, neighbours, occupied),
-        [field, field],
-        8,
+        [HBM] * 4,
+        [field, field, raw, raw, links, flags, sems],
+        10,
         nbytes=2 << 20,
     )
     got = exchange(sent)
-    terms_shape = jax.ShapeDtypeStruct((ROWS, 128), F32)
     hidden, own, other = call(
         main_kernel,
-        (jax.ShapeDtypeStruct((4, 512, 128), BF), terms_shape, terms_shape),
-        (voxels, cotangent, neighbours, occupied, first_weight, second_weight) + got,
-        [field] + sides + padded + padded + [pairs, field, turned, turned],
+        (blocks, terms_shape, terms_shape),
+        (masked, grad_out, neighbours, occupied, first_weight, second_weight) + got,
+        [VMEM] * 2 + [HBM] * 4 + [VMEM] * 5,
+        [field] + sides + padded + padded + [pairs, field, turned, turned, weights, weights, links, flags, sems],
         32,
         flops=8 << 30,
         nbytes=8 << 20,
     )
     other = lax.ppermute(other, "core", PARTNER)
     chunks = jax.ShapeDtypeStruct((64 * CHUNK, 128), BF)
-    terms = call(pair_kernel, chunks, (own, other), [], 8, nbytes=4 << 20)
+    terms = call(pair_kernel, chunks, (own, other), [VMEM] * 2, [], 8, nbytes=4 << 20)
     parts = lax.all_to_all(
         terms.reshape(64, CHUNK, 128), PEERS, split_axis=0, concat_axis=0, tiled=True
     )
-    sent = call(hidden_faces_kernel, send_shapes(1), (hidden, neighbours), [field], 6, nbytes=1 << 20)
+    sent = call(
+        hidden_faces_kernel,
+        send_shapes(1),
+        (hidden, neighbours),
+        [VMEM, HBM],
+        [field, links, sems],
+        6,
+        nbytes=1 << 20,
+    )
     got = exchange(sent)
     spread = call(
         sum_kernel,
         jax.ShapeDtypeStruct((64, CHUNK, 128), BF),
-        (parts,) + got,
+        (parts,) + tuple(sent),
+        [VMEM] + [ANY] * 5,
         [],
         6,
         nbytes=2 << 20,
-        unread=5,
     )
     mine = lax.all_to_all(spread, PEERS, split_axis=0, concat_axis=0, tiled=True)
     output = call(
         last_kernel,
         jax.ShapeDtypeStruct((1, 4, 512, 128), BF),
-        (voxels, hidden, neighbours, occupied, second_weight) + got,
-        [field] + sides + padded + [pairs],
+        (masked, hidden, neighbours, occupied, second_weight) + got,
+        [VMEM] * 2 + [HBM] * 3 + [VMEM] * 5,
+        [field] + sides + padded + [pairs, weights, links, flags, sems],
         20,
         flops=3 << 30,
         nbytes=4 << 20,
@@ -422,8 +486,20 @@
     mine, output = lax.optimization_barrier((mine, output))
     mine = mine.reshape(64 * CHUNK, 128)
     theirs = lax.ppermute(mine, "core", PARTNER)
+    wide = pltpu.VMEM((ROWS, 128), F32)
+    grads = call(
+        finish_own_kernel, (terms_shape, terms_shape), (mine,), [VMEM], [wide, sems], 4, nbytes=3 << 20, out_specs=HBM
+    )
     first_grad, second_grad = call(
-        finish_kernel, (terms_shape, terms_shape), (mine, theirs), [], 10, nbytes=6 << 20
+        finish_other_kernel,
+        (terms_shape, terms_shape),
+        (theirs,) + tuple(grads),
+        [VMEM, HBM, HBM],
+        [wide, sems],
+        4,
+        nbytes=3 << 20,
+        out_specs=HBM,
+        aliases={1: 0, 2: 1},
     )
     return output, first_grad.reshape(27, 128, 128), second_grad.reshape(27, 128, 128)
 
@@ -439,7 +515,7 @@
         P("rep", SPACE, None, None),
     )
     return jax.shard_map(
-        local,
+        step,
         mesh=mesh,
         in_specs=placed,
         out_specs=(P("rep", SPACE, None, None), P(), P()),

time: 105 us -> 97.5 us (0.929); the launches traced: 105 us -> 95.7 us
  local copies, waits for them, and re-layouts: 9.18 us -> 0 us
  starting transfers between devices: 42.4 us -> 38.2 us
  waiting for transfers between devices: 23.1 us -> 25.8 us
  Pallas kernels: 29.1 us -> 30.8 us
    unnamed x28 -> x0, local copies, waits for them, and re-layouts: 9.18 us -> none
    all_to_all x2, waiting for transfers between devices: 11.5 us -> 15.1 us  [the longest x1 15.1 us: step(): lax.all_to_all(terms.reshape(64, CHUNK, 128), PEERS, split_axis=0, concat...]
    ppermute x12, starting transfers between devices: 24.2 us -> 22 us  [the longest x10 21.8 us: exchange(): got.append(lax.ppermute(sent[way], SPACE, SWAPS[way]))]
    all_to_all x2, starting transfers between devices: 18.2 us -> 16.2 us  [the longest x1 11.3 us: step(): lax.all_to_all(terms.reshape(64, CHUNK, 128), PEERS, split_axis=0, concat...]
    pallas_call x7 -> x8, Pallas kernels: 29.1 us -> 30.8 us  [call(): pl.pallas_call(kernel, out_shape=outs, in_specs=specs, out_specs=tuple((o...]
  transfers between devices with their start and end apart: 14 -> 14, of which waited for: 7 -> 6; matrix products, arithmetic and copies ran while one was open for 0% -> 0% of each run, Pallas kernels for 6% -> 9%
where the time goes in v2:
time: 97.5 us; the launch traced here: 95.7 us
  starting transfers between devices  38.2 us (39%)
  Pallas kernels  30.8 us (32%)
  waiting for transfers between devices  25.8 us (26%)
    pallas_call x8, Pallas kernels, call(): pl.pallas_call(kernel, out_shape=outs, in_specs=specs, out_specs=tuple((o...  30.8 us
    ppermute x10, starting transfers between devices, exchange(): got.append(lax.ppermute(sent[way], SPACE, SWAPS[way]))  21.8 us
    all_to_all x1, waiting for transfers between devices, step(): lax.all_to_all(terms.reshape(64, CHUNK, 128), PEERS, split_axis=0, concat...  15.1 us
    all_to_all x1, starting transfers between devices, step(): lax.all_to_all(terms.reshape(64, CHUNK, 128), PEERS, split_axis=0, concat...  11.3 us
    ppermute x10, waiting for transfers between devices, exchange(): got.append(lax.ppermute(sent[way], SPACE, SWAPS[way]))  5.8 us
    all_to_all x1, starting transfers between devices, step(): lax.all_to_all(spread, PEERS, split_axis=0, concat_axis=0, tiled=True)  4.86 us
    ppermute x1, waiting for transfers between devices, step(): other = lax.ppermute(other, 'core', PARTNER)  3.68 us
  transfers between devices with their start and end apart: 14, of which 6 were waited for; matrix products, arithmetic and copies ran while one was open for 0% of the time, Pallas kernels for 9%

profile of v2, /device:TPU:1, one launch (start us, length us, event | category | flops | bytes accessed | tf_op | source)
XLA Modules:
  0.0 95.7 jit_solution(9646376982065449011)
XLA Ops:
  0.6 1.6 %shard_map.85 = (bf16[256,128]{1,0:T(8,128)(2,1)S(1)}, bf16[256,128]{1,0:T(8,128)(2,1)S(1)}, bf16[256,128]{1,0:T(8,128)(2,1)S(1)}, bf16[256,128]{1,0:T(8,128)(2,...) custom-call(bf16[1,4,512,128]{3,2,1,0:T(8,128)(2,1)} %voxels.1, ...), custom_call_target="tpu_custom_call" | custom-call | bytes 2097152 | tf_op jit(solution)/shard_map/pallas_call | solution.py:404
  2.2 4.5 %collective-permute-start.4 = (bf16[512,128]{1,0:T(8,128)(2,1)S(1)}, bf16[512,128]{1,0:T(8,128)(2,1)S(1)}, u32[]{:S(2)}, u32[]{:S(2)}) collective-permute-start(bf16[512,128]{1,0:T(8,128)(2,1)S(1)} %get-tuple-element.30), channel_id=1, source_target_pairs={{0,64},{4,68},{8,72},{12,76},{16,80},{20,84},{24,88},{28,92},{32,9... | collective-permute-start | bytes 393224 | tf_op jit(solution)/shard_map/ppermute | solution.py:59
  6.7 1.0 %collective-permute-start = (bf16[256,128]{1,0:T(8,128)(2,1)S(1)}, bf16[256,128]{1,0:T(8,128)(2,1)S(1)}, u32[]{:S(2)}, u32[]{:S(2)}) collective-permute-start(bf16[256,128]{1,0:T(8,128)(2,1)S(1)} %get-tuple-element.26), channel_id=1, source_target_pairs={{0,4},{4,0},{8,12},{12,8},{16,20},{20,16},{24,28},{28,24},{32,36},... | collective-permute-start | bytes 196616 | tf_op jit(solution)/shard_map/ppermute | solution.py:59
  7.7 4.6 %collective-permute-start.1 = (bf16[256,128]{1,0:T(8,128)(2,1)S(1)}, bf16[256,128]{1,0:T(8,128)(2,1)S(1)}, u32[]{:S(2)}, u32[]{:S(2)}) collective-permute-start(bf16[256,128]{1,0:T(8,128)(2,1)S(1)} %get-tuple-element.27), channel_id=1, source_target_pairs={{4,16},{12,24},{16,4},{24,12},{36,48},{44,56},{48,36},{56,44},{68,... | collective-permute-start | bytes 196616 | tf_op jit(solution)/shard_map/ppermute | solution.py:59
  12.3 0.3 collective-permute-start.2
  12.6 0.7 collective-permute-start.3
  13.3 0.0 collective-permute-done.g0
  13.3 1.5 %collective-permute-done.1.g1 = bf16[256,128]{1,0:T(8,128)(2,1)S(1)} collective-permute-done((bf16[256,128]{1,0:T(8,128)(2,1)S(1)}, bf16[256,128]{1,0:T(8,128)(2,1)S(1)}, u32[]{:S(2)}, u32[]{:S(2)}) %collective-permute-start.1) | collective-permute-done | bytes 65568 | tf_op jit(solution)/shard_map/ppermute | solution.py:59
  14.8 1.0 %collective-permute-done.2.g2 = bf16[256,128]{1,0:T(8,128)(2,1)S(1)} collective-permute-done((bf16[256,128]{1,0:T(8,128)(2,1)S(1)}, bf16[256,128]{1,0:T(8,128)(2,1)S(1)}, u32[]{:S(2)}, u32[]{:S(2)}) %collective-permute-start.2) | collective-permute-done | bytes 65568 | tf_op jit(solution)/shard_map/ppermute | solution.py:59
  15.8 0.0 collective-permute-done.3.g3
  15.8 0.0 collective-permute-done.4.g4
  15.8 17.5 %shard_map.86 = (bf16[4,512,128]{2,1,0:T(8,128)(2,1)S(1)}, f32[3456,128]{1,0:T(8,128)S(1)}, f32[3456,128]{1,0:T(8,128)S(1)}) custom-call(bf16[4,512,128]{2,1,0:T(8,128)(2,1)S(1)} %get-tuple-element.24.masked, bf16[4,512,128]{2,1,0:T(8,128)(2,1)S(1)} %get-tuple-element.25.grad_out, s32[1,4,6]{2,1,0:T(4,128)} %links_in.7, s32[1,4]{1,0:T(1,128)} %occupied_in.5, ...), custom_call_target="tpu_custom_call" | custom-call | flops 8589934592 | bytes 8388608 | tf_op jit(solution)/shard_map/pallas_call | solution.py:404
  33.3 0.1 collective-permute-start.5
  33.4 3.7 %collective-permute-done.5.other = f32[3456,128]{1,0:T(8,128)S(1)} collective-permute-done((f32[3456,128]{1,0:T(8,128)S(1)}, f32[3456,128]{1,0:T(8,128)S(1)}, u32[]{:S(2)}, u32[]{:S(2)}) %collective-permute-start.5) | collective-permute-done | bytes 1769504 | tf_op jit(solution)/shard_map/ppermute | solution.py:450
  37.1 1.1 %shard_map.87 = bf16[3584,128]{1,0:T(8,128)(2,1)} custom-call(f32[3456,128]{1,0:T(8,128)S(1)} %get-tuple-element.31.own, f32[3456,128]{1,0:T(8,128)S(1)} %collective-permute-done.5.other), custom_call_target="tpu_custom_call" | custom-call | bytes 4194304 | tf_op jit(solution)/shard_map/pallas_call | solution.py:404
  38.1 11.3 %all-to-all-start = ((bf16[64,56,128]{2,1,0:T(8,128)(2,1)}), bf16[64,56,128]{2,1,0:T(8,128)(2,1)S(1)}, u32[]{:S(2)}, u32[]{:S(2)}) async-start(bf16[64,56,128]{2,1,0:T(8,128)(2,1)} %bitcast), calls=%async_computation | async-start | bytes 1835008 | tf_op jit(solution)/shard_map/all_to_all | solution.py:453
  49.5 1.1 %shard_map.88 = (bf16[128,128]{1,0:T(8,128)(2,1)S(1)}, bf16[128,128]{1,0:T(8,128)(2,1)S(1)}, bf16[128,128]{1,0:T(8,128)(2,1)S(1)}, bf16[128,128]{1,0:T(8,128)(2,1)S(1)}, bf16[256,128]{1,0:T(8,128)(2,1)S(1)}) custom-call(bf16[4,512,128]{2,1,0:T(8,128)(2,1)S(1)} %get-tuple-element.33.hidden, s32[1,4,6]{2,1,0:T(4,128)} %links_in.7), custom_call_target="tpu_custom_call" | custom-call | bytes 1048576 | tf_op jit(solution)/shard_map/pallas_call | solution.py:404
  50.6 15.1 %all-to-all-done.chunks = bf16[64,56,128]{2,1,0:T(8,128)(2,1)S(1)} async-done(((bf16[64,56,128]{2,1,0:T(8,128)(2,1)}), bf16[64,56,128]{2,1,0:T(8,128)(2,1)S(1)}, u32[]{:S(2)}, u32[]{:S(2)}) %all-to-all-start) | async-done | bytes 917536 | tf_op jit(solution)/shard_map/all_to_all | solution.py:453
  65.7 1.2 %shard_map.89 = bf16[64,56,128]{2,1,0:T(8,128)(2,1)} custom-call(bf16[64,56,128]{2,1,0:T(8,128)(2,1)S(1)} %all-to-all-done.chunks, bf16[128,128]{1,0:T(8,128)(2,1)S(1)} %get-tuple-element.34.rest_0_, bf16[128,128]{1,0:T(8,128)(2,1)S(1)} %get-tuple-element.35.rest_1_, bf16[128,128]{1,0:T(8,128)(2,1)S(1)} %get-tuple-element.36.rest_2_, ...), custom_call_target="tpu_custom_call" | custom-call | bytes 2097152 | tf_op jit(solution)/shard_map/pallas_call | solution.py:404
  66.9 4.9 %all-to-all-start.1 = ((bf16[64,56,128]{2,1,0:T(8,128)(2,1)}), bf16[64,56,128]{2,1,0:T(8,128)(2,1)S(1)}, u32[]{:S(2)}, u32[]{:S(2)}) async-start(bf16[64,56,128]{2,1,0:T(8,128)(2,1)} %shard_map.89), calls=%async_computation.1 | async-start | bytes 1835008 | tf_op jit(solution)/shard_map/all_to_all | solution.py:475
  71.7 2.7 %collective-permute-start.10 = (bf16[256,128]{1,0:T(8,128)(2,1)S(1)}, bf16[256,128]{1,0:T(8,128)(2,1)S(1)}, u32[]{:S(2)}, u32[]{:S(2)}) collective-permute-start(bf16[256,128]{1,0:T(8,128)(2,1)S(1)} %get-tuple-element.38.rest_4_), channel_id=1, source_target_pairs={{0,64},{4,68},{8,72},{12,76},{16,80},{20,84},{24,88},{28,92},{32,9... | collective-permute-start | bytes 196616 | tf_op jit(solution)/shard_map/ppermute | solution.py:59
  74.4 2.6 %collective-permute-start.6 = (bf16[128,128]{1,0:T(8,128)(2,1)S(1)}, bf16[128,128]{1,0:T(8,128)(2,1)S(1)}, u32[]{:S(2)}, u32[]{:S(2)}) collective-permute-start(bf16[128,128]{1,0:T(8,128)(2,1)S(1)} %get-tuple-element.34.rest_0_), channel_id=1, source_target_pairs={{0,4},{4,0},{8,12},{12,8},{16,20},{20,16},{24,28},{28,24},{32,36},... | collective-permute-start | bytes 98312 | tf_op jit(solution)/shard_map/ppermute | solution.py:59
  77.0 4.5 %collective-permute-start.7 = (bf16[128,128]{1,0:T(8,128)(2,1)S(1)}, bf16[128,128]{1,0:T(8,128)(2,1)S(1)}, u32[]{:S(2)}, u32[]{:S(2)}) collective-permute-start(bf16[128,128]{1,0:T(8,128)(2,1)S(1)} %get-tuple-element.35.rest_1_), channel_id=1, source_target_pairs={{4,16},{12,24},{16,4},{24,12},{36,48},{44,56},{48,36},{56,44},{68,... | collective-permute-start | bytes 98312 | tf_op jit(solution)/shard_map/ppermute | solution.py:59
  81.6 0.4 collective-permute-start.8
  82.0 0.7 collective-permute-start.9
  82.6 0.0 collective-permute-done.6.g0
  82.6 3.3 %collective-permute-done.7.g1 = bf16[128,128]{1,0:T(8,128)(2,1)S(1)} collective-permute-done((bf16[128,128]{1,0:T(8,128)(2,1)S(1)}, bf16[128,128]{1,0:T(8,128)(2,1)S(1)}, u32[]{:S(2)}, u32[]{:S(2)}) %collective-permute-start.7) | collective-permute-done | bytes 32800 | tf_op jit(solution)/shard_map/ppermute | solution.py:59
  85.9 0.0 collective-permute-done.8.g2
  85.9 0.0 collective-permute-done.9.g3
  85.9 0.0 collective-permute-done.10.g4
  85.9 5.8 %shard_map.90 = bf16[1,4,512,128]{3,2,1,0:T(8,128)(2,1)} custom-call(bf16[4,512,128]{2,1,0:T(8,128)(2,1)S(1)} %get-tuple-element.24.masked, bf16[4,512,128]{2,1,0:T(8,128)(2,1)S(1)} %get-tuple-element.33.hidden, s32[1,4,6]{2,1,0:T(4,128)} %links_in.7, s32[1,4]{1,0:T(1,128)} %occupied_in.5, bf16[27,128,128]{2,1,0:T(8,128)(2,1)} %second_in.3, ...), custom_call_target="tpu_custom_call" | custom-call | flops 3221225472 | bytes 4194304 | tf_op jit(solution)/shard_map/pallas_call | solution.py:404
  91.7 0.0 all-to-all-done.1
  91.7 0.1 collective-permute-start.11
  91.8 1.3 %shard_map.91 = (f32[3456,128]{1,0:T(8,128)}, f32[3456,128]{1,0:T(8,128)}) custom-call(bf16[3584,128]{1,0:T(8,128)(2,1)S(1)} %bitcast.5), custom_call_target="tpu_custom_call" | custom-call | bytes 3145728 | tf_op jit(solution)/shard_map/pallas_call | solution.py:404
  93.1 1.2 %collective-permute-done.11.other = bf16[3584,128]{1,0:T(8,128)(2,1)S(1)} collective-permute-done((bf16[3584,128]{1,0:T(8,128)(2,1)S(1)}, bf16[3584,128]{1,0:T(8,128)(2,1)S(1)}, u32[]{:S(2)}, u32[]{:S(2)}) %collective-permute-start.11) | collective-permute-done | bytes 917536 | tf_op jit(solution)/shard_map/ppermute | solution.py:488
  94.2 1.3 %shard_map.92 = (f32[3456,128]{1,0:T(8,128)}, f32[3456,128]{1,0:T(8,128)}) custom-call(bf16[3584,128]{1,0:T(8,128)(2,1)S(1)} %collective-permute-done.11.other, f32[3456,128]{1,0:T(8,128)} %get-tuple-element.41.first_in, f32[3456,128]{1,0:T(8,128)} %get-tuple-element.42.second_in), custom_call_target="tpu_custom_call", output_to_operand_aliasing={{0}: (1, {}), {1}: (2, {})} | custom-call | bytes 3145728 | tf_op jit(solution)/shard_map/pallas_call | solution.py:404
Async XLA Ops:
  2.2 13.6 %collective-permute-start.4 = (bf16[512,128]{1,0:T(8,128)(2,1)S(1)}, bf16[512,128]{1,0:T(8,128)(2,1)S(1)}, u32[]{:S(2)}, u32[]{:S(2)}) collective-permute-start(bf16[512,128]{1,0:T(8,128)(2,1)S(1)} %get-tuple-element.30), channel_id=1, source_target_pairs={{0,64},{4,68},{8,72},{12,76},{16,80},{20,84},{24,88},{28,92},{32,9... | collective-permute-start | bytes 393224 | tf_op jit(solution)/shard_map/ppermute | solution.py:59
  6.7 6.5 %collective-permute-start = (bf16[256,128]{1,0:T(8,128)(2,1)S(1)}, bf16[256,128]{1,0:T(8,128)(2,1)S(1)}, u32[]{:S(2)}, u32[]{:S(2)}) collective-permute-start(bf16[256,128]{1,0:T(8,128)(2,1)S(1)} %get-tuple-element.26), channel_id=1, source_target_pairs={{0,4},{4,0},{8,12},{12,8},{16,20},{20,16},{24,28},{28,24},{32,36},... | collective-permute-start | bytes 196616 | tf_op jit(solution)/shard_map/ppermute | solution.py:59
  7.7 7.1 %collective-permute-start.1 = (bf16[256,128]{1,0:T(8,128)(2,1)S(1)}, bf16[256,128]{1,0:T(8,128)(2,1)S(1)}, u32[]{:S(2)}, u32[]{:S(2)}) collective-permute-start(bf16[256,128]{1,0:T(8,128)(2,1)S(1)} %get-tuple-element.27), channel_id=1, source_target_pairs={{4,16},{12,24},{16,4},{24,12},{36,48},{44,56},{48,36},{56,44},{68,... | collective-permute-start | bytes 196616 | tf_op jit(solution)/shard_map/ppermute | solution.py:59
  12.3 3.5 %collective-permute-start.2 = (bf16[256,128]{1,0:T(8,128)(2,1)S(1)}, bf16[256,128]{1,0:T(8,128)(2,1)S(1)}, u32[]{:S(2)}, u32[]{:S(2)}) collective-permute-start(bf16[256,128]{1,0:T(8,128)(2,1)S(1)} %get-tuple-element.28), channel_id=1, source_target_pairs={{0,8},{4,12},{8,0},{12,4},{16,24},{20,28},{24,16},{28,20},{32,40},... | collective-permute-start | bytes 196616 | tf_op jit(solution)/shard_map/ppermute | solution.py:59
  12.6 3.2 %collective-permute-start.3 = (bf16[256,128]{1,0:T(8,128)(2,1)S(1)}, bf16[256,128]{1,0:T(8,128)(2,1)S(1)}, u32[]{:S(2)}, u32[]{:S(2)}) collective-permute-start(bf16[256,128]{1,0:T(8,128)(2,1)S(1)} %get-tuple-element.29), channel_id=1, source_target_pairs={{8,32},{12,36},{24,48},{28,52},{32,8},{36,12},{48,24},{52,28},{72,... | collective-permute-start | bytes 196616 | tf_op jit(solution)/shard_map/ppermute | solution.py:59
  33.3 3.8 %collective-permute-start.5 = (f32[3456,128]{1,0:T(8,128)S(1)}, f32[3456,128]{1,0:T(8,128)S(1)}, u32[]{:S(2)}, u32[]{:S(2)}) collective-permute-start(f32[3456,128]{1,0:T(8,128)S(1)} %get-tuple-element.32), channel_id=1, source_target_pairs={{0,4},{4,0},{1,5},{5,1},{2,6},{6,2},{3,7},{7,3},{8,12},{12,8},{9,1... | collective-permute-start | bytes 5308424 | tf_op jit(solution)/shard_map/ppermute | solution.py:450
  38.1 27.6 %all-to-all-start = ((bf16[64,56,128]{2,1,0:T(8,128)(2,1)}), bf16[64,56,128]{2,1,0:T(8,128)(2,1)S(1)}, u32[]{:S(2)}, u32[]{:S(2)}) async-start(bf16[64,56,128]{2,1,0:T(8,128)(2,1)} %bitcast), calls=%async_computation | async-start | bytes 1835008 | tf_op jit(solution)/shard_map/all_to_all | solution.py:453
  66.9 24.8 %all-to-all-start.1 = ((bf16[64,56,128]{2,1,0:T(8,128)(2,1)}), bf16[64,56,128]{2,1,0:T(8,128)(2,1)S(1)}, u32[]{:S(2)}, u32[]{:S(2)}) async-start(bf16[64,56,128]{2,1,0:T(8,128)(2,1)} %shard_map.89), calls=%async_computation.1 | async-start | bytes 1835008 | tf_op jit(solution)/shard_map/all_to_all | solution.py:475
  71.7 14.1 %collective-permute-start.10 = (bf16[256,128]{1,0:T(8,128)(2,1)S(1)}, bf16[256,128]{1,0:T(8,128)(2,1)S(1)}, u32[]{:S(2)}, u32[]{:S(2)}) collective-permute-start(bf16[256,128]{1,0:T(8,128)(2,1)S(1)} %get-tuple-element.38.rest_4_), channel_id=1, source_target_pairs={{0,64},{4,68},{8,72},{12,76},{16,80},{20,84},{24,88},{28,92},{32,9... | collective-permute-start | bytes 196616 | tf_op jit(solution)/shard_map/ppermute | solution.py:59
  74.4 8.2 %collective-permute-start.6 = (bf16[128,128]{1,0:T(8,128)(2,1)S(1)}, bf16[128,128]{1,0:T(8,128)(2,1)S(1)}, u32[]{:S(2)}, u32[]{:S(2)}) collective-permute-start(bf16[128,128]{1,0:T(8,128)(2,1)S(1)} %get-tuple-element.34.rest_0_), channel_id=1, source_target_pairs={{0,4},{4,0},{8,12},{12,8},{16,20},{20,16},{24,28},{28,24},{32,36},... | collective-permute-start | bytes 98312 | tf_op jit(solution)/shard_map/ppermute | solution.py:59
  77.0 8.9 %collective-permute-start.7 = (bf16[128,128]{1,0:T(8,128)(2,1)S(1)}, bf16[128,128]{1,0:T(8,128)(2,1)S(1)}, u32[]{:S(2)}, u32[]{:S(2)}) collective-permute-start(bf16[128,128]{1,0:T(8,128)(2,1)S(1)} %get-tuple-element.35.rest_1_), channel_id=1, source_target_pairs={{4,16},{12,24},{16,4},{24,12},{36,48},{44,56},{48,36},{56,44},{68,... | collective-permute-start | bytes 98312 | tf_op jit(solution)/shard_map/ppermute | solution.py:59
  81.6 4.3 %collective-permute-start.8 = (bf16[128,128]{1,0:T(8,128)(2,1)S(1)}, bf16[128,128]{1,0:T(8,128)(2,1)S(1)}, u32[]{:S(2)}, u32[]{:S(2)}) collective-permute-start(bf16[128,128]{1,0:T(8,128)(2,1)S(1)} %get-tuple-element.36.rest_2_), channel_id=1, source_target_pairs={{0,8},{4,12},{8,0},{12,4},{16,24},{20,28},{24,16},{28,20},{32,40},... | collective-permute-start | bytes 98312 | tf_op jit(solution)/shard_map/ppermute | solution.py:59
  82.0 3.9 %collective-permute-start.9 = (bf16[128,128]{1,0:T(8,128)(2,1)S(1)}, bf16[128,128]{1,0:T(8,128)(2,1)S(1)}, u32[]{:S(2)}, u32[]{:S(2)}) collective-permute-start(bf16[128,128]{1,0:T(8,128)(2,1)S(1)} %get-tuple-element.37.rest_3_), channel_id=1, source_target_pairs={{8,32},{12,36},{24,48},{28,52},{32,8},{36,12},{48,24},{52,28},{72,... | collective-permute-start | bytes 98312 | tf_op jit(solution)/shard_map/ppermute | solution.py:59
  91.7 2.6 %collective-permute-start.11 = (bf16[3584,128]{1,0:T(8,128)(2,1)S(1)}, bf16[3584,128]{1,0:T(8,128)(2,1)S(1)}, u32[]{:S(2)}, u32[]{:S(2)}) collective-permute-start(bf16[3584,128]{1,0:T(8,128)(2,1)S(1)} %bitcast.4), channel_id=1, source_target_pairs={{0,4},{4,0},{1,5},{5,1},{2,6},{6,2},{3,7},{7,3},{8,12},{12,8},{9,1... | collective-permute-start | bytes 2752520 | tf_op jit(solution)/shard_map/ppermute | solution.py:488

commit v3 on v2

--- a/solution.py
+++ b/solution.py
@@ -34,12 +34,8 @@
         elif kind == "z":
             z ^= 1
         elif kind == "xo":
-            if a not in (1, 2):
-                continue
             a = 3 - a
         elif kind == "yo":
-            if b not in (1, 2):
-                continue
             b = 3 - b
         pairs.append((s, owner_of(a, b, z)))
     return pairs
@@ -48,8 +44,8 @@
 SWAPS = tuple(swaps(kind) for kind in ("xe", "xo", "ye", "yo", "z"))
 
 
-SPACE = ("chip", "core")
-PEERS = ("chip", "rep")
+SPACE = ("z", "x", "core")
+PEERS = ("x", "rep", "z")
 PARTNER = ((0, 1), (1, 0))
 
 
@@ -231,6 +227,17 @@
     pack_faces((x, g), links, device, sends)
 
 
+def prepare_kernel(masked, grad_out, first_in, second_in, x, g, first_pairs, second_pairs, first_weight, second_weight, sems):
+    copies = fetch(sems, (first_in, first_weight), (second_in, second_weight))
+    for n in range(4):
+        x[n] = masked[n].astype(F32)
+        g[n] = grad_out[n].astype(F32)
+    copies[0].wait()
+    lay_weights(first_pairs, lambda t: first_weight[t])
+    copies[1].wait()
+    lay_weights(second_pairs, lambda t: second_weight[26 - t].T)
+
+
 def hidden_faces_kernel(hidden, links_in, *rest):
     sends, (x, links, sems) = rest[:5], rest[5:]
     device = lax.axis_index(SPACE)
@@ -242,33 +249,22 @@
 
 
 def main_kernel(
-    masked, grad_out, links_in, occupied_in, first_in, second_in, g0, g1, g2, g3, g4,
+    x, g, first_pairs, second_pairs, links_in, occupied_in, g0, g1, g2, g3, g4,
     hidden, own_terms, other_terms,
-    x, fx, fy, fz, wide, odd, wide_grad, odd_grad, pair_weights, slope, hidden_turned, grad_turned,
-    first_weight, second_weight, links, occupied, sems,
+    fx, fy, fz, wide, odd, wide_grad, odd_grad, slope, hidden_turned, grad_turned, links, occupied, sems,
 ):
-    copies = fetch(
-        sems,
-        (links_in, links),
-        (occupied_in, occupied),
-        (first_in, first_weight),
-        (second_in, second_weight),
-    )
+    copies = fetch(sems, (links_in, links), (occupied_in, occupied))
     device = lax.axis_index(SPACE)
     got = (g0, g1, g2, g3, g4)
     faces = (fx, fy, fz)
-    for n in range(4):
-        x[n] = masked[n].astype(F32)
     copies[0].wait()
     copies[1].wait()
     take_faces(x, links, device, got, 0, faces)
     build(wide, odd, x, faces)
-    copies[2].wait()
-    lay_weights(pair_weights, lambda t: first_weight[t])
 
     def forward(n, carry):
         keep = occupied[0, n].astype(F32)
-        first = convolve(wide, odd, pair_weights, n)
+        first = convolve(wide, odd, first_pairs, n)
         sigma = jax.nn.sigmoid(first)
         value = (first * sigma * keep).astype(BF)
         hidden[n] = value
@@ -278,12 +274,8 @@
 
     lax.fori_loop(0, 4, forward, 0)
 
-    for n in range(4):
-        x[n] = grad_out[n].astype(F32)
-    take_faces(x, links, device, got, 1, faces)
-    build(wide_grad, odd_grad, x, faces)
-    copies[3].wait()
-    lay_weights(pair_weights, lambda t: second_weight[26 - t].T)
+    take_faces(g, links, device, got, 1, faces)
+    build(wide_grad, odd_grad, g, faces)
 
     core = device & 1
 
@@ -304,7 +296,7 @@
     weight_terms(wide_grad, odd_grad, hidden_turned, put_second)
 
     def backward(n, carry):
-        grad = convolve(wide_grad, odd_grad, pair_weights, n) * slope[n]
+        grad = convolve(wide_grad, odd_grad, second_pairs, n) * slope[n]
         grad_turned[:, pl.ds(pl.multiple_of(n * 512, 512), 512)] = grad.astype(BF).T
         return carry
 
@@ -413,6 +405,10 @@
     )(*ins)
 
 
+def in_vmem(shape, dtype):
+    return pltpu.VMEM(shape, dtype)
+
+
 def step(voxels, occupied, neighbours, first_weight, second_weight, cotangent):
     field = pltpu.VMEM((4, 512, 128), F32)
     raw = pltpu.VMEM((1, 4, 512, 128), BF)
@@ -437,13 +433,23 @@
         nbytes=2 << 20,
     )
     got = exchange(sent)
+    prepared = call(
+        prepare_kernel,
+        (in_vmem((4, 512, 128), F32),) * 2 + (in_vmem((4608, 256), BF),) * 2,
+        (masked, grad_out, first_weight, second_weight),
+        [VMEM] * 2 + [HBM] * 2,
+        [weights, weights, sems],
+        6,
+        flops=1 << 20,
+        nbytes=8 << 20,
+    )
     hidden, own, other = call(
         main_kernel,
         (blocks, terms_shape, terms_shape),
-        (masked, grad_out, neighbours, occupied, first_weight, second_weight) + got,
-        [VMEM] * 2 + [HBM] * 4 + [VMEM] * 5,
-        [field] + sides + padded + padded + [pairs, field, turned, turned, weights, weights, links, flags, sems],
-        32,
+        tuple(prepared) + (neighbours, occupied) + got,
+        [VMEM] * 4 + [HBM] * 2 + [VMEM] * 5,
+        sides + padded + padded + [field, turned, turned, links, flags, sems],
+        26,
         flops=8 << 30,
         nbytes=8 << 20,
     )
@@ -505,7 +511,7 @@
 
 
 def solution(mesh):
-    mesh = jax.sharding.Mesh(mesh.devices.reshape(16, 2, 4), ("chip", "core", "rep"))
+    mesh = jax.sharding.Mesh(mesh.devices.reshape(4, 4, 2, 4), ("z", "x", "core", "rep"))
     placed = (
         P("rep", SPACE, None, None),
         P("rep", SPACE),

time: 97.5 us -> 93.1 us (0.955); the launches traced: 95.7 us -> 92.7 us
  starting transfers between devices: 38.2 us -> 33.9 us
  Pallas kernels: 30.8 us -> 32.1 us
    all_to_all x1, starting transfers between devices: 11.3 us -> 7.28 us  [step(): lax.all_to_all(terms.reshape(64, CHUNK, 128), PEERS, split_axis=0, concat...]
    ppermute x10, starting transfers between devices: 21.8 us -> 19.3 us  [exchange(): got.append(lax.ppermute(sent[way], SPACE, SWAPS[way]))]
    ppermute x1, starting transfers between devices: 0.09 us -> 1.4 us  [step(): other = lax.ppermute(other, 'core', PARTNER)]
    pallas_call x8 -> x9, Pallas kernels: 30.8 us -> 32.1 us  [call(): pl.pallas_call(kernel, out_shape=outs, in_specs=specs, out_specs=tuple((o...]
    ppermute x10, waiting for transfers between devices: 5.8 us -> 7 us  [exchange(): got.append(lax.ppermute(sent[way], SPACE, SWAPS[way]))]
  transfers between devices with their start and end apart: 14 -> 14, of which waited for: 6 -> 5; matrix products, arithmetic and copies ran while one was open for 0% -> 0% of each run, Pallas kernels for 9% -> 11%
where the time goes in v3:
time: 93.1 us; the launch traced here: 92.7 us
  starting transfers between devices  33.9 us (36%)
  Pallas kernels  32.1 us (34%)
  waiting for transfers between devices  25.9 us (28%)
    pallas_call x9, Pallas kernels, call(): pl.pallas_call(kernel, out_shape=outs, in_specs=specs, out_specs=tuple((o...  32.1 us
    ppermute x10, starting transfers between devices, exchange(): got.append(lax.ppermute(sent[way], SPACE, SWAPS[way]))  19.3 us
    all_to_all x1, waiting for transfers between devices, step(): lax.all_to_all(terms.reshape(64, CHUNK, 128), PEERS, split_axis=0, concat...  14.7 us
    all_to_all x1, starting transfers between devices, step(): lax.all_to_all(terms.reshape(64, CHUNK, 128), PEERS, split_axis=0, concat...  7.28 us
    ppermute x10, waiting for transfers between devices, exchange(): got.append(lax.ppermute(sent[way], SPACE, SWAPS[way]))  7 us
    all_to_all x1, starting transfers between devices, step(): lax.all_to_all(spread, PEERS, split_axis=0, concat_axis=0, tiled=True)  5.22 us
    ppermute x1, waiting for transfers between devices, step(): other = lax.ppermute(other, 'core', PARTNER)  3.32 us
  transfers between devices with their start and end apart: 14, of which 5 were waited for; matrix products, arithmetic and copies ran while one was open for 0% of the time, Pallas kernels for 11%

profile of v3, /device:TPU:1, one launch (start us, length us, event | category | flops | bytes accessed | tf_op | source)
XLA Modules:
  0.0 92.7 jit_solution(5273810893486119837)
XLA Ops:
  0.6 1.6 %shard_map.85 = (bf16[256,128]{1,0:T(8,128)(2,1)S(1)}, bf16[256,128]{1,0:T(8,128)(2,1)S(1)}, bf16[256,128]{1,0:T(8,128)(2,1)S(1)}, bf16[256,128]{1,0:T(8,128)(2,...) custom-call(bf16[1,4,512,128]{3,2,1,0:T(8,128)(2,1)} %voxels.1, ...), custom_call_target="tpu_custom_call" | custom-call | bytes 2097152 | tf_op jit(solution)/shard_map/pallas_call | solution.py:396
  2.2 4.5 %collective-permute-start.4 = (bf16[512,128]{1,0:T(8,128)(2,1)S(1)}, bf16[512,128]{1,0:T(8,128)(2,1)S(1)}, u32[]{:S(2)}, u32[]{:S(2)}) collective-permute-start(bf16[512,128]{1,0:T(8,128)(2,1)S(1)} %get-tuple-element.38), channel_id=1, source_target_pairs={{0,64},{4,68},{8,72},{12,76},{16,80},{20,84},{24,88},{28,92},{32,9... | collective-permute-start | bytes 393224 | tf_op jit(solution)/shard_map/ppermute | solution.py:55
  6.7 1.0 %collective-permute-start = (bf16[256,128]{1,0:T(8,128)(2,1)S(1)}, bf16[256,128]{1,0:T(8,128)(2,1)S(1)}, u32[]{:S(2)}, u32[]{:S(2)}) collective-permute-start(bf16[256,128]{1,0:T(8,128)(2,1)S(1)} %get-tuple-element.34), channel_id=1, source_target_pairs={{0,4},{4,0},{8,12},{12,8},{16,20},{20,16},{24,28},{28,24},{32,36},... | collective-permute-start | bytes 196616 | tf_op jit(solution)/shard_map/ppermute | solution.py:55
  7.7 2.7 %collective-permute-start.1 = (bf16[256,128]{1,0:T(8,128)(2,1)S(1)}, bf16[256,128]{1,0:T(8,128)(2,1)S(1)}, u32[]{:S(2)}, u32[]{:S(2)}) collective-permute-start(bf16[256,128]{1,0:T(8,128)(2,1)S(1)} %get-tuple-element.35), channel_id=1, source_target_pairs={{0,20},{4,16},{8,28},{12,24},{16,4},{20,0},{24,12},{28,8},{32,52},... | collective-permute-start | bytes 196616 | tf_op jit(solution)/shard_map/ppermute | solution.py:55
  10.4 0.2 collective-permute-start.2
  10.6 1.6 %collective-permute-start.3 = (bf16[256,128]{1,0:T(8,128)(2,1)S(1)}, bf16[256,128]{1,0:T(8,128)(2,1)S(1)}, u32[]{:S(2)}, u32[]{:S(2)}) collective-permute-start(bf16[256,128]{1,0:T(8,128)(2,1)S(1)} %get-tuple-element.37), channel_id=1, source_target_pairs={{0,40},{4,44},{8,32},{12,36},{16,56},{20,60},{24,48},{28,52},{32,8... | collective-permute-start | bytes 196616 | tf_op jit(solution)/shard_map/ppermute | solution.py:55
  12.2 1.9 %shard_map.86 = (f32[4,512,128]{2,1,0:T(8,128)S(1)}, f32[4,512,128]{2,1,0:T(8,128)S(1)}, bf16[4608,256]{1,0:T(8,128)(2,1)S(1)}, bf16[4608,256]{1,0:T(8,128)(2,1)S(1)}) custom-call(bf16[4,512,128]{2,1,0:T(8,128)(2,1)S(1)} %get-tuple-element.28.masked, bf16[4,512,128]{2,1,0:T(8,128)(2,1)S(1)} %get-tuple-element.29.grad_out, bf16[27,128,128]{2,1,0:T(8,128)(2,1)} %first_in.1, ...), custom_call_target="tpu_custom_call" | custom-call | flops 1048576 | bytes 8388608 | tf_op jit(solution)/shard_map/pallas_call | solution.py:396
  14.1 0.0 collective-permute-done.g0
  14.1 0.0 collective-permute-done.1.g1
  14.1 0.0 collective-permute-done.2.g2
  14.1 1.4 %collective-permute-done.3.g3 = bf16[256,128]{1,0:T(8,128)(2,1)S(1)} collective-permute-done((bf16[256,128]{1,0:T(8,128)(2,1)S(1)}, bf16[256,128]{1,0:T(8,128)(2,1)S(1)}, u32[]{:S(2)}, u32[]{:S(2)}) %collective-permute-start.3) | collective-permute-done | bytes 65568 | tf_op jit(solution)/shard_map/ppermute | solution.py:55
  15.5 0.0 collective-permute-done.4.g4
  15.5 17.1 %shard_map.87 = (bf16[4,512,128]{2,1,0:T(8,128)(2,1)S(1)}, f32[3456,128]{1,0:T(8,128)S(1)}, f32[3456,128]{1,0:T(8,128)S(1)}) custom-call(f32[4,512,128]{2,1,0:T(8,128)S(1)} %get-tuple-element.30.x, f32[4,512,128]{2,1,0:T(8,128)S(1)} %get-tuple-element.31.g, bf16[4608,256]{1,0:T(8,128)(2,1)S(1)} %get-tuple-element.32.first_pairs, ...), custom_call_target="tpu_custom_call" | custom-call | flops 8589934592 | bytes 8388608 | tf_op jit(solution)/shard_map/pallas_call | solution.py:396
  32.7 1.4 %collective-permute-start.5 = (f32[3456,128]{1,0:T(8,128)S(1)}, f32[3456,128]{1,0:T(8,128)S(1)}, u32[]{:S(2)}, u32[]{:S(2)}) collective-permute-start(f32[3456,128]{1,0:T(8,128)S(1)} %get-tuple-element.40), channel_id=1, source_target_pairs={{0,4},{4,0},{1,5},{5,1},{2,6},{6,2},{3,7},{7,3},{8,12},{12,8},{9,1... | collective-permute-start | bytes 5308424 | tf_op jit(solution)/shard_map/ppermute | solution.py:456
  34.1 3.3 %collective-permute-done.5.other = f32[3456,128]{1,0:T(8,128)S(1)} collective-permute-done((f32[3456,128]{1,0:T(8,128)S(1)}, f32[3456,128]{1,0:T(8,128)S(1)}, u32[]{:S(2)}, u32[]{:S(2)}) %collective-permute-start.5) | collective-permute-done | bytes 1769504 | tf_op jit(solution)/shard_map/ppermute | solution.py:456
  37.4 1.1 %shard_map.88 = bf16[3584,128]{1,0:T(8,128)(2,1)} custom-call(f32[3456,128]{1,0:T(8,128)S(1)} %get-tuple-element.39.own, f32[3456,128]{1,0:T(8,128)S(1)} %collective-permute-done.5.other), custom_call_target="tpu_custom_call" | custom-call | bytes 4194304 | tf_op jit(solution)/shard_map/pallas_call | solution.py:396
  38.5 7.3 %all-to-all-start = ((bf16[64,56,128]{2,1,0:T(8,128)(2,1)}), bf16[64,56,128]{2,1,0:T(8,128)(2,1)S(1)}, u32[]{:S(2)}, u32[]{:S(2)}) async-start(bf16[64,56,128]{2,1,0:T(8,128)(2,1)} %bitcast), calls=%async_computation | async-start | bytes 1835008 | tf_op jit(solution)/shard_map/all_to_all | solution.py:459
  45.7 1.0 %shard_map.89 = (bf16[128,128]{1,0:T(8,128)(2,1)S(1)}, bf16[128,128]{1,0:T(8,128)(2,1)S(1)}, bf16[128,128]{1,0:T(8,128)(2,1)S(1)}, bf16[128,128]{1,0:T(8,128)(2,1)S(1)}, bf16[256,128]{1,0:T(8,128)(2,1)S(1)}) custom-call(bf16[4,512,128]{2,1,0:T(8,128)(2,1)S(1)} %get-tuple-element.41.hidden, s32[1,4,6]{2,1,0:T(4,128)} %links_in.7), custom_call_target="tpu_custom_call" | custom-call | bytes 1048576 | tf_op jit(solution)/shard_map/pallas_call | solution.py:396
  46.7 14.7 %all-to-all-done.chunks = bf16[64,56,128]{2,1,0:T(8,128)(2,1)S(1)} async-done(((bf16[64,56,128]{2,1,0:T(8,128)(2,1)}), bf16[64,56,128]{2,1,0:T(8,128)(2,1)S(1)}, u32[]{:S(2)}, u32[]{:S(2)}) %all-to-all-start) | async-done | bytes 917536 | tf_op jit(solution)/shard_map/all_to_all | solution.py:459
  61.4 1.2 %shard_map.90 = bf16[64,56,128]{2,1,0:T(8,128)(2,1)} custom-call(bf16[64,56,128]{2,1,0:T(8,128)(2,1)S(1)} %all-to-all-done.chunks, bf16[128,128]{1,0:T(8,128)(2,1)S(1)} %get-tuple-element.42.rest_0_, bf16[128,128]{1,0:T(8,128)(2,1)S(1)} %get-tuple-element.43.rest_1_, bf16[128,128]{1,0:T(8,128)(2,1)S(1)} %get-tuple-element.44.rest_2_, ...), custom_call_target="tpu_custom_call" | custom-call | bytes 2097152 | tf_op jit(solution)/shard_map/pallas_call | solution.py:396
  62.6 5.2 %all-to-all-start.1 = ((bf16[64,56,128]{2,1,0:T(8,128)(2,1)}), bf16[64,56,128]{2,1,0:T(8,128)(2,1)S(1)}, u32[]{:S(2)}, u32[]{:S(2)}) async-start(bf16[64,56,128]{2,1,0:T(8,128)(2,1)} %shard_map.90), calls=%async_computation.1 | async-start | bytes 1835008 | tf_op jit(solution)/shard_map/all_to_all | solution.py:481
  67.8 2.6 %collective-permute-start.10 = (bf16[256,128]{1,0:T(8,128)(2,1)S(1)}, bf16[256,128]{1,0:T(8,128)(2,1)S(1)}, u32[]{:S(2)}, u32[]{:S(2)}) collective-permute-start(bf16[256,128]{1,0:T(8,128)(2,1)S(1)} %get-tuple-element.46.rest_4_), channel_id=1, source_target_pairs={{0,64},{4,68},{8,72},{12,76},{16,80},{20,84},{24,88},{28,92},{32,9... | collective-permute-start | bytes 196616 | tf_op jit(solution)/shard_map/ppermute | solution.py:55
  70.4 2.6 %collective-permute-start.6 = (bf16[128,128]{1,0:T(8,128)(2,1)S(1)}, bf16[128,128]{1,0:T(8,128)(2,1)S(1)}, u32[]{:S(2)}, u32[]{:S(2)}) collective-permute-start(bf16[128,128]{1,0:T(8,128)(2,1)S(1)} %get-tuple-element.42.rest_0_), channel_id=1, source_target_pairs={{0,4},{4,0},{8,12},{12,8},{16,20},{20,16},{24,28},{28,24},{32,36},... | collective-permute-start | bytes 98312 | tf_op jit(solution)/shard_map/ppermute | solution.py:55
  73.0 2.7 %collective-permute-start.7 = (bf16[128,128]{1,0:T(8,128)(2,1)S(1)}, bf16[128,128]{1,0:T(8,128)(2,1)S(1)}, u32[]{:S(2)}, u32[]{:S(2)}) collective-permute-start(bf16[128,128]{1,0:T(8,128)(2,1)S(1)} %get-tuple-element.43.rest_1_), channel_id=1, source_target_pairs={{0,20},{4,16},{8,28},{12,24},{16,4},{20,0},{24,12},{28,8},{32,52},... | collective-permute-start | bytes 98312 | tf_op jit(solution)/shard_map/ppermute | solution.py:55
  75.7 0.4 collective-permute-start.8
  76.1 1.1 %collective-permute-start.9 = (bf16[128,128]{1,0:T(8,128)(2,1)S(1)}, bf16[128,128]{1,0:T(8,128)(2,1)S(1)}, u32[]{:S(2)}, u32[]{:S(2)}) collective-permute-start(bf16[128,128]{1,0:T(8,128)(2,1)S(1)} %get-tuple-element.45.rest_3_), channel_id=1, source_target_pairs={{0,40},{4,44},{8,32},{12,36},{16,56},{20,60},{24,48},{28,52},{32,8... | collective-permute-start | bytes 98312 | tf_op jit(solution)/shard_map/ppermute | solution.py:55
  77.1 0.0 collective-permute-done.6.g0
  77.1 5.6 %collective-permute-done.7.g1 = bf16[128,128]{1,0:T(8,128)(2,1)S(1)} collective-permute-done((bf16[128,128]{1,0:T(8,128)(2,1)S(1)}, bf16[128,128]{1,0:T(8,128)(2,1)S(1)}, u32[]{:S(2)}, u32[]{:S(2)}) %collective-permute-start.7) | collective-permute-done | bytes 32800 | tf_op jit(solution)/shard_map/ppermute | solution.py:55
  82.7 0.0 collective-permute-done.8.g2
  82.7 0.0 collective-permute-done.9.g3
  82.7 0.0 collective-permute-done.10.g4
  82.8 5.8 %shard_map.91 = bf16[1,4,512,128]{3,2,1,0:T(8,128)(2,1)} custom-call(bf16[4,512,128]{2,1,0:T(8,128)(2,1)S(1)} %get-tuple-element.28.masked, bf16[4,512,128]{2,1,0:T(8,128)(2,1)S(1)} %get-tuple-element.41.hidden, s32[1,4,6]{2,1,0:T(4,128)} %links_in.7, s32[1,4]{1,0:T(1,128)} %occupied_in.5, bf16[27,128,128]{2,1,0:T(8,128)(2,1)} %second_in.3, ...), custom_call_target="tpu_custom_call" | custom-call | flops 3221225472 | bytes 4194304 | tf_op jit(solution)/shard_map/pallas_call | solution.py:396
  88.5 0.0 all-to-all-done.1
  88.5 0.6 collective-permute-start.11
  89.2 1.3 %shard_map.92 = (f32[3456,128]{1,0:T(8,128)}, f32[3456,128]{1,0:T(8,128)}) custom-call(bf16[3584,128]{1,0:T(8,128)(2,1)S(1)} %bitcast.5), custom_call_target="tpu_custom_call" | custom-call | bytes 3145728 | tf_op jit(solution)/shard_map/pallas_call | solution.py:396
  90.4 0.8 collective-permute-done.11.other
  91.3 1.3 %shard_map.93 = (f32[3456,128]{1,0:T(8,128)}, f32[3456,128]{1,0:T(8,128)}) custom-call(bf16[3584,128]{1,0:T(8,128)(2,1)S(1)} %collective-permute-done.11.other, f32[3456,128]{1,0:T(8,128)} %get-tuple-element.49.first_in, f32[3456,128]{1,0:T(8,128)} %get-tuple-element.50.second_in), custom_call_target="tpu_custom_call", output_to_operand_aliasing={{0}: (1, {}), {1}: (2, {})} | custom-call | bytes 3145728 | tf_op jit(solution)/shard_map/pallas_call | solution.py:396
Async XLA Ops:
  2.2 13.3 %collective-permute-start.4 = (bf16[512,128]{1,0:T(8,128)(2,1)S(1)}, bf16[512,128]{1,0:T(8,128)(2,1)S(1)}, u32[]{:S(2)}, u32[]{:S(2)}) collective-permute-start(bf16[512,128]{1,0:T(8,128)(2,1)S(1)} %get-tuple-element.38), channel_id=1, source_target_pairs={{0,64},{4,68},{8,72},{12,76},{16,80},{20,84},{24,88},{28,92},{32,9... | collective-permute-start | bytes 393224 | tf_op jit(solution)/shard_map/ppermute | solution.py:55
  6.7 7.4 %collective-permute-start = (bf16[256,128]{1,0:T(8,128)(2,1)S(1)}, bf16[256,128]{1,0:T(8,128)(2,1)S(1)}, u32[]{:S(2)}, u32[]{:S(2)}) collective-permute-start(bf16[256,128]{1,0:T(8,128)(2,1)S(1)} %get-tuple-element.34), channel_id=1, source_target_pairs={{0,4},{4,0},{8,12},{12,8},{16,20},{20,16},{24,28},{28,24},{32,36},... | collective-permute-start | bytes 196616 | tf_op jit(solution)/shard_map/ppermute | solution.py:55
  7.7 6.4 %collective-permute-start.1 = (bf16[256,128]{1,0:T(8,128)(2,1)S(1)}, bf16[256,128]{1,0:T(8,128)(2,1)S(1)}, u32[]{:S(2)}, u32[]{:S(2)}) collective-permute-start(bf16[256,128]{1,0:T(8,128)(2,1)S(1)} %get-tuple-element.35), channel_id=1, source_target_pairs={{0,20},{4,16},{8,28},{12,24},{16,4},{20,0},{24,12},{28,8},{32,52},... | collective-permute-start | bytes 196616 | tf_op jit(solution)/shard_map/ppermute | solution.py:55
  10.4 3.8 %collective-permute-start.2 = (bf16[256,128]{1,0:T(8,128)(2,1)S(1)}, bf16[256,128]{1,0:T(8,128)(2,1)S(1)}, u32[]{:S(2)}, u32[]{:S(2)}) collective-permute-start(bf16[256,128]{1,0:T(8,128)(2,1)S(1)} %get-tuple-element.36), channel_id=1, source_target_pairs={{0,8},{4,12},{8,0},{12,4},{16,24},{20,28},{24,16},{28,20},{32,40},... | collective-permute-start | bytes 196616 | tf_op jit(solution)/shard_map/ppermute | solution.py:55
  10.6 4.9 %collective-permute-start.3 = (bf16[256,128]{1,0:T(8,128)(2,1)S(1)}, bf16[256,128]{1,0:T(8,128)(2,1)S(1)}, u32[]{:S(2)}, u32[]{:S(2)}) collective-permute-start(bf16[256,128]{1,0:T(8,128)(2,1)S(1)} %get-tuple-element.37), channel_id=1, source_target_pairs={{0,40},{4,44},{8,32},{12,36},{16,56},{20,60},{24,48},{28,52},{32,8... | collective-permute-start | bytes 196616 | tf_op jit(solution)/shard_map/ppermute | solution.py:55
  32.7 4.7 %collective-permute-start.5 = (f32[3456,128]{1,0:T(8,128)S(1)}, f32[3456,128]{1,0:T(8,128)S(1)}, u32[]{:S(2)}, u32[]{:S(2)}) collective-permute-start(f32[3456,128]{1,0:T(8,128)S(1)} %get-tuple-element.40), channel_id=1, source_target_pairs={{0,4},{4,0},{1,5},{5,1},{2,6},{6,2},{3,7},{7,3},{8,12},{12,8},{9,1... | collective-permute-start | bytes 5308424 | tf_op jit(solution)/shard_map/ppermute | solution.py:456
  38.5 23.0 %all-to-all-start = ((bf16[64,56,128]{2,1,0:T(8,128)(2,1)}), bf16[64,56,128]{2,1,0:T(8,128)(2,1)S(1)}, u32[]{:S(2)}, u32[]{:S(2)}) async-start(bf16[64,56,128]{2,1,0:T(8,128)(2,1)} %bitcast), calls=%async_computation | async-start | bytes 1835008 | tf_op jit(solution)/shard_map/all_to_all | solution.py:459
  62.6 26.0 %all-to-all-start.1 = ((bf16[64,56,128]{2,1,0:T(8,128)(2,1)}), bf16[64,56,128]{2,1,0:T(8,128)(2,1)S(1)}, u32[]{:S(2)}, u32[]{:S(2)}) async-start(bf16[64,56,128]{2,1,0:T(8,128)(2,1)} %shard_map.90), calls=%async_computation.1 | async-start | bytes 1835008 | tf_op jit(solution)/shard_map/all_to_all | solution.py:481
  67.8 14.9 %collective-permute-start.10 = (bf16[256,128]{1,0:T(8,128)(2,1)S(1)}, bf16[256,128]{1,0:T(8,128)(2,1)S(1)}, u32[]{:S(2)}, u32[]{:S(2)}) collective-permute-start(bf16[256,128]{1,0:T(8,128)(2,1)S(1)} %get-tuple-element.46.rest_4_), channel_id=1, source_target_pairs={{0,64},{4,68},{8,72},{12,76},{16,80},{20,84},{24,88},{28,92},{32,9... | collective-permute-start | bytes 196616 | tf_op jit(solution)/shard_map/ppermute | solution.py:55
  70.4 6.7 %collective-permute-start.6 = (bf16[128,128]{1,0:T(8,128)(2,1)S(1)}, bf16[128,128]{1,0:T(8,128)(2,1)S(1)}, u32[]{:S(2)}, u32[]{:S(2)}) collective-permute-start(bf16[128,128]{1,0:T(8,128)(2,1)S(1)} %get-tuple-element.42.rest_0_), channel_id=1, source_target_pairs={{0,4},{4,0},{8,12},{12,8},{16,20},{20,16},{24,28},{28,24},{32,36},... | collective-permute-start | bytes 98312 | tf_op jit(solution)/shard_map/ppermute | solution.py:55
  73.0 9.8 %collective-permute-start.7 = (bf16[128,128]{1,0:T(8,128)(2,1)S(1)}, bf16[128,128]{1,0:T(8,128)(2,1)S(1)}, u32[]{:S(2)}, u32[]{:S(2)}) collective-permute-start(bf16[128,128]{1,0:T(8,128)(2,1)S(1)} %get-tuple-element.43.rest_1_), channel_id=1, source_target_pairs={{0,20},{4,16},{8,28},{12,24},{16,4},{20,0},{24,12},{28,8},{32,52},... | collective-permute-start | bytes 98312 | tf_op jit(solution)/shard_map/ppermute | solution.py:55
  75.7 7.1 %collective-permute-start.8 = (bf16[128,128]{1,0:T(8,128)(2,1)S(1)}, bf16[128,128]{1,0:T(8,128)(2,1)S(1)}, u32[]{:S(2)}, u32[]{:S(2)}) collective-permute-start(bf16[128,128]{1,0:T(8,128)(2,1)S(1)} %get-tuple-element.44.rest_2_), channel_id=1, source_target_pairs={{0,8},{4,12},{8,0},{12,4},{16,24},{20,28},{24,16},{28,20},{32,40},... | collective-permute-start | bytes 98312 | tf_op jit(solution)/shard_map/ppermute | solution.py:55
  76.1 6.7 %collective-permute-start.9 = (bf16[128,128]{1,0:T(8,128)(2,1)S(1)}, bf16[128,128]{1,0:T(8,128)(2,1)S(1)}, u32[]{:S(2)}, u32[]{:S(2)}) collective-permute-start(bf16[128,128]{1,0:T(8,128)(2,1)S(1)} %get-tuple-element.45.rest_3_), channel_id=1, source_target_pairs={{0,40},{4,44},{8,32},{12,36},{16,56},{20,60},{24,48},{28,52},{32,8... | collective-permute-start | bytes 98312 | tf_op jit(solution)/shard_map/ppermute | solution.py:55
  88.5 2.7 %collective-permute-start.11 = (bf16[3584,128]{1,0:T(8,128)(2,1)S(1)}, bf16[3584,128]{1,0:T(8,128)(2,1)S(1)}, u32[]{:S(2)}, u32[]{:S(2)}) collective-permute-start(bf16[3584,128]{1,0:T(8,128)(2,1)S(1)} %bitcast.4), channel_id=1, source_target_pairs={{0,4},{4,0},{1,5},{5,1},{2,6},{6,2},{3,7},{7,3},{8,12},{12,8},{9,1... | collective-permute-start | bytes 2752520 | tf_op jit(solution)/shard_map/ppermute | solution.py:494

commit v4 on v3

--- a/solution.py
+++ b/solution.py
@@ -12,6 +12,7 @@
 HBM = pl.BlockSpec(memory_space=pltpu.HBM)
 ANY = pl.BlockSpec(memory_space=pl.ANY)
 ROWS = 3456
+SLOTS = 2
 CHUNK = 56
 
 
@@ -168,12 +169,12 @@
         for tj in range(3):
             for tk in range(3):
                 columns.append(
-                    jnp.concatenate([tap(wide, odd, n, 2 * p + layer, tj, tk) for p in range(4)], axis=0)
+                    jnp.concatenate([tap(wide, odd, SLOTS * n + q, 2 * p + layer, tj, tk) for q in range(SLOTS) for p in range(4)], axis=0)
                 )
     group = jnp.concatenate(columns, axis=1)
     both = jnp.dot(group, pair_weights[...], preferred_element_type=F32)
     rows = []
-    for p in range(4):
+    for p in range(4 * SLOTS):
         for half in range(2):
             rows.append(both[p * 64 : (p + 1) * 64, half * 128 : (half + 1) * 128])
     return jnp.concatenate(rows, axis=0)
@@ -210,31 +211,39 @@
     return copies
 
 
-def first_faces_kernel(voxels, cotangent, links_in, occupied_in, *rest):
-    sends, (masked, grad_out), (x, g, raw_x, raw_g, links, occupied, sems) = rest[:5], rest[5:7], rest[7:]
+def first_faces_kernel(voxels, cotangent, links_in, *rest):
+    sends, (x, g, raw_x, raw_g, links, sems) = rest[:5], rest[5:]
     device = lax.axis_index(SPACE)
-    copies = fetch(
-        sems, (links_in, links), (occupied_in, occupied), (voxels, raw_x), (cotangent, raw_g)
-    )
-    copies[0].wait()
-    copies[1].wait()
-    for copy, raw, wide, kept in ((copies[2], raw_x, x, masked), (copies[3], raw_g, g, grad_out)):
+    copies = fetch(sems, (links_in, links), (voxels, raw_x), (cotangent, raw_g))
+    for copy, raw, wide in ((copies[1], raw_x, x), (copies[2], raw_g, g)):
         copy.wait()
         for n in range(4):
-            value = raw[0, n].astype(F32) * occupied[0, n].astype(F32)
-            wide[n] = value
-            kept[n] = value.astype(BF)
+            wide[n] = raw[0, n].astype(F32)
+    copies[0].wait()
     pack_faces((x, g), links, device, sends)
 
 
-def prepare_kernel(masked, grad_out, first_in, second_in, x, g, first_pairs, second_pairs, first_weight, second_weight, sems):
-    copies = fetch(sems, (first_in, first_weight), (second_in, second_weight))
-    for n in range(4):
-        x[n] = masked[n].astype(F32)
-        g[n] = grad_out[n].astype(F32)
+def prepare_kernel(
+    voxels, cotangent, occupied_in, first_in, second_in,
+    x, g, first_pairs, second_pairs,
+    raw_x, raw_g, first_weight, second_weight, occupied, sems,
+):
+    copies = fetch(
+        sems,
+        (occupied_in, occupied),
+        (voxels, raw_x),
+        (cotangent, raw_g),
+        (first_in, first_weight),
+        (second_in, second_weight),
+    )
     copies[0].wait()
+    for copy, raw, wide in ((copies[1], raw_x, x), (copies[2], raw_g, g)):
+        copy.wait()
+        for n in range(4):
+            wide[n] = raw[0, n].astype(F32) * occupied[0, n].astype(F32)
+    copies[3].wait()
     lay_weights(first_pairs, lambda t: first_weight[t])
-    copies[1].wait()
+    copies[4].wait()
     lay_weights(second_pairs, lambda t: second_weight[26 - t].T)
 
 
@@ -263,16 +272,19 @@
     build(wide, odd, x, faces)
 
     def forward(n, carry):
-        keep = occupied[0, n].astype(F32)
-        first = convolve(wide, odd, first_pairs, n)
-        sigma = jax.nn.sigmoid(first)
-        value = (first * sigma * keep).astype(BF)
-        hidden[n] = value
-        hidden_turned[:, pl.ds(pl.multiple_of(n * 512, 512), 512)] = value.T
-        slope[n] = sigma * (1.0 + first * (1.0 - sigma)) * keep
+        firsts = convolve(wide, odd, first_pairs, n)
+        for q in range(SLOTS):
+            m = SLOTS * n + q
+            keep = occupied[0, m].astype(F32)
+            first = firsts[q * 512 : (q + 1) * 512]
+            sigma = jax.nn.sigmoid(first)
+            value = (first * sigma * keep).astype(BF)
+            hidden[m] = value
+            hidden_turned[:, pl.ds(pl.multiple_of(m * 512, 512), 512)] = value.T
+            slope[m] = sigma * (1.0 + first * (1.0 - sigma)) * keep
         return carry
 
-    lax.fori_loop(0, 4, forward, 0)
+    lax.fori_loop(0, 4 // SLOTS, forward, 0)
 
     take_faces(g, links, device, got, 1, faces)
     build(wide_grad, odd_grad, g, faces)
@@ -296,11 +308,14 @@
     weight_terms(wide_grad, odd_grad, hidden_turned, put_second)
 
     def backward(n, carry):
-        grad = convolve(wide_grad, odd_grad, second_pairs, n) * slope[n]
-        grad_turned[:, pl.ds(pl.multiple_of(n * 512, 512), 512)] = grad.astype(BF).T
+        grads = convolve(wide_grad, odd_grad, second_pairs, n)
+        for q in range(SLOTS):
+            m = SLOTS * n + q
+            grad = grads[q * 512 : (q + 1) * 512] * slope[m]
+            grad_turned[:, pl.ds(pl.multiple_of(m * 512, 512), 512)] = grad.astype(BF).T
         return carry
 
-    lax.fori_loop(0, 4, backward, 0)
+    lax.fori_loop(0, 4 // SLOTS, backward, 0)
 
     def put_first(t, block):
         put(0, t, block.T)
@@ -328,33 +343,47 @@
     lay_weights(pair_weights, lambda t: second_weight[t])
 
     def forward(n, carry):
-        keep = occupied[0, n].astype(F32)
-        second = convolve(wide, odd, pair_weights, n)
-        output[0, n] = ((masked[n].astype(F32) + second) * keep).astype(BF)
+        seconds = convolve(wide, odd, pair_weights, n)
+        for q in range(SLOTS):
+            m = SLOTS * n + q
+            keep = occupied[0, m].astype(F32)
+            output[0, m] = ((masked[m] + seconds[q * 512 : (q + 1) * 512]) * keep).astype(BF)
         return carry
 
-    lax.fori_loop(0, 4, forward, 0)
-
-
-def pair_kernel(own, other, terms):
-    terms[pl.ds(0, ROWS), :] = (own[...] + other[...]).astype(BF)
-    terms[pl.ds(ROWS, 64 * CHUNK - ROWS), :] = jnp.zeros((64 * CHUNK - ROWS, 128), BF)
+    lax.fori_loop(0, 4 // SLOTS, forward, 0)
+
+
+def pair_kernel(own, other, terms, staged, sems):
+    copies = []
+    for q in range(8):
+        rows = pl.ds(q * 448, 448)
+        if q == 7:
+            staged[pl.ds(3136, 320), :] = (own[pl.ds(3136, 320), :] + other[pl.ds(3136, 320), :]).astype(BF)
+            staged[pl.ds(ROWS, 128), :] = jnp.zeros((128, 128), BF)
+        else:
+            staged[rows, :] = (own[rows, :] + other[rows, :]).astype(BF)
+        copies.append(pltpu.make_async_copy(staged.at[rows], terms.at[rows], sems.at[q]))
+        copies[-1].start()
+    for copy in copies:
+        copy.wait()
 
 
 def sum_kernel(chunks, *rest):
-    spread = rest[-1]
-    total = chunks[0].astype(F32)
-
-    def add(p, total):
-        return total + chunks[p].astype(F32)
-
-    total = lax.fori_loop(1, 64, add, total, unroll=7).astype(BF)
-
-    def put(p, carry):
-        spread[p] = total
-        return carry
-
-    lax.fori_loop(0, 64, put, 0, unroll=8)
+    spread, total, sems = rest[-3:]
+    first = chunks[0].astype(F32)
+
+    def add(p, so_far):
+        return so_far + chunks[p].astype(F32)
+
+    total[...] = lax.fori_loop(1, 64, add, first, unroll=7).astype(BF)
+
+    def send(p):
+        return pltpu.make_async_copy(total, spread.at[p], sems.at[p])
+
+    for p in range(64):
+        send(p).start()
+    for p in range(64):
+        send(p).wait()
 
 
 def finish(core_of_first, source, outs, wide, sems):
@@ -419,16 +448,16 @@
     padded = [pltpu.VMEM((3, 4, 10, 80, 128), BF), pltpu.VMEM((3, 4, 10, 64, 128), BF)]
     pairs = pltpu.VMEM((4608, 256), BF)
     turned = pltpu.VMEM((128, 2048), BF)
-    sems = pltpu.SemaphoreType.DMA((4,))
+    sems = pltpu.SemaphoreType.DMA((5,))
     blocks = jax.ShapeDtypeStruct((4, 512, 128), BF)
     terms_shape = jax.ShapeDtypeStruct((ROWS, 128), F32)
 
-    *sent, masked, grad_out = call(
+    sent = call(
         first_faces_kernel,
-        send_shapes(2) + (blocks, blocks),
-        (voxels, cotangent, neighbours, occupied),
-        [HBM] * 4,
-        [field, field, raw, raw, links, flags, sems],
+        send_shapes(2),
+        (voxels, cotangent, neighbours),
+        [HBM] * 3,
+        [field, field, raw, raw, links, sems],
         10,
         nbytes=2 << 20,
     )
@@ -436,10 +465,10 @@
     prepared = call(
         prepare_kernel,
         (in_vmem((4, 512, 128), F32),) * 2 + (in_vmem((4608, 256), BF),) * 2,
-        (masked, grad_out, first_weight, second_weight),
-        [VMEM] * 2 + [HBM] * 2,
-        [weights, weights, sems],
-        6,
+        (voxels, cotangent, occupied, first_weight, second_weight),
+        [HBM] * 5,
+        [raw, raw, weights, weights, flags, sems],
+        8,
         flops=1 << 20,
         nbytes=8 << 20,
     )
@@ -455,7 +484,16 @@
     )
     other = lax.ppermute(other, "core", PARTNER)
     chunks = jax.ShapeDtypeStruct((64 * CHUNK, 128), BF)
-    terms = call(pair_kernel, chunks, (own, other), [VMEM] * 2, [], 8, nbytes=4 << 20)
+    terms = call(
+        pair_kernel,
+        chunks,
+        (own, other),
+        [VMEM] * 2,
+        [pltpu.VMEM((64 * CHUNK, 128), BF), pltpu.SemaphoreType.DMA((8,))],
+        4,
+        nbytes=4 << 20,
+        out_specs=HBM,
+    )
     parts = lax.all_to_all(
         terms.reshape(64, CHUNK, 128), PEERS, split_axis=0, concat_axis=0, tiled=True
     )
@@ -474,15 +512,16 @@
         jax.ShapeDtypeStruct((64, CHUNK, 128), BF),
         (parts,) + tuple(sent),
         [VMEM] + [ANY] * 5,
-        [],
-        6,
+        [pltpu.VMEM((CHUNK, 128), BF), pltpu.SemaphoreType.DMA((64,))],
+        4,
         nbytes=2 << 20,
+        out_specs=HBM,
     )
     mine = lax.all_to_all(spread, PEERS, split_axis=0, concat_axis=0, tiled=True)
     output = call(
         last_kernel,
         jax.ShapeDtypeStruct((1, 4, 512, 128), BF),
-        (masked, hidden, neighbours, occupied, second_weight) + got,
+        (prepared[0], hidden, neighbours, occupied, second_weight) + got,
         [VMEM] * 2 + [HBM] * 3 + [VMEM] * 5,
         [field] + sides + padded + [pairs, weights, links, flags, sems],
         20,

time: 93.1 us -> 92.3 us (level)
  no operation moved by 1% of the time
where the time goes in v4:
time: 92.3 us; the launch traced here: 91.9 us
  starting transfers between devices  34.1 us (37%)
  Pallas kernels  31.4 us (34%)
  waiting for transfers between devices  25.5 us (28%)
    pallas_call x9, Pallas kernels, call(): pl.pallas_call(kernel, out_shape=outs, in_specs=specs, out_specs=tuple((o...  31.4 us
    ppermute x10, starting transfers between devices, exchange(): got.append(lax.ppermute(sent[way], SPACE, SWAPS[way]))  19.3 us
    all_to_all x1, waiting for transfers between devices, step(): lax.all_to_all(terms.reshape(64, CHUNK, 128), PEERS, split_axis=0, concat...  14.7 us
    all_to_all x1, starting transfers between devices, step(): lax.all_to_all(terms.reshape(64, CHUNK, 128), PEERS, split_axis=0, concat...  7.31 us
    ppermute x10, waiting for transfers between devices, exchange(): got.append(lax.ppermute(sent[way], SPACE, SWAPS[way]))  6.67 us
    all_to_all x1, starting transfers between devices, step(): lax.all_to_all(spread, PEERS, split_axis=0, concat_axis=0, tiled=True)  5.23 us
    ppermute x1, waiting for transfers between devices, step(): other = lax.ppermute(other, 'core', PARTNER)  3.32 us
  transfers between devices with their start and end apart: 14, of which 5 were waited for; matrix products, arithmetic and copies ran while one was open for 0% of the time, Pallas kernels for 11%

profile of v4, /device:TPU:1, one launch (start us, length us, event | category | flops | bytes accessed | tf_op | source)
XLA Modules:
  0.0 91.9 jit_solution(3920209161440457918)
XLA Ops:
  0.6 1.6 %shard_map.86 = (bf16[256,128]{1,0:T(8,128)(2,1)S(1)}, bf16[256,128]{1,0:T(8,128)(2,1)S(1)}, bf16[256,128]{1,0:T(8,128)(2,1)S(1)}, bf16[256,128]{1,0:T(8,128)(2,1)S(1)}, bf16[512,128]{1,0:T(8,128)(2,1)S(1)}) custom-call(bf16[1,4,512,128]{3,2,1,0:T(8,128)(2,1)} %voxels.3, bf16[1,4,512,128]{3,2,1,0:T(8,128)(2,1)} %cotangent.3, s32[1,4,6]{2,1,0:T(4,128)} %links_in.7), custom_call_target="tpu_custom_call" | custom-call | bytes 2097152 | tf_op jit(solution)/shard_map/pallas_call | solution.py:425
  2.2 4.5 %collective-permute-start.4 = (bf16[512,128]{1,0:T(8,128)(2,1)S(1)}, bf16[512,128]{1,0:T(8,128)(2,1)S(1)}, u32[]{:S(2)}, u32[]{:S(2)}) collective-permute-start(bf16[512,128]{1,0:T(8,128)(2,1)S(1)} %get-tuple-element.34), channel_id=1, source_target_pairs={{0,64},{4,68},{8,72},{12,76},{16,80},{20,84},{24,88},{28,92},{32,9... | collective-permute-start | bytes 393224 | tf_op jit(solution)/shard_map/ppermute | solution.py:56
  6.7 1.0 %collective-permute-start = (bf16[256,128]{1,0:T(8,128)(2,1)S(1)}, bf16[256,128]{1,0:T(8,128)(2,1)S(1)}, u32[]{:S(2)}, u32[]{:S(2)}) collective-permute-start(bf16[256,128]{1,0:T(8,128)(2,1)S(1)} %get-tuple-element.30), channel_id=1, source_target_pairs={{0,4},{4,0},{8,12},{12,8},{16,20},{20,16},{24,28},{28,24},{32,36},... | collective-permute-start | bytes 196616 | tf_op jit(solution)/shard_map/ppermute | solution.py:56
  7.7 2.7 %collective-permute-start.1 = (bf16[256,128]{1,0:T(8,128)(2,1)S(1)}, bf16[256,128]{1,0:T(8,128)(2,1)S(1)}, u32[]{:S(2)}, u32[]{:S(2)}) collective-permute-start(bf16[256,128]{1,0:T(8,128)(2,1)S(1)} %get-tuple-element.31), channel_id=1, source_target_pairs={{0,20},{4,16},{8,28},{12,24},{16,4},{20,0},{24,12},{28,8},{32,52},... | collective-permute-start | bytes 196616 | tf_op jit(solution)/shard_map/ppermute | solution.py:56
  10.3 0.2 collective-permute-start.2
  10.6 1.6 %collective-permute-start.3 = (bf16[256,128]{1,0:T(8,128)(2,1)S(1)}, bf16[256,128]{1,0:T(8,128)(2,1)S(1)}, u32[]{:S(2)}, u32[]{:S(2)}) collective-permute-start(bf16[256,128]{1,0:T(8,128)(2,1)S(1)} %get-tuple-element.33), channel_id=1, source_target_pairs={{0,40},{4,44},{8,32},{12,36},{16,56},{20,60},{24,48},{28,52},{32,8... | collective-permute-start | bytes 196616 | tf_op jit(solution)/shard_map/ppermute | solution.py:56
  12.2 2.2 %shard_map.85 = (f32[4,512,128]{2,1,0:T(8,128)S(1)}, f32[4,512,128]{2,1,0:T(8,128)S(1)}, bf16[4608,256]{1,0:T(8,128)(2,1)S(1)}, bf16[4608,256]{1,0:T(8,128)(2,1)S(1)}) custom-call(bf16[1,4,512,128]{3,2,1,0:T(8,128)(2,1)} %voxels.3, bf16[1,4,512,128]{3,2,1,0:T(8,128)(2,1)} %cotangent.3, s32[1,4]{1,0:T(1,128)} %occupied_in.5, bf16[27,128,128]{2,1,0:T(8,128)(2,1)} %first_in.1, ...), custom_call_target="tpu_custom_call" | custom-call | flops 1048576 | bytes 8388608 | tf_op jit(solution)/shard_map/pallas_call | solution.py:425
  14.4 0.0 collective-permute-done.g0
  14.4 0.0 collective-permute-done.1.g1
  14.4 0.0 collective-permute-done.2.g2
  14.4 1.1 %collective-permute-done.3.g3 = bf16[256,128]{1,0:T(8,128)(2,1)S(1)} collective-permute-done((bf16[256,128]{1,0:T(8,128)(2,1)S(1)}, bf16[256,128]{1,0:T(8,128)(2,1)S(1)}, u32[]{:S(2)}, u32[]{:S(2)}) %collective-permute-start.3) | collective-permute-done | bytes 65568 | tf_op jit(solution)/shard_map/ppermute | solution.py:56
  15.5 0.0 collective-permute-done.4.g4
  15.5 16.1 %shard_map.87 = (bf16[4,512,128]{2,1,0:T(8,128)(2,1)S(1)}, f32[3456,128]{1,0:T(8,128)S(1)}, f32[3456,128]{1,0:T(8,128)S(1)}) custom-call(f32[4,512,128]{2,1,0:T(8,128)S(1)} %get-tuple-element.26.x.masked, f32[4,512,128]{2,1,0:T(8,128)S(1)} %get-tuple-element.27.g, bf16[4608,256]{1,0:T(8,128)(2,1)S(1)} %get-tuple-element.28.first_pairs, ...), custom_call_target="tpu_custom_call" | custom-call | flops 8589934592 | bytes 8388608 | tf_op jit(solution)/shard_map/pallas_call | solution.py:425
  31.6 1.6 %collective-permute-start.5 = (f32[3456,128]{1,0:T(8,128)S(1)}, f32[3456,128]{1,0:T(8,128)S(1)}, u32[]{:S(2)}, u32[]{:S(2)}) collective-permute-start(f32[3456,128]{1,0:T(8,128)S(1)} %get-tuple-element.36), channel_id=1, source_target_pairs={{0,4},{4,0},{1,5},{5,1},{2,6},{6,2},{3,7},{7,3},{8,12},{12,8},{9,1... | collective-permute-start | bytes 5308424 | tf_op jit(solution)/shard_map/ppermute | solution.py:485
  33.2 3.3 %collective-permute-done.5.other = f32[3456,128]{1,0:T(8,128)S(1)} collective-permute-done((f32[3456,128]{1,0:T(8,128)S(1)}, f32[3456,128]{1,0:T(8,128)S(1)}, u32[]{:S(2)}, u32[]{:S(2)}) %collective-permute-start.5) | collective-permute-done | bytes 1769504 | tf_op jit(solution)/shard_map/ppermute | solution.py:485
  36.5 1.0 %shard_map.88 = bf16[3584,128]{1,0:T(8,128)(2,1)} custom-call(f32[3456,128]{1,0:T(8,128)S(1)} %get-tuple-element.35.own, f32[3456,128]{1,0:T(8,128)S(1)} %collective-permute-done.5.other), custom_call_target="tpu_custom_call" | custom-call | bytes 4194304 | tf_op jit(solution)/shard_map/pallas_call | solution.py:425
  37.5 7.3 %all-to-all-start = ((bf16[64,56,128]{2,1,0:T(8,128)(2,1)}), bf16[64,56,128]{2,1,0:T(8,128)(2,1)S(1)}, u32[]{:S(2)}, u32[]{:S(2)}) async-start(bf16[64,56,128]{2,1,0:T(8,128)(2,1)} %bitcast), calls=%async_computation | async-start | bytes 1835008 | tf_op jit(solution)/shard_map/all_to_all | solution.py:497
  44.8 1.0 %shard_map.89 = (bf16[128,128]{1,0:T(8,128)(2,1)S(1)}, bf16[128,128]{1,0:T(8,128)(2,1)S(1)}, bf16[128,128]{1,0:T(8,128)(2,1)S(1)}, bf16[128,128]{1,0:T(8,128)(2,1)S(1)}, bf16[256,128]{1,0:T(8,128)(2,1)S(1)}) custom-call(bf16[4,512,128]{2,1,0:T(8,128)(2,1)S(1)} %get-tuple-element.37.hidden, s32[1,4,6]{2,1,0:T(4,128)} %links_in.7), custom_call_target="tpu_custom_call" | custom-call | bytes 1048576 | tf_op jit(solution)/shard_map/pallas_call | solution.py:425
  45.8 14.7 %all-to-all-done.chunks = bf16[64,56,128]{2,1,0:T(8,128)(2,1)S(1)} async-done(((bf16[64,56,128]{2,1,0:T(8,128)(2,1)}), bf16[64,56,128]{2,1,0:T(8,128)(2,1)S(1)}, u32[]{:S(2)}, u32[]{:S(2)}) %all-to-all-start) | async-done | bytes 917536 | tf_op jit(solution)/shard_map/all_to_all | solution.py:497
  60.5 1.6 %shard_map.90 = bf16[64,56,128]{2,1,0:T(8,128)(2,1)} custom-call(bf16[64,56,128]{2,1,0:T(8,128)(2,1)S(1)} %all-to-all-done.chunks, bf16[128,128]{1,0:T(8,128)(2,1)S(1)} %get-tuple-element.38.rest_0_, bf16[128,128]{1,0:T(8,128)(2,1)S(1)} %get-tuple-element.39.rest_1_, bf16[128,128]{1,0:T(8,128)(2,1)S(1)} %get-tuple-element.40.rest_2_, ...), custom_call_target="tpu_custom_call" | custom-call | bytes 2097152 | tf_op jit(solution)/shard_map/pallas_call | solution.py:425
  62.1 5.2 %all-to-all-start.1 = ((bf16[64,56,128]{2,1,0:T(8,128)(2,1)}), bf16[64,56,128]{2,1,0:T(8,128)(2,1)S(1)}, u32[]{:S(2)}, u32[]{:S(2)}) async-start(bf16[64,56,128]{2,1,0:T(8,128)(2,1)} %shard_map.90), calls=%async_computation.1 | async-start | bytes 1835008 | tf_op jit(solution)/shard_map/all_to_all | solution.py:520
  67.4 2.6 %collective-permute-start.10 = (bf16[256,128]{1,0:T(8,128)(2,1)S(1)}, bf16[256,128]{1,0:T(8,128)(2,1)S(1)}, u32[]{:S(2)}, u32[]{:S(2)}) collective-permute-start(bf16[256,128]{1,0:T(8,128)(2,1)S(1)} %get-tuple-element.42.rest_4_), channel_id=1, source_target_pairs={{0,64},{4,68},{8,72},{12,76},{16,80},{20,84},{24,88},{28,92},{32,9... | collective-permute-start | bytes 196616 | tf_op jit(solution)/shard_map/ppermute | solution.py:56
  70.0 2.6 %collective-permute-start.6 = (bf16[128,128]{1,0:T(8,128)(2,1)S(1)}, bf16[128,128]{1,0:T(8,128)(2,1)S(1)}, u32[]{:S(2)}, u32[]{:S(2)}) collective-permute-start(bf16[128,128]{1,0:T(8,128)(2,1)S(1)} %get-tuple-element.38.rest_0_), channel_id=1, source_target_pairs={{0,4},{4,0},{8,12},{12,8},{16,20},{20,16},{24,28},{28,24},{32,36},... | collective-permute-start | bytes 98312 | tf_op jit(solution)/shard_map/ppermute | solution.py:56
  72.5 2.7 %collective-permute-start.7 = (bf16[128,128]{1,0:T(8,128)(2,1)S(1)}, bf16[128,128]{1,0:T(8,128)(2,1)S(1)}, u32[]{:S(2)}, u32[]{:S(2)}) collective-permute-start(bf16[128,128]{1,0:T(8,128)(2,1)S(1)} %get-tuple-element.39.rest_1_), channel_id=1, source_target_pairs={{0,20},{4,16},{8,28},{12,24},{16,4},{20,0},{24,12},{28,8},{32,52},... | collective-permute-start | bytes 98312 | tf_op jit(solution)/shard_map/ppermute | solution.py:56
  75.2 0.4 collective-permute-start.8
  75.6 1.1 %collective-permute-start.9 = (bf16[128,128]{1,0:T(8,128)(2,1)S(1)}, bf16[128,128]{1,0:T(8,128)(2,1)S(1)}, u32[]{:S(2)}, u32[]{:S(2)}) collective-permute-start(bf16[128,128]{1,0:T(8,128)(2,1)S(1)} %get-tuple-element.41.rest_3_), channel_id=1, source_target_pairs={{0,40},{4,44},{8,32},{12,36},{16,56},{20,60},{24,48},{28,52},{32,8... | collective-permute-start | bytes 98312 | tf_op jit(solution)/shard_map/ppermute | solution.py:56
  76.7 0.0 collective-permute-done.6.g0
  76.7 5.6 %collective-permute-done.7.g1 = bf16[128,128]{1,0:T(8,128)(2,1)S(1)} collective-permute-done((bf16[128,128]{1,0:T(8,128)(2,1)S(1)}, bf16[128,128]{1,0:T(8,128)(2,1)S(1)}, u32[]{:S(2)}, u32[]{:S(2)}) %collective-permute-start.7) | collective-permute-done | bytes 32800 | tf_op jit(solution)/shard_map/ppermute | solution.py:56
  82.3 0.0 collective-permute-done.8.g2
  82.3 0.0 collective-permute-done.9.g3
  82.3 0.0 collective-permute-done.10.g4
  82.3 5.4 %shard_map.91 = bf16[1,4,512,128]{3,2,1,0:T(8,128)(2,1)} custom-call(f32[4,512,128]{2,1,0:T(8,128)S(1)} %get-tuple-element.26.x.masked, bf16[4,512,128]{2,1,0:T(8,128)(2,1)S(1)} %get-tuple-element.37.hidden, s32[1,4,6]{2,1,0:T(4,128)} %links_in.7, s32[1,4]{1,0:T(1,128)} %occupied_in.5, bf16[27,128,128]{2,1,0:T(8,128)(2,1)} %second_in.3, ...), custom_call_target="tpu_custom_call" | custom-call | flops 3221225472 | bytes 4194304 | tf_op jit(solution)/shard_map/pallas_call | solution.py:425
  87.7 0.0 all-to-all-done.1
  87.8 0.6 collective-permute-start.11
  88.4 1.3 %shard_map.92 = (f32[3456,128]{1,0:T(8,128)}, f32[3456,128]{1,0:T(8,128)}) custom-call(bf16[3584,128]{1,0:T(8,128)(2,1)S(1)} %bitcast.5), custom_call_target="tpu_custom_call" | custom-call | bytes 3145728 | tf_op jit(solution)/shard_map/pallas_call | solution.py:425
  89.7 0.8 collective-permute-done.11.other
  90.5 1.3 %shard_map.93 = (f32[3456,128]{1,0:T(8,128)}, f32[3456,128]{1,0:T(8,128)}) custom-call(bf16[3584,128]{1,0:T(8,128)(2,1)S(1)} %collective-permute-done.11.other, f32[3456,128]{1,0:T(8,128)} %get-tuple-element.45.first_in, f32[3456,128]{1,0:T(8,128)} %get-tuple-element.46.second_in), custom_call_target="tpu_custom_call", output_to_operand_aliasing={{0}: (1, {}), {1}: (2, {})} | custom-call | bytes 3145728 | tf_op jit(solution)/shard_map/pallas_call | solution.py:425
Async XLA Ops:
  2.2 13.3 %collective-permute-start.4 = (bf16[512,128]{1,0:T(8,128)(2,1)S(1)}, bf16[512,128]{1,0:T(8,128)(2,1)S(1)}, u32[]{:S(2)}, u32[]{:S(2)}) collective-permute-start(bf16[512,128]{1,0:T(8,128)(2,1)S(1)} %get-tuple-element.34), channel_id=1, source_target_pairs={{0,64},{4,68},{8,72},{12,76},{16,80},{20,84},{24,88},{28,92},{32,9... | collective-permute-start | bytes 393224 | tf_op jit(solution)/shard_map/ppermute | solution.py:56
  6.7 7.7 %collective-permute-start = (bf16[256,128]{1,0:T(8,128)(2,1)S(1)}, bf16[256,128]{1,0:T(8,128)(2,1)S(1)}, u32[]{:S(2)}, u32[]{:S(2)}) collective-permute-start(bf16[256,128]{1,0:T(8,128)(2,1)S(1)} %get-tuple-element.30), channel_id=1, source_target_pairs={{0,4},{4,0},{8,12},{12,8},{16,20},{20,16},{24,28},{28,24},{32,36},... | collective-permute-start | bytes 196616 | tf_op jit(solution)/shard_map/ppermute | solution.py:56
  7.7 6.8 %collective-permute-start.1 = (bf16[256,128]{1,0:T(8,128)(2,1)S(1)}, bf16[256,128]{1,0:T(8,128)(2,1)S(1)}, u32[]{:S(2)}, u32[]{:S(2)}) collective-permute-start(bf16[256,128]{1,0:T(8,128)(2,1)S(1)} %get-tuple-element.31), channel_id=1, source_target_pairs={{0,20},{4,16},{8,28},{12,24},{16,4},{20,0},{24,12},{28,8},{32,52},... | collective-permute-start | bytes 196616 | tf_op jit(solution)/shard_map/ppermute | solution.py:56
  10.3 4.1 %collective-permute-start.2 = (bf16[256,128]{1,0:T(8,128)(2,1)S(1)}, bf16[256,128]{1,0:T(8,128)(2,1)S(1)}, u32[]{:S(2)}, u32[]{:S(2)}) collective-permute-start(bf16[256,128]{1,0:T(8,128)(2,1)S(1)} %get-tuple-element.32), channel_id=1, source_target_pairs={{0,8},{4,12},{8,0},{12,4},{16,24},{20,28},{24,16},{28,20},{32,40},... | collective-permute-start | bytes 196616 | tf_op jit(solution)/shard_map/ppermute | solution.py:56
  10.6 4.9 %collective-permute-start.3 = (bf16[256,128]{1,0:T(8,128)(2,1)S(1)}, bf16[256,128]{1,0:T(8,128)(2,1)S(1)}, u32[]{:S(2)}, u32[]{:S(2)}) collective-permute-start(bf16[256,128]{1,0:T(8,128)(2,1)S(1)} %get-tuple-element.33), channel_id=1, source_target_pairs={{0,40},{4,44},{8,32},{12,36},{16,56},{20,60},{24,48},{28,52},{32,8... | collective-permute-start | bytes 196616 | tf_op jit(solution)/shard_map/ppermute | solution.py:56
  31.6 4.9 %collective-permute-start.5 = (f32[3456,128]{1,0:T(8,128)S(1)}, f32[3456,128]{1,0:T(8,128)S(1)}, u32[]{:S(2)}, u32[]{:S(2)}) collective-permute-start(f32[3456,128]{1,0:T(8,128)S(1)} %get-tuple-element.36), channel_id=1, source_target_pairs={{0,4},{4,0},{1,5},{5,1},{2,6},{6,2},{3,7},{7,3},{8,12},{12,8},{9,1... | collective-permute-start | bytes 5308424 | tf_op jit(solution)/shard_map/ppermute | solution.py:485
  37.5 23.0 %all-to-all-start = ((bf16[64,56,128]{2,1,0:T(8,128)(2,1)}), bf16[64,56,128]{2,1,0:T(8,128)(2,1)S(1)}, u32[]{:S(2)}, u32[]{:S(2)}) async-start(bf16[64,56,128]{2,1,0:T(8,128)(2,1)} %bitcast), calls=%async_computation | async-start | bytes 1835008 | tf_op jit(solution)/shard_map/all_to_all | solution.py:497
  62.1 25.6 %all-to-all-start.1 = ((bf16[64,56,128]{2,1,0:T(8,128)(2,1)}), bf16[64,56,128]{2,1,0:T(8,128)(2,1)S(1)}, u32[]{:S(2)}, u32[]{:S(2)}) async-start(bf16[64,56,128]{2,1,0:T(8,128)(2,1)} %shard_map.90), calls=%async_computation.1 | async-start | bytes 1835008 | tf_op jit(solution)/shard_map/all_to_all | solution.py:520
  67.4 14.9 %collective-permute-start.10 = (bf16[256,128]{1,0:T(8,128)(2,1)S(1)}, bf16[256,128]{1,0:T(8,128)(2,1)S(1)}, u32[]{:S(2)}, u32[]{:S(2)}) collective-permute-start(bf16[256,128]{1,0:T(8,128)(2,1)S(1)} %get-tuple-element.42.rest_4_), channel_id=1, source_target_pairs={{0,64},{4,68},{8,72},{12,76},{16,80},{20,84},{24,88},{28,92},{32,9... | collective-permute-start | bytes 196616 | tf_op jit(solution)/shard_map/ppermute | solution.py:56
  70.0 6.7 %collective-permute-start.6 = (bf16[128,128]{1,0:T(8,128)(2,1)S(1)}, bf16[128,128]{1,0:T(8,128)(2,1)S(1)}, u32[]{:S(2)}, u32[]{:S(2)}) collective-permute-start(bf16[128,128]{1,0:T(8,128)(2,1)S(1)} %get-tuple-element.38.rest_0_), channel_id=1, source_target_pairs={{0,4},{4,0},{8,12},{12,8},{16,20},{20,16},{24,28},{28,24},{32,36},... | collective-permute-start | bytes 98312 | tf_op jit(solution)/shard_map/ppermute | solution.py:56
  72.5 9.8 %collective-permute-start.7 = (bf16[128,128]{1,0:T(8,128)(2,1)S(1)}, bf16[128,128]{1,0:T(8,128)(2,1)S(1)}, u32[]{:S(2)}, u32[]{:S(2)}) collective-permute-start(bf16[128,128]{1,0:T(8,128)(2,1)S(1)} %get-tuple-element.39.rest_1_), channel_id=1, source_target_pairs={{0,20},{4,16},{8,28},{12,24},{16,4},{20,0},{24,12},{28,8},{32,52},... | collective-permute-start | bytes 98312 | tf_op jit(solution)/shard_map/ppermute | solution.py:56
  75.2 7.1 %collective-permute-start.8 = (bf16[128,128]{1,0:T(8,128)(2,1)S(1)}, bf16[128,128]{1,0:T(8,128)(2,1)S(1)}, u32[]{:S(2)}, u32[]{:S(2)}) collective-permute-start(bf16[128,128]{1,0:T(8,128)(2,1)S(1)} %get-tuple-element.40.rest_2_), channel_id=1, source_target_pairs={{0,8},{4,12},{8,0},{12,4},{16,24},{20,28},{24,16},{28,20},{32,40},... | collective-permute-start | bytes 98312 | tf_op jit(solution)/shard_map/ppermute | solution.py:56
  75.6 6.7 %collective-permute-start.9 = (bf16[128,128]{1,0:T(8,128)(2,1)S(1)}, bf16[128,128]{1,0:T(8,128)(2,1)S(1)}, u32[]{:S(2)}, u32[]{:S(2)}) collective-permute-start(bf16[128,128]{1,0:T(8,128)(2,1)S(1)} %get-tuple-element.41.rest_3_), channel_id=1, source_target_pairs={{0,40},{4,44},{8,32},{12,36},{16,56},{20,60},{24,48},{28,52},{32,8... | collective-permute-start | bytes 98312 | tf_op jit(solution)/shard_map/ppermute | solution.py:56
  87.8 2.7 %collective-permute-start.11 = (bf16[3584,128]{1,0:T(8,128)(2,1)S(1)}, bf16[3584,128]{1,0:T(8,128)(2,1)S(1)}, u32[]{:S(2)}, u32[]{:S(2)}) collective-permute-start(bf16[3584,128]{1,0:T(8,128)(2,1)S(1)} %bitcast.4), channel_id=1, source_target_pairs={{0,4},{4,0},{1,5},{5,1},{2,6},{6,2},{3,7},{7,3},{8,12},{12,8},{9,1... | collective-permute-start | bytes 2752520 | tf_op jit(solution)/shard_map/ppermute | solution.py:533

commit v5 on v4

--- a/solution.py
+++ b/solution.py
@@ -123,12 +123,12 @@
                 faces[axis][n, side] = value
 
 
-def build(wide, odd, x, faces):
+def build(wide, odd, x, faces, slots):
     k_of = lax.broadcasted_iota(jnp.int32, (10, 8, 128), 1)
     at_low, at_high = k_of == 0, k_of == 7
     none = jnp.zeros((1, 8, 128), F32)
 
-    def block(n, carry):
+    def block(n):
         for i in range(10):
             if i in (0, 9):
                 core = faces[0][n, 0 if i == 0 else 1].reshape(8, 8, 128)
@@ -152,9 +152,9 @@
             for tk, shifted in enumerate((before, layers, after)):
                 wide[tk, n, i] = shifted.reshape(80, 128).astype(BF)
                 odd[tk, n, i] = shifted[1:9].reshape(64, 128).astype(BF)
-        return carry
-
-    lax.fori_loop(0, 4, block, 0)
+
+    for n in slots:
+        block(n)
 
 
 def tap(wide, odd, n, i, tj, tk):
@@ -200,8 +200,7 @@
                     )
                 )
         total = jnp.dot(turned[...], jnp.concatenate(columns, axis=1), preferred_element_type=F32)
-        for q in range(9):
-            put(9 * ti + q, total[:, q * 128 : (q + 1) * 128])
+        put(ti, [total[:, q * 128 : (q + 1) * 128] for q in range(9)])
 
 
 def fetch(sems, *pairs):
@@ -260,7 +259,7 @@
 def main_kernel(
     x, g, first_pairs, second_pairs, links_in, occupied_in, g0, g1, g2, g3, g4,
     hidden, own_terms, other_terms,
-    fx, fy, fz, wide, odd, wide_grad, odd_grad, slope, hidden_turned, grad_turned, links, occupied, sems,
+    fx, fy, fz, gx, gy, gz, wide, odd, wide_grad, odd_grad, slope, hidden_turned, grad_turned, links, occupied, sems,
 ):
     copies = fetch(sems, (links_in, links), (occupied_in, occupied))
     device = lax.axis_index(SPACE)
@@ -269,9 +268,12 @@
     copies[0].wait()
     copies[1].wait()
     take_faces(x, links, device, got, 0, faces)
-    build(wide, odd, x, faces)
+    take_faces(g, links, device, got, 1, (gx, gy, gz))
 
     def forward(n, carry):
+        slots = [SLOTS * n + q for q in range(SLOTS)]
+        build(wide, odd, x, faces, slots)
+        build(wide_grad, odd_grad, g, (gx, gy, gz), slots)
         firsts = convolve(wide, odd, first_pairs, n)
         for q in range(SLOTS):
             m = SLOTS * n + q
@@ -284,26 +286,25 @@
             slope[m] = sigma * (1.0 + first * (1.0 - sigma)) * keep
         return carry
 
-    lax.fori_loop(0, 4 // SLOTS, forward, 0)
-
-    take_faces(g, links, device, got, 1, faces)
-    build(wide_grad, odd_grad, g, faces)
+    lax.fori_loop(0, 4 // SLOTS, forward, 0, unroll=True)
+
 
     core = device & 1
 
-    def put(of_core, t, block):
-        rows = pl.ds(t * 128, 128)
+    def put(of_core, start, blocks):
+        rows = pl.ds(start * 128, 1152)
+        stacked = jnp.concatenate(blocks, axis=0)
 
         @pl.when(core == of_core)
         def _():
-            own_terms[rows, :] = block
+            own_terms[rows, :] = stacked
 
         @pl.when(core != of_core)
         def _():
-            other_terms[rows, :] = block
-
-    def put_second(t, block):
-        put(1, 26 - t, block)
+            other_terms[rows, :] = stacked
+
+    def put_second(ti, blocks):
+        put(1, 18 - 9 * ti, blocks[::-1])
 
     weight_terms(wide_grad, odd_grad, hidden_turned, put_second)
 
@@ -315,10 +316,10 @@
             grad_turned[:, pl.ds(pl.multiple_of(m * 512, 512), 512)] = grad.astype(BF).T
         return carry
 
-    lax.fori_loop(0, 4 // SLOTS, backward, 0)
-
-    def put_first(t, block):
-        put(0, t, block.T)
+    lax.fori_loop(0, 4 // SLOTS, backward, 0, unroll=True)
+
+    def put_first(ti, blocks):
+        put(0, 9 * ti, [block.T for block in blocks])
 
     weight_terms(wide, odd, grad_turned, put_first)
 
@@ -338,11 +339,11 @@
     copies[0].wait()
     copies[1].wait()
     take_faces(x, links, device, (g0, g1, g2, g3, g4), 0, faces)
-    build(wide, odd, x, faces)
     copies[2].wait()
     lay_weights(pair_weights, lambda t: second_weight[t])
 
     def forward(n, carry):
+        build(wide, odd, x, faces, [SLOTS * n + q for q in range(SLOTS)])
         seconds = convolve(wide, odd, pair_weights, n)
         for q in range(SLOTS):
             m = SLOTS * n + q
@@ -350,7 +351,7 @@
             output[0, m] = ((masked[m] + seconds[q * 512 : (q + 1) * 512]) * keep).astype(BF)
         return carry
 
-    lax.fori_loop(0, 4 // SLOTS, forward, 0)
+    lax.fori_loop(0, 4 // SLOTS, forward, 0, unroll=True)
 
 
 def pair_kernel(own, other, terms, staged, sems):
@@ -369,21 +370,19 @@
 
 
 def sum_kernel(chunks, *rest):
-    spread, total, sems = rest[-3:]
-    first = chunks[0].astype(F32)
-
-    def add(p, so_far):
-        return so_far + chunks[p].astype(F32)
-
-    total[...] = lax.fori_loop(1, 64, add, first, unroll=7).astype(BF)
-
-    def send(p):
-        return pltpu.make_async_copy(total, spread.at[p], sems.at[p])
-
-    for p in range(64):
-        send(p).start()
-    for p in range(64):
-        send(p).wait()
+    spread = rest[-1]
+    total = chunks[0].astype(F32)
+
+    def add(p, total):
+        return total + chunks[p].astype(F32)
+
+    total = lax.fori_loop(1, 64, add, total, unroll=7).astype(BF)
+
+    def put(p, carry):
+        spread[p] = total
+        return carry
+
+    lax.fori_loop(0, 64, put, 0, unroll=8)
 
 
 def finish(core_of_first, source, outs, wide, sems):
@@ -477,7 +476,7 @@
         (blocks, terms_shape, terms_shape),
         tuple(prepared) + (neighbours, occupied) + got,
         [VMEM] * 4 + [HBM] * 2 + [VMEM] * 5,
-        sides + padded + padded + [field, turned, turned, links, flags, sems],
+        sides + sides + padded + padded + [field, turned, turned, links, flags, sems],
         26,
         flops=8 << 30,
         nbytes=8 << 20,
@@ -512,10 +511,9 @@
         jax.ShapeDtypeStruct((64, CHUNK, 128), BF),
         (parts,) + tuple(sent),
         [VMEM] + [ANY] * 5,
-        [pltpu.VMEM((CHUNK, 128), BF), pltpu.SemaphoreType.DMA((64,))],
-        4,
+        [],
+        6,
         nbytes=2 << 20,
-        out_specs=HBM,
     )
     mine = lax.all_to_all(spread, PEERS, split_axis=0, concat_axis=0, tiled=True)
     output = call(

time: 92.3 us -> 87.6 us (0.949)
  Pallas kernels: 31.4 us -> 26.7 us
    pallas_call x9, Pallas kernels: 31.4 us -> 26.7 us  [call(): pl.pallas_call(kernel, out_shape=outs, in_specs=specs, out_specs=tuple((o...]
where the time goes in v5:
time: 87.6 us; the launch traced here: 87.2 us
  starting transfers between devices  34 us (39%)
  Pallas kernels  26.7 us (30%)
  waiting for transfers between devices  25.5 us (29%)
  between operations  0.91 us (1%)
    pallas_call x9, Pallas kernels, call(): pl.pallas_call(kernel, out_shape=outs, in_specs=specs, out_specs=tuple((o...  26.7 us
    ppermute x10, starting transfers between devices, exchange(): got.append(lax.ppermute(sent[way], SPACE, SWAPS[way]))  19.3 us
    all_to_all x1, waiting for transfers between devices, step(): lax.all_to_all(terms.reshape(64, CHUNK, 128), PEERS, split_axis=0, concat...  14.7 us
    all_to_all x1, starting transfers between devices, step(): lax.all_to_all(terms.reshape(64, CHUNK, 128), PEERS, split_axis=0, concat...  7.31 us
    ppermute x10, waiting for transfers between devices, exchange(): got.append(lax.ppermute(sent[way], SPACE, SWAPS[way]))  6.67 us
    all_to_all x1, starting transfers between devices, step(): lax.all_to_all(spread, PEERS, split_axis=0, concat_axis=0, tiled=True)  5.22 us
    ppermute x1, waiting for transfers between devices, step(): other = lax.ppermute(other, 'core', PARTNER)  3.32 us
  transfers between devices with their start and end apart: 14, of which 5 were waited for; matrix products, arithmetic and copies ran while one was open for 0% of the time, Pallas kernels for 11%

profile of v5, /device:TPU:1, one launch (start us, length us, event | category | flops | bytes accessed | tf_op | source)
XLA Modules:
  0.0 87.2 jit_solution(12654634344772788586)
XLA Ops:
  0.6 1.6 %shard_map.86 = (bf16[256,128]{1,0:T(8,128)(2,1)S(1)}, bf16[256,128]{1,0:T(8,128)(2,1)S(1)}, bf16[256,128]{1,0:T(8,128)(2,1)S(1)}, bf16[256,128]{1,0:T(8,128)(2,1)S(1)}, bf16[512,128]{1,0:T(8,128)(2,1)S(1)}) custom-call(bf16[1,4,512,128]{3,2,1,0:T(8,128)(2,1)} %voxels.3, bf16[1,4,512,128]{3,2,1,0:T(8,128)(2,1)} %cotangent.3, s32[1,4,6]{2,1,0:T(4,128)} %links_in.7), custom_call_target="tpu_custom_call" | custom-call | bytes 2097152 | tf_op jit(solution)/shard_map/pallas_call | solution.py:424
  2.2 4.5 %collective-permute-start.4 = (bf16[512,128]{1,0:T(8,128)(2,1)S(1)}, bf16[512,128]{1,0:T(8,128)(2,1)S(1)}, u32[]{:S(2)}, u32[]{:S(2)}) collective-permute-start(bf16[512,128]{1,0:T(8,128)(2,1)S(1)} %get-tuple-element.34), channel_id=1, source_target_pairs={{0,64},{4,68},{8,72},{12,76},{16,80},{20,84},{24,88},{28,92},{32,9... | collective-permute-start | bytes 393224 | tf_op jit(solution)/shard_map/ppermute | solution.py:56
  6.7 1.0 %collective-permute-start = (bf16[256,128]{1,0:T(8,128)(2,1)S(1)}, bf16[256,128]{1,0:T(8,128)(2,1)S(1)}, u32[]{:S(2)}, u32[]{:S(2)}) collective-permute-start(bf16[256,128]{1,0:T(8,128)(2,1)S(1)} %get-tuple-element.30), channel_id=1, source_target_pairs={{0,4},{4,0},{8,12},{12,8},{16,20},{20,16},{24,28},{28,24},{32,36},... | collective-permute-start | bytes 196616 | tf_op jit(solution)/shard_map/ppermute | solution.py:56
  7.7 2.7 %collective-permute-start.1 = (bf16[256,128]{1,0:T(8,128)(2,1)S(1)}, bf16[256,128]{1,0:T(8,128)(2,1)S(1)}, u32[]{:S(2)}, u32[]{:S(2)}) collective-permute-start(bf16[256,128]{1,0:T(8,128)(2,1)S(1)} %get-tuple-element.31), channel_id=1, source_target_pairs={{0,20},{4,16},{8,28},{12,24},{16,4},{20,0},{24,12},{28,8},{32,52},... | collective-permute-start | bytes 196616 | tf_op jit(solution)/shard_map/ppermute | solution.py:56
  10.3 0.2 collective-permute-start.2
  10.6 1.6 %collective-permute-start.3 = (bf16[256,128]{1,0:T(8,128)(2,1)S(1)}, bf16[256,128]{1,0:T(8,128)(2,1)S(1)}, u32[]{:S(2)}, u32[]{:S(2)}) collective-permute-start(bf16[256,128]{1,0:T(8,128)(2,1)S(1)} %get-tuple-element.33), channel_id=1, source_target_pairs={{0,40},{4,44},{8,32},{12,36},{16,56},{20,60},{24,48},{28,52},{32,8... | collective-permute-start | bytes 196616 | tf_op jit(solution)/shard_map/ppermute | solution.py:56
  12.2 2.2 %shard_map.85 = (f32[4,512,128]{2,1,0:T(8,128)S(1)}, f32[4,512,128]{2,1,0:T(8,128)S(1)}, bf16[4608,256]{1,0:T(8,128)(2,1)S(1)}, bf16[4608,256]{1,0:T(8,128)(2,1)S(1)}) custom-call(bf16[1,4,512,128]{3,2,1,0:T(8,128)(2,1)} %voxels.3, bf16[1,4,512,128]{3,2,1,0:T(8,128)(2,1)} %cotangent.3, s32[1,4]{1,0:T(1,128)} %occupied_in.5, bf16[27,128,128]{2,1,0:T(8,128)(2,1)} %first_in.1, ...), custom_call_target="tpu_custom_call" | custom-call | flops 1048576 | bytes 8388608 | tf_op jit(solution)/shard_map/pallas_call | solution.py:424
  14.4 0.0 collective-permute-done.g0
  14.4 0.0 collective-permute-done.1.g1
  14.4 0.0 collective-permute-done.2.g2
  14.4 1.1 %collective-permute-done.3.g3 = bf16[256,128]{1,0:T(8,128)(2,1)S(1)} collective-permute-done((bf16[256,128]{1,0:T(8,128)(2,1)S(1)}, bf16[256,128]{1,0:T(8,128)(2,1)S(1)}, u32[]{:S(2)}, u32[]{:S(2)}) %collective-permute-start.3) | collective-permute-done | bytes 65568 | tf_op jit(solution)/shard_map/ppermute | solution.py:56
  15.5 0.0 collective-permute-done.4.g4
  15.5 12.5 %shard_map.87 = (bf16[4,512,128]{2,1,0:T(8,128)(2,1)S(1)}, f32[3456,128]{1,0:T(8,128)S(1)}, f32[3456,128]{1,0:T(8,128)S(1)}) custom-call(f32[4,512,128]{2,1,0:T(8,128)S(1)} %get-tuple-element.26.x.masked, f32[4,512,128]{2,1,0:T(8,128)S(1)} %get-tuple-element.27.g, bf16[4608,256]{1,0:T(8,128)(2,1)S(1)} %get-tuple-element.28.first_pairs, ...), custom_call_target="tpu_custom_call" | custom-call | flops 8589934592 | bytes 8388608 | tf_op jit(solution)/shard_map/pallas_call | solution.py:424
  28.0 1.5 %collective-permute-start.5 = (f32[3456,128]{1,0:T(8,128)S(1)}, f32[3456,128]{1,0:T(8,128)S(1)}, u32[]{:S(2)}, u32[]{:S(2)}) collective-permute-start(f32[3456,128]{1,0:T(8,128)S(1)} %get-tuple-element.36), channel_id=1, source_target_pairs={{0,4},{4,0},{1,5},{5,1},{2,6},{6,2},{3,7},{7,3},{8,12},{12,8},{9,1... | collective-permute-start | bytes 5308424 | tf_op jit(solution)/shard_map/ppermute | solution.py:484
  29.5 3.3 %collective-permute-done.5.other = f32[3456,128]{1,0:T(8,128)S(1)} collective-permute-done((f32[3456,128]{1,0:T(8,128)S(1)}, f32[3456,128]{1,0:T(8,128)S(1)}, u32[]{:S(2)}, u32[]{:S(2)}) %collective-permute-start.5) | collective-permute-done | bytes 1769504 | tf_op jit(solution)/shard_map/ppermute | solution.py:484
  32.8 1.0 %shard_map.88 = bf16[3584,128]{1,0:T(8,128)(2,1)} custom-call(f32[3456,128]{1,0:T(8,128)S(1)} %get-tuple-element.35.own, f32[3456,128]{1,0:T(8,128)S(1)} %collective-permute-done.5.other), custom_call_target="tpu_custom_call" | custom-call | bytes 4194304 | tf_op jit(solution)/shard_map/pallas_call | solution.py:424
  33.9 7.3 %all-to-all-start = ((bf16[64,56,128]{2,1,0:T(8,128)(2,1)}), bf16[64,56,128]{2,1,0:T(8,128)(2,1)S(1)}, u32[]{:S(2)}, u32[]{:S(2)}) async-start(bf16[64,56,128]{2,1,0:T(8,128)(2,1)} %bitcast), calls=%async_computation | async-start | bytes 1835008 | tf_op jit(solution)/shard_map/all_to_all | solution.py:496
  41.2 1.0 %shard_map.89 = (bf16[128,128]{1,0:T(8,128)(2,1)S(1)}, bf16[128,128]{1,0:T(8,128)(2,1)S(1)}, bf16[128,128]{1,0:T(8,128)(2,1)S(1)}, bf16[128,128]{1,0:T(8,128)(2,1)S(1)}, bf16[256,128]{1,0:T(8,128)(2,1)S(1)}) custom-call(bf16[4,512,128]{2,1,0:T(8,128)(2,1)S(1)} %get-tuple-element.37.hidden, s32[1,4,6]{2,1,0:T(4,128)} %links_in.7), custom_call_target="tpu_custom_call" | custom-call | bytes 1048576 | tf_op jit(solution)/shard_map/pallas_call | solution.py:424
  42.2 14.7 %all-to-all-done.chunks = bf16[64,56,128]{2,1,0:T(8,128)(2,1)S(1)} async-done(((bf16[64,56,128]{2,1,0:T(8,128)(2,1)}), bf16[64,56,128]{2,1,0:T(8,128)(2,1)S(1)}, u32[]{:S(2)}, u32[]{:S(2)}) %all-to-all-start) | async-done | bytes 917536 | tf_op jit(solution)/shard_map/all_to_all | solution.py:496
  56.9 1.2 %shard_map.90 = bf16[64,56,128]{2,1,0:T(8,128)(2,1)} custom-call(bf16[64,56,128]{2,1,0:T(8,128)(2,1)S(1)} %all-to-all-done.chunks, bf16[128,128]{1,0:T(8,128)(2,1)S(1)} %get-tuple-element.38.rest_0_, bf16[128,128]{1,0:T(8,128)(2,1)S(1)} %get-tuple-element.39.rest_1_, bf16[128,128]{1,0:T(8,128)(2,1)S(1)} %get-tuple-element.40.rest_2_, ...), custom_call_target="tpu_custom_call" | custom-call | bytes 2097152 | tf_op jit(solution)/shard_map/pallas_call | solution.py:424
  58.0 5.2 %all-to-all-start.1 = ((bf16[64,56,128]{2,1,0:T(8,128)(2,1)}), bf16[64,56,128]{2,1,0:T(8,128)(2,1)S(1)}, u32[]{:S(2)}, u32[]{:S(2)}) async-start(bf16[64,56,128]{2,1,0:T(8,128)(2,1)} %shard_map.90), calls=%async_computation.1 | async-start | bytes 1835008 | tf_op jit(solution)/shard_map/all_to_all | solution.py:518
  63.2 2.6 %collective-permute-start.10 = (bf16[256,128]{1,0:T(8,128)(2,1)S(1)}, bf16[256,128]{1,0:T(8,128)(2,1)S(1)}, u32[]{:S(2)}, u32[]{:S(2)}) collective-permute-start(bf16[256,128]{1,0:T(8,128)(2,1)S(1)} %get-tuple-element.42.rest_4_), channel_id=1, source_target_pairs={{0,64},{4,68},{8,72},{12,76},{16,80},{20,84},{24,88},{28,92},{32,9... | collective-permute-start | bytes 196616 | tf_op jit(solution)/shard_map/ppermute | solution.py:56
  65.8 2.6 %collective-permute-start.6 = (bf16[128,128]{1,0:T(8,128)(2,1)S(1)}, bf16[128,128]{1,0:T(8,128)(2,1)S(1)}, u32[]{:S(2)}, u32[]{:S(2)}) collective-permute-start(bf16[128,128]{1,0:T(8,128)(2,1)S(1)} %get-tuple-element.38.rest_0_), channel_id=1, source_target_pairs={{0,4},{4,0},{8,12},{12,8},{16,20},{20,16},{24,28},{28,24},{32,36},... | collective-permute-start | bytes 98312 | tf_op jit(solution)/shard_map/ppermute | solution.py:56
  68.4 2.7 %collective-permute-start.7 = (bf16[128,128]{1,0:T(8,128)(2,1)S(1)}, bf16[128,128]{1,0:T(8,128)(2,1)S(1)}, u32[]{:S(2)}, u32[]{:S(2)}) collective-permute-start(bf16[128,128]{1,0:T(8,128)(2,1)S(1)} %get-tuple-element.39.rest_1_), channel_id=1, source_target_pairs={{0,20},{4,16},{8,28},{12,24},{16,4},{20,0},{24,12},{28,8},{32,52},... | collective-permute-start | bytes 98312 | tf_op jit(solution)/shard_map/ppermute | solution.py:56
  71.1 0.4 collective-permute-start.8
  71.5 1.1 %collective-permute-start.9 = (bf16[128,128]{1,0:T(8,128)(2,1)S(1)}, bf16[128,128]{1,0:T(8,128)(2,1)S(1)}, u32[]{:S(2)}, u32[]{:S(2)}) collective-permute-start(bf16[128,128]{1,0:T(8,128)(2,1)S(1)} %get-tuple-element.41.rest_3_), channel_id=1, source_target_pairs={{0,40},{4,44},{8,32},{12,36},{16,56},{20,60},{24,48},{28,52},{32,8... | collective-permute-start | bytes 98312 | tf_op jit(solution)/shard_map/ppermute | solution.py:56
  72.6 0.0 collective-permute-done.6.g0
  72.6 5.6 %collective-permute-done.7.g1 = bf16[128,128]{1,0:T(8,128)(2,1)S(1)} collective-permute-done((bf16[128,128]{1,0:T(8,128)(2,1)S(1)}, bf16[128,128]{1,0:T(8,128)(2,1)S(1)}, u32[]{:S(2)}, u32[]{:S(2)}) %collective-permute-start.7) | collective-permute-done | bytes 32800 | tf_op jit(solution)/shard_map/ppermute | solution.py:56
  78.2 0.0 collective-permute-done.8.g2
  78.2 0.0 collective-permute-done.9.g3
  78.2 0.0 collective-permute-done.10.g4
  78.2 4.8 %shard_map.91 = bf16[1,4,512,128]{3,2,1,0:T(8,128)(2,1)} custom-call(f32[4,512,128]{2,1,0:T(8,128)S(1)} %get-tuple-element.26.x.masked, bf16[4,512,128]{2,1,0:T(8,128)(2,1)S(1)} %get-tuple-element.37.hidden, s32[1,4,6]{2,1,0:T(4,128)} %links_in.7, s32[1,4]{1,0:T(1,128)} %occupied_in.5, bf16[27,128,128]{2,1,0:T(8,128)(2,1)} %second_in.3, ...), custom_call_target="tpu_custom_call" | custom-call | flops 3221225472 | bytes 4194304 | tf_op jit(solution)/shard_map/pallas_call | solution.py:424
  83.0 0.0 all-to-all-done.1
  83.0 0.6 collective-permute-start.11
  83.6 1.3 %shard_map.92 = (f32[3456,128]{1,0:T(8,128)}, f32[3456,128]{1,0:T(8,128)}) custom-call(bf16[3584,128]{1,0:T(8,128)(2,1)S(1)} %bitcast.5), custom_call_target="tpu_custom_call" | custom-call | bytes 3145728 | tf_op jit(solution)/shard_map/pallas_call | solution.py:424
  84.9 0.8 collective-permute-done.11.other
  85.7 1.3 %shard_map.93 = (f32[3456,128]{1,0:T(8,128)}, f32[3456,128]{1,0:T(8,128)}) custom-call(bf16[3584,128]{1,0:T(8,128)(2,1)S(1)} %collective-permute-done.11.other, f32[3456,128]{1,0:T(8,128)} %get-tuple-element.45.first_in, f32[3456,128]{1,0:T(8,128)} %get-tuple-element.46.second_in), custom_call_target="tpu_custom_call", output_to_operand_aliasing={{0}: (1, {}), {1}: (2, {})} | custom-call | bytes 3145728 | tf_op jit(solution)/shard_map/pallas_call | solution.py:424
Async XLA Ops:
  2.2 13.3 %collective-permute-start.4 = (bf16[512,128]{1,0:T(8,128)(2,1)S(1)}, bf16[512,128]{1,0:T(8,128)(2,1)S(1)}, u32[]{:S(2)}, u32[]{:S(2)}) collective-permute-start(bf16[512,128]{1,0:T(8,128)(2,1)S(1)} %get-tuple-element.34), channel_id=1, source_target_pairs={{0,64},{4,68},{8,72},{12,76},{16,80},{20,84},{24,88},{28,92},{32,9... | collective-permute-start | bytes 393224 | tf_op jit(solution)/shard_map/ppermute | solution.py:56
  6.7 7.7 %collective-permute-start = (bf16[256,128]{1,0:T(8,128)(2,1)S(1)}, bf16[256,128]{1,0:T(8,128)(2,1)S(1)}, u32[]{:S(2)}, u32[]{:S(2)}) collective-permute-start(bf16[256,128]{1,0:T(8,128)(2,1)S(1)} %get-tuple-element.30), channel_id=1, source_target_pairs={{0,4},{4,0},{8,12},{12,8},{16,20},{20,16},{24,28},{28,24},{32,36},... | collective-permute-start | bytes 196616 | tf_op jit(solution)/shard_map/ppermute | solution.py:56
  7.7 6.8 %collective-permute-start.1 = (bf16[256,128]{1,0:T(8,128)(2,1)S(1)}, bf16[256,128]{1,0:T(8,128)(2,1)S(1)}, u32[]{:S(2)}, u32[]{:S(2)}) collective-permute-start(bf16[256,128]{1,0:T(8,128)(2,1)S(1)} %get-tuple-element.31), channel_id=1, source_target_pairs={{0,20},{4,16},{8,28},{12,24},{16,4},{20,0},{24,12},{28,8},{32,52},... | collective-permute-start | bytes 196616 | tf_op jit(solution)/shard_map/ppermute | solution.py:56
  10.3 4.1 %collective-permute-start.2 = (bf16[256,128]{1,0:T(8,128)(2,1)S(1)}, bf16[256,128]{1,0:T(8,128)(2,1)S(1)}, u32[]{:S(2)}, u32[]{:S(2)}) collective-permute-start(bf16[256,128]{1,0:T(8,128)(2,1)S(1)} %get-tuple-element.32), channel_id=1, source_target_pairs={{0,8},{4,12},{8,0},{12,4},{16,24},{20,28},{24,16},{28,20},{32,40},... | collective-permute-start | bytes 196616 | tf_op jit(solution)/shard_map/ppermute | solution.py:56
  10.6 4.9 %collective-permute-start.3 = (bf16[256,128]{1,0:T(8,128)(2,1)S(1)}, bf16[256,128]{1,0:T(8,128)(2,1)S(1)}, u32[]{:S(2)}, u32[]{:S(2)}) collective-permute-start(bf16[256,128]{1,0:T(8,128)(2,1)S(1)} %get-tuple-element.33), channel_id=1, source_target_pairs={{0,40},{4,44},{8,32},{12,36},{16,56},{20,60},{24,48},{28,52},{32,8... | collective-permute-start | bytes 196616 | tf_op jit(solution)/shard_map/ppermute | solution.py:56
  28.0 4.8 %collective-permute-start.5 = (f32[3456,128]{1,0:T(8,128)S(1)}, f32[3456,128]{1,0:T(8,128)S(1)}, u32[]{:S(2)}, u32[]{:S(2)}) collective-permute-start(f32[3456,128]{1,0:T(8,128)S(1)} %get-tuple-element.36), channel_id=1, source_target_pairs={{0,4},{4,0},{1,5},{5,1},{2,6},{6,2},{3,7},{7,3},{8,12},{12,8},{9,1... | collective-permute-start | bytes 5308424 | tf_op jit(solution)/shard_map/ppermute | solution.py:484
  33.9 23.0 %all-to-all-start = ((bf16[64,56,128]{2,1,0:T(8,128)(2,1)}), bf16[64,56,128]{2,1,0:T(8,128)(2,1)S(1)}, u32[]{:S(2)}, u32[]{:S(2)}) async-start(bf16[64,56,128]{2,1,0:T(8,128)(2,1)} %bitcast), calls=%async_computation | async-start | bytes 1835008 | tf_op jit(solution)/shard_map/all_to_all | solution.py:496
  58.0 25.0 %all-to-all-start.1 = ((bf16[64,56,128]{2,1,0:T(8,128)(2,1)}), bf16[64,56,128]{2,1,0:T(8,128)(2,1)S(1)}, u32[]{:S(2)}, u32[]{:S(2)}) async-start(bf16[64,56,128]{2,1,0:T(8,128)(2,1)} %shard_map.90), calls=%async_computation.1 | async-start | bytes 1835008 | tf_op jit(solution)/shard_map/all_to_all | solution.py:518
  63.2 14.9 %collective-permute-start.10 = (bf16[256,128]{1,0:T(8,128)(2,1)S(1)}, bf16[256,128]{1,0:T(8,128)(2,1)S(1)}, u32[]{:S(2)}, u32[]{:S(2)}) collective-permute-start(bf16[256,128]{1,0:T(8,128)(2,1)S(1)} %get-tuple-element.42.rest_4_), channel_id=1, source_target_pairs={{0,64},{4,68},{8,72},{12,76},{16,80},{20,84},{24,88},{28,92},{32,9... | collective-permute-start | bytes 196616 | tf_op jit(solution)/shard_map/ppermute | solution.py:56
  65.8 6.7 %collective-permute-start.6 = (bf16[128,128]{1,0:T(8,128)(2,1)S(1)}, bf16[128,128]{1,0:T(8,128)(2,1)S(1)}, u32[]{:S(2)}, u32[]{:S(2)}) collective-permute-start(bf16[128,128]{1,0:T(8,128)(2,1)S(1)} %get-tuple-element.38.rest_0_), channel_id=1, source_target_pairs={{0,4},{4,0},{8,12},{12,8},{16,20},{20,16},{24,28},{28,24},{32,36},... | collective-permute-start | bytes 98312 | tf_op jit(solution)/shard_map/ppermute | solution.py:56
  68.4 9.8 %collective-permute-start.7 = (bf16[128,128]{1,0:T(8,128)(2,1)S(1)}, bf16[128,128]{1,0:T(8,128)(2,1)S(1)}, u32[]{:S(2)}, u32[]{:S(2)}) collective-permute-start(bf16[128,128]{1,0:T(8,128)(2,1)S(1)} %get-tuple-element.39.rest_1_), channel_id=1, source_target_pairs={{0,20},{4,16},{8,28},{12,24},{16,4},{20,0},{24,12},{28,8},{32,52},... | collective-permute-start | bytes 98312 | tf_op jit(solution)/shard_map/ppermute | solution.py:56
  71.1 7.1 %collective-permute-start.8 = (bf16[128,128]{1,0:T(8,128)(2,1)S(1)}, bf16[128,128]{1,0:T(8,128)(2,1)S(1)}, u32[]{:S(2)}, u32[]{:S(2)}) collective-permute-start(bf16[128,128]{1,0:T(8,128)(2,1)S(1)} %get-tuple-element.40.rest_2_), channel_id=1, source_target_pairs={{0,8},{4,12},{8,0},{12,4},{16,24},{20,28},{24,16},{28,20},{32,40},... | collective-permute-start | bytes 98312 | tf_op jit(solution)/shard_map/ppermute | solution.py:56
  71.5 6.7 %collective-permute-start.9 = (bf16[128,128]{1,0:T(8,128)(2,1)S(1)}, bf16[128,128]{1,0:T(8,128)(2,1)S(1)}, u32[]{:S(2)}, u32[]{:S(2)}) collective-permute-start(bf16[128,128]{1,0:T(8,128)(2,1)S(1)} %get-tuple-element.41.rest_3_), channel_id=1, source_target_pairs={{0,40},{4,44},{8,32},{12,36},{16,56},{20,60},{24,48},{28,52},{32,8... | collective-permute-start | bytes 98312 | tf_op jit(solution)/shard_map/ppermute | solution.py:56
  83.0 2.7 %collective-permute-start.11 = (bf16[3584,128]{1,0:T(8,128)(2,1)S(1)}, bf16[3584,128]{1,0:T(8,128)(2,1)S(1)}, u32[]{:S(2)}, u32[]{:S(2)}) collective-permute-start(bf16[3584,128]{1,0:T(8,128)(2,1)S(1)} %bitcast.4), channel_id=1, source_target_pairs={{0,4},{4,0},{1,5},{5,1},{2,6},{6,2},{3,7},{7,3},{8,12},{12,8},{9,1... | collective-permute-start | bytes 2752520 | tf_op jit(solution)/shard_map/ppermute | solution.py:531

commit v6 on v5

--- a/solution.py
+++ b/solution.py
@@ -301,7 +301,7 @@
 
         @pl.when(core != of_core)
         def _():
-            other_terms[rows, :] = stacked
+            other_terms[rows, :] = stacked.astype(BF)
 
     def put_second(ti, blocks):
         put(1, 18 - 9 * ti, blocks[::-1])
@@ -359,10 +359,10 @@
     for q in range(8):
         rows = pl.ds(q * 448, 448)
         if q == 7:
-            staged[pl.ds(3136, 320), :] = (own[pl.ds(3136, 320), :] + other[pl.ds(3136, 320), :]).astype(BF)
+            staged[pl.ds(3136, 320), :] = (own[pl.ds(3136, 320), :] + other[pl.ds(3136, 320), :].astype(F32)).astype(BF)
             staged[pl.ds(ROWS, 128), :] = jnp.zeros((128, 128), BF)
         else:
-            staged[rows, :] = (own[rows, :] + other[rows, :]).astype(BF)
+            staged[rows, :] = (own[rows, :] + other[rows, :].astype(F32)).astype(BF)
         copies.append(pltpu.make_async_copy(staged.at[rows], terms.at[rows], sems.at[q]))
         copies[-1].start()
     for copy in copies:
@@ -473,7 +473,7 @@
     )
     hidden, own, other = call(
         main_kernel,
-        (blocks, terms_shape, terms_shape),
+        (blocks, terms_shape, jax.ShapeDtypeStruct((ROWS, 128), BF)),
         tuple(prepared) + (neighbours, occupied) + got,
         [VMEM] * 4 + [HBM] * 2 + [VMEM] * 5,
         sides + sides + padded + padded + [field, turned, turned, links, flags, sems],

time: 87.6 us -> 86.3 us (0.985)
  waiting for transfers between devices: 25.5 us -> 24.3 us
    ppermute x1, waiting for transfers between devices: 3.32 us -> 2.05 us  [step(): other = lax.ppermute(other, 'core', PARTNER)]
where the time goes in v6:
time: 86.3 us; the launch traced here: 85.8 us
  starting transfers between devices  34 us (39%)
  Pallas kernels  26.7 us (31%)
  waiting for transfers between devices  24.3 us (28%)
  between operations  0.91 us (1%)
    pallas_call x9, Pallas kernels, call(): pl.pallas_call(kernel, out_shape=outs, in_specs=specs, out_specs=tuple((o...  26.7 us
    ppermute x10, starting transfers between devices, exchange(): got.append(lax.ppermute(sent[way], SPACE, SWAPS[way]))  19.3 us
    all_to_all x1, waiting for transfers between devices, step(): lax.all_to_all(terms.reshape(64, CHUNK, 128), PEERS, split_axis=0, concat...  14.7 us
    all_to_all x1, starting transfers between devices, step(): lax.all_to_all(terms.reshape(64, CHUNK, 128), PEERS, split_axis=0, concat...  7.31 us
    ppermute x10, waiting for transfers between devices, exchange(): got.append(lax.ppermute(sent[way], SPACE, SWAPS[way]))  6.67 us
    all_to_all x1, starting transfers between devices, step(): lax.all_to_all(spread, PEERS, split_axis=0, concat_axis=0, tiled=True)  5.22 us
    ppermute x1, waiting for transfers between devices, step(): other = lax.ppermute(other, 'core', PARTNER)  2.05 us
  transfers between devices with their start and end apart: 14, of which 5 were waited for; matrix products, arithmetic and copies ran while one was open for 0% of the time, Pallas kernels for 11%

profile of v6, /device:TPU:1, one launch (start us, length us, event | category | flops | bytes accessed | tf_op | source)
XLA Modules:
  0.0 85.8 jit_solution(1532818179146924626)
XLA Ops:
  0.6 1.6 %shard_map.86 = (bf16[256,128]{1,0:T(8,128)(2,1)S(1)}, bf16[256,128]{1,0:T(8,128)(2,1)S(1)}, bf16[256,128]{1,0:T(8,128)(2,1)S(1)}, bf16[256,128]{1,0:T(8,128)(2,1)S(1)}, bf16[512,128]{1,0:T(8,128)(2,1)S(1)}) custom-call(bf16[1,4,512,128]{3,2,1,0:T(8,128)(2,1)} %voxels.3, bf16[1,4,512,128]{3,2,1,0:T(8,128)(2,1)} %cotangent.3, s32[1,4,6]{2,1,0:T(4,128)} %links_in.7), custom_call_target="tpu_custom_call" | custom-call | bytes 2097152 | tf_op jit(solution)/shard_map/pallas_call | solution.py:424
  2.2 4.5 %collective-permute-start.4 = (bf16[512,128]{1,0:T(8,128)(2,1)S(1)}, bf16[512,128]{1,0:T(8,128)(2,1)S(1)}, u32[]{:S(2)}, u32[]{:S(2)}) collective-permute-start(bf16[512,128]{1,0:T(8,128)(2,1)S(1)} %get-tuple-element.34), channel_id=1, source_target_pairs={{0,64},{4,68},{8,72},{12,76},{16,80},{20,84},{24,88},{28,92},{32,9... | collective-permute-start | bytes 393224 | tf_op jit(solution)/shard_map/ppermute | solution.py:56
  6.7 1.0 %collective-permute-start = (bf16[256,128]{1,0:T(8,128)(2,1)S(1)}, bf16[256,128]{1,0:T(8,128)(2,1)S(1)}, u32[]{:S(2)}, u32[]{:S(2)}) collective-permute-start(bf16[256,128]{1,0:T(8,128)(2,1)S(1)} %get-tuple-element.30), channel_id=1, source_target_pairs={{0,4},{4,0},{8,12},{12,8},{16,20},{20,16},{24,28},{28,24},{32,36},... | collective-permute-start | bytes 196616 | tf_op jit(solution)/shard_map/ppermute | solution.py:56
  7.7 2.7 %collective-permute-start.1 = (bf16[256,128]{1,0:T(8,128)(2,1)S(1)}, bf16[256,128]{1,0:T(8,128)(2,1)S(1)}, u32[]{:S(2)}, u32[]{:S(2)}) collective-permute-start(bf16[256,128]{1,0:T(8,128)(2,1)S(1)} %get-tuple-element.31), channel_id=1, source_target_pairs={{0,20},{4,16},{8,28},{12,24},{16,4},{20,0},{24,12},{28,8},{32,52},... | collective-permute-start | bytes 196616 | tf_op jit(solution)/shard_map/ppermute | solution.py:56
  10.3 0.2 collective-permute-start.2
  10.6 1.6 %collective-permute-start.3 = (bf16[256,128]{1,0:T(8,128)(2,1)S(1)}, bf16[256,128]{1,0:T(8,128)(2,1)S(1)}, u32[]{:S(2)}, u32[]{:S(2)}) collective-permute-start(bf16[256,128]{1,0:T(8,128)(2,1)S(1)} %get-tuple-element.33), channel_id=1, source_target_pairs={{0,40},{4,44},{8,32},{12,36},{16,56},{20,60},{24,48},{28,52},{32,8... | collective-permute-start | bytes 196616 | tf_op jit(solution)/shard_map/ppermute | solution.py:56
  12.2 2.2 %shard_map.85 = (f32[4,512,128]{2,1,0:T(8,128)S(1)}, f32[4,512,128]{2,1,0:T(8,128)S(1)}, bf16[4608,256]{1,0:T(8,128)(2,1)S(1)}, bf16[4608,256]{1,0:T(8,128)(2,1)S(1)}) custom-call(bf16[1,4,512,128]{3,2,1,0:T(8,128)(2,1)} %voxels.3, bf16[1,4,512,128]{3,2,1,0:T(8,128)(2,1)} %cotangent.3, s32[1,4]{1,0:T(1,128)} %occupied_in.5, bf16[27,128,128]{2,1,0:T(8,128)(2,1)} %first_in.1, ...), custom_call_target="tpu_custom_call" | custom-call | flops 1048576 | bytes 8388608 | tf_op jit(solution)/shard_map/pallas_call | solution.py:424
  14.4 0.0 collective-permute-done.g0
  14.4 0.0 collective-permute-done.1.g1
  14.4 0.0 collective-permute-done.2.g2
  14.4 1.1 %collective-permute-done.3.g3 = bf16[256,128]{1,0:T(8,128)(2,1)S(1)} collective-permute-done((bf16[256,128]{1,0:T(8,128)(2,1)S(1)}, bf16[256,128]{1,0:T(8,128)(2,1)S(1)}, u32[]{:S(2)}, u32[]{:S(2)}) %collective-permute-start.3) | collective-permute-done | bytes 65568 | tf_op jit(solution)/shard_map/ppermute | solution.py:56
  15.5 0.0 collective-permute-done.4.g4
  15.5 12.5 %shard_map.87 = (bf16[4,512,128]{2,1,0:T(8,128)(2,1)S(1)}, f32[3456,128]{1,0:T(8,128)S(1)}, bf16[3456,128]{1,0:T(8,128)(2,1)S(1)}) custom-call(f32[4,512,128]{2,1,0:T(8,128)S(1)} %get-tuple-element.26.x.masked, f32[4,512,128]{2,1,0:T(8,128)S(1)} %get-tuple-element.27.g, bf16[4608,256]{1,0:T(8,128)(2,1)S(1)} %get-tuple-element.28.first_pairs, ...), custom_call_target="tpu_custom_call" | custom-call | flops 8589934592 | bytes 8388608 | tf_op jit(solution)/shard_map/pallas_call | solution.py:424
  28.0 1.5 %collective-permute-start.5 = (bf16[3456,128]{1,0:T(8,128)(2,1)S(1)}, bf16[3456,128]{1,0:T(8,128)(2,1)S(1)}, u32[]{:S(2)}, u32[]{:S(2)}) collective-permute-start(bf16[3456,128]{1,0:T(8,128)(2,1)S(1)} %get-tuple-element.36), channel_id=1, source_target_pairs={{0,4},{4,0},{1,5},{5,1},{2,6},{6,2},{3,7},{7,3},{8,12},{12,8},{9,1... | collective-permute-start | bytes 2654216 | tf_op jit(solution)/shard_map/ppermute | solution.py:484
  29.5 2.1 %collective-permute-done.5.other = bf16[3456,128]{1,0:T(8,128)(2,1)S(1)} collective-permute-done((bf16[3456,128]{1,0:T(8,128)(2,1)S(1)}, bf16[3456,128]{1,0:T(8,128)(2,1)S(1)}, u32[]{:S(2)}, u32[]{:S(2)}) %collective-permute-start.5) | collective-permute-done | bytes 884768 | tf_op jit(solution)/shard_map/ppermute | solution.py:484
  31.5 1.0 %shard_map.88 = bf16[3584,128]{1,0:T(8,128)(2,1)} custom-call(f32[3456,128]{1,0:T(8,128)S(1)} %get-tuple-element.35.own, bf16[3456,128]{1,0:T(8,128)(2,1)S(1)} %collective-permute-done.5.other), custom_call_target="tpu_custom_call" | custom-call | bytes 4194304 | tf_op jit(solution)/shard_map/pallas_call | solution.py:424
  32.5 7.3 %all-to-all-start = ((bf16[64,56,128]{2,1,0:T(8,128)(2,1)}), bf16[64,56,128]{2,1,0:T(8,128)(2,1)S(1)}, u32[]{:S(2)}, u32[]{:S(2)}) async-start(bf16[64,56,128]{2,1,0:T(8,128)(2,1)} %bitcast), calls=%async_computation | async-start | bytes 1835008 | tf_op jit(solution)/shard_map/all_to_all | solution.py:496
  39.9 1.0 %shard_map.89 = (bf16[128,128]{1,0:T(8,128)(2,1)S(1)}, bf16[128,128]{1,0:T(8,128)(2,1)S(1)}, bf16[128,128]{1,0:T(8,128)(2,1)S(1)}, bf16[128,128]{1,0:T(8,128)(2,1)S(1)}, bf16[256,128]{1,0:T(8,128)(2,1)S(1)}) custom-call(bf16[4,512,128]{2,1,0:T(8,128)(2,1)S(1)} %get-tuple-element.37.hidden, s32[1,4,6]{2,1,0:T(4,128)} %links_in.7), custom_call_target="tpu_custom_call" | custom-call | bytes 1048576 | tf_op jit(solution)/shard_map/pallas_call | solution.py:424
  40.8 14.7 %all-to-all-done.chunks = bf16[64,56,128]{2,1,0:T(8,128)(2,1)S(1)} async-done(((bf16[64,56,128]{2,1,0:T(8,128)(2,1)}), bf16[64,56,128]{2,1,0:T(8,128)(2,1)S(1)}, u32[]{:S(2)}, u32[]{:S(2)}) %all-to-all-start) | async-done | bytes 917536 | tf_op jit(solution)/shard_map/all_to_all | solution.py:496
  55.5 1.2 %shard_map.90 = bf16[64,56,128]{2,1,0:T(8,128)(2,1)} custom-call(bf16[64,56,128]{2,1,0:T(8,128)(2,1)S(1)} %all-to-all-done.chunks, bf16[128,128]{1,0:T(8,128)(2,1)S(1)} %get-tuple-element.38.rest_0_, bf16[128,128]{1,0:T(8,128)(2,1)S(1)} %get-tuple-element.39.rest_1_, bf16[128,128]{1,0:T(8,128)(2,1)S(1)} %get-tuple-element.40.rest_2_, ...), custom_call_target="tpu_custom_call" | custom-call | bytes 2097152 | tf_op jit(solution)/shard_map/pallas_call | solution.py:424
  56.7 5.2 %all-to-all-start.1 = ((bf16[64,56,128]{2,1,0:T(8,128)(2,1)}), bf16[64,56,128]{2,1,0:T(8,128)(2,1)S(1)}, u32[]{:S(2)}, u32[]{:S(2)}) async-start(bf16[64,56,128]{2,1,0:T(8,128)(2,1)} %shard_map.90), calls=%async_computation.1 | async-start | bytes 1835008 | tf_op jit(solution)/shard_map/all_to_all | solution.py:518
  61.9 2.6 %collective-permute-start.10 = (bf16[256,128]{1,0:T(8,128)(2,1)S(1)}, bf16[256,128]{1,0:T(8,128)(2,1)S(1)}, u32[]{:S(2)}, u32[]{:S(2)}) collective-permute-start(bf16[256,128]{1,0:T(8,128)(2,1)S(1)} %get-tuple-element.42.rest_4_), channel_id=1, source_target_pairs={{0,64},{4,68},{8,72},{12,76},{16,80},{20,84},{24,88},{28,92},{32,9... | collective-permute-start | bytes 196616 | tf_op jit(solution)/shard_map/ppermute | solution.py:56
  64.5 2.6 %collective-permute-start.6 = (bf16[128,128]{1,0:T(8,128)(2,1)S(1)}, bf16[128,128]{1,0:T(8,128)(2,1)S(1)}, u32[]{:S(2)}, u32[]{:S(2)}) collective-permute-start(bf16[128,128]{1,0:T(8,128)(2,1)S(1)} %get-tuple-element.38.rest_0_), channel_id=1, source_target_pairs={{0,4},{4,0},{8,12},{12,8},{16,20},{20,16},{24,28},{28,24},{32,36},... | collective-permute-start | bytes 98312 | tf_op jit(solution)/shard_map/ppermute | solution.py:56
  67.1 2.7 %collective-permute-start.7 = (bf16[128,128]{1,0:T(8,128)(2,1)S(1)}, bf16[128,128]{1,0:T(8,128)(2,1)S(1)}, u32[]{:S(2)}, u32[]{:S(2)}) collective-permute-start(bf16[128,128]{1,0:T(8,128)(2,1)S(1)} %get-tuple-element.39.rest_1_), channel_id=1, source_target_pairs={{0,20},{4,16},{8,28},{12,24},{16,4},{20,0},{24,12},{28,8},{32,52},... | collective-permute-start | bytes 98312 | tf_op jit(solution)/shard_map/ppermute | solution.py:56
  69.8 0.4 collective-permute-start.8
  70.2 1.1 %collective-permute-start.9 = (bf16[128,128]{1,0:T(8,128)(2,1)S(1)}, bf16[128,128]{1,0:T(8,128)(2,1)S(1)}, u32[]{:S(2)}, u32[]{:S(2)}) collective-permute-start(bf16[128,128]{1,0:T(8,128)(2,1)S(1)} %get-tuple-element.41.rest_3_), channel_id=1, source_target_pairs={{0,40},{4,44},{8,32},{12,36},{16,56},{20,60},{24,48},{28,52},{32,8... | collective-permute-start | bytes 98312 | tf_op jit(solution)/shard_map/ppermute | solution.py:56
  71.3 0.0 collective-permute-done.6.g0
  71.3 5.6 %collective-permute-done.7.g1 = bf16[128,128]{1,0:T(8,128)(2,1)S(1)} collective-permute-done((bf16[128,128]{1,0:T(8,128)(2,1)S(1)}, bf16[128,128]{1,0:T(8,128)(2,1)S(1)}, u32[]{:S(2)}, u32[]{:S(2)}) %collective-permute-start.7) | collective-permute-done | bytes 32800 | tf_op jit(solution)/shard_map/ppermute | solution.py:56
  76.9 0.0 collective-permute-done.8.g2
  76.9 0.0 collective-permute-done.9.g3
  76.9 0.0 collective-permute-done.10.g4
  76.9 4.8 %shard_map.91 = bf16[1,4,512,128]{3,2,1,0:T(8,128)(2,1)} custom-call(f32[4,512,128]{2,1,0:T(8,128)S(1)} %get-tuple-element.26.x.masked, bf16[4,512,128]{2,1,0:T(8,128)(2,1)S(1)} %get-tuple-element.37.hidden, s32[1,4,6]{2,1,0:T(4,128)} %links_in.7, s32[1,4]{1,0:T(1,128)} %occupied_in.5, bf16[27,128,128]{2,1,0:T(8,128)(2,1)} %second_in.3, ...), custom_call_target="tpu_custom_call" | custom-call | flops 3221225472 | bytes 4194304 | tf_op jit(solution)/shard_map/pallas_call | solution.py:424
  81.7 0.0 all-to-all-done.1
  81.7 0.6 collective-permute-start.11
  82.3 1.3 %shard_map.92 = (f32[3456,128]{1,0:T(8,128)}, f32[3456,128]{1,0:T(8,128)}) custom-call(bf16[3584,128]{1,0:T(8,128)(2,1)S(1)} %bitcast.5), custom_call_target="tpu_custom_call" | custom-call | bytes 3145728 | tf_op jit(solution)/shard_map/pallas_call | solution.py:424
  83.6 0.8 collective-permute-done.11.other
  84.4 1.3 %shard_map.93 = (f32[3456,128]{1,0:T(8,128)}, f32[3456,128]{1,0:T(8,128)}) custom-call(bf16[3584,128]{1,0:T(8,128)(2,1)S(1)} %collective-permute-done.11.other, f32[3456,128]{1,0:T(8,128)} %get-tuple-element.45.first_in, f32[3456,128]{1,0:T(8,128)} %get-tuple-element.46.second_in), custom_call_target="tpu_custom_call", output_to_operand_aliasing={{0}: (1, {}), {1}: (2, {})} | custom-call | bytes 3145728 | tf_op jit(solution)/shard_map/pallas_call | solution.py:424
Async XLA Ops:
  2.2 13.3 %collective-permute-start.4 = (bf16[512,128]{1,0:T(8,128)(2,1)S(1)}, bf16[512,128]{1,0:T(8,128)(2,1)S(1)}, u32[]{:S(2)}, u32[]{:S(2)}) collective-permute-start(bf16[512,128]{1,0:T(8,128)(2,1)S(1)} %get-tuple-element.34), channel_id=1, source_target_pairs={{0,64},{4,68},{8,72},{12,76},{16,80},{20,84},{24,88},{28,92},{32,9... | collective-permute-start | bytes 393224 | tf_op jit(solution)/shard_map/ppermute | solution.py:56
  6.7 7.7 %collective-permute-start = (bf16[256,128]{1,0:T(8,128)(2,1)S(1)}, bf16[256,128]{1,0:T(8,128)(2,1)S(1)}, u32[]{:S(2)}, u32[]{:S(2)}) collective-permute-start(bf16[256,128]{1,0:T(8,128)(2,1)S(1)} %get-tuple-element.30), channel_id=1, source_target_pairs={{0,4},{4,0},{8,12},{12,8},{16,20},{20,16},{24,28},{28,24},{32,36},... | collective-permute-start | bytes 196616 | tf_op jit(solution)/shard_map/ppermute | solution.py:56
  7.7 6.8 %collective-permute-start.1 = (bf16[256,128]{1,0:T(8,128)(2,1)S(1)}, bf16[256,128]{1,0:T(8,128)(2,1)S(1)}, u32[]{:S(2)}, u32[]{:S(2)}) collective-permute-start(bf16[256,128]{1,0:T(8,128)(2,1)S(1)} %get-tuple-element.31), channel_id=1, source_target_pairs={{0,20},{4,16},{8,28},{12,24},{16,4},{20,0},{24,12},{28,8},{32,52},... | collective-permute-start | bytes 196616 | tf_op jit(solution)/shard_map/ppermute | solution.py:56
  10.3 4.1 %collective-permute-start.2 = (bf16[256,128]{1,0:T(8,128)(2,1)S(1)}, bf16[256,128]{1,0:T(8,128)(2,1)S(1)}, u32[]{:S(2)}, u32[]{:S(2)}) collective-permute-start(bf16[256,128]{1,0:T(8,128)(2,1)S(1)} %get-tuple-element.32), channel_id=1, source_target_pairs={{0,8},{4,12},{8,0},{12,4},{16,24},{20,28},{24,16},{28,20},{32,40},... | collective-permute-start | bytes 196616 | tf_op jit(solution)/shard_map/ppermute | solution.py:56
  10.6 4.9 %collective-permute-start.3 = (bf16[256,128]{1,0:T(8,128)(2,1)S(1)}, bf16[256,128]{1,0:T(8,128)(2,1)S(1)}, u32[]{:S(2)}, u32[]{:S(2)}) collective-permute-start(bf16[256,128]{1,0:T(8,128)(2,1)S(1)} %get-tuple-element.33), channel_id=1, source_target_pairs={{0,40},{4,44},{8,32},{12,36},{16,56},{20,60},{24,48},{28,52},{32,8... | collective-permute-start | bytes 196616 | tf_op jit(solution)/shard_map/ppermute | solution.py:56
  28.0 3.6 %collective-permute-start.5 = (bf16[3456,128]{1,0:T(8,128)(2,1)S(1)}, bf16[3456,128]{1,0:T(8,128)(2,1)S(1)}, u32[]{:S(2)}, u32[]{:S(2)}) collective-permute-start(bf16[3456,128]{1,0:T(8,128)(2,1)S(1)} %get-tuple-element.36), channel_id=1, source_target_pairs={{0,4},{4,0},{1,5},{5,1},{2,6},{6,2},{3,7},{7,3},{8,12},{12,8},{9,1... | collective-permute-start | bytes 2654216 | tf_op jit(solution)/shard_map/ppermute | solution.py:484
  32.5 23.0 %all-to-all-start = ((bf16[64,56,128]{2,1,0:T(8,128)(2,1)}), bf16[64,56,128]{2,1,0:T(8,128)(2,1)S(1)}, u32[]{:S(2)}, u32[]{:S(2)}) async-start(bf16[64,56,128]{2,1,0:T(8,128)(2,1)} %bitcast), calls=%async_computation | async-start | bytes 1835008 | tf_op jit(solution)/shard_map/all_to_all | solution.py:496
  56.7 25.0 %all-to-all-start.1 = ((bf16[64,56,128]{2,1,0:T(8,128)(2,1)}), bf16[64,56,128]{2,1,0:T(8,128)(2,1)S(1)}, u32[]{:S(2)}, u32[]{:S(2)}) async-start(bf16[64,56,128]{2,1,0:T(8,128)(2,1)} %shard_map.90), calls=%async_computation.1 | async-start | bytes 1835008 | tf_op jit(solution)/shard_map/all_to_all | solution.py:518
  61.9 14.9 %collective-permute-start.10 = (bf16[256,128]{1,0:T(8,128)(2,1)S(1)}, bf16[256,128]{1,0:T(8,128)(2,1)S(1)}, u32[]{:S(2)}, u32[]{:S(2)}) collective-permute-start(bf16[256,128]{1,0:T(8,128)(2,1)S(1)} %get-tuple-element.42.rest_4_), channel_id=1, source_target_pairs={{0,64},{4,68},{8,72},{12,76},{16,80},{20,84},{24,88},{28,92},{32,9... | collective-permute-start | bytes 196616 | tf_op jit(solution)/shard_map/ppermute | solution.py:56
  64.5 6.7 %collective-permute-start.6 = (bf16[128,128]{1,0:T(8,128)(2,1)S(1)}, bf16[128,128]{1,0:T(8,128)(2,1)S(1)}, u32[]{:S(2)}, u32[]{:S(2)}) collective-permute-start(bf16[128,128]{1,0:T(8,128)(2,1)S(1)} %get-tuple-element.38.rest_0_), channel_id=1, source_target_pairs={{0,4},{4,0},{8,12},{12,8},{16,20},{20,16},{24,28},{28,24},{32,36},... | collective-permute-start | bytes 98312 | tf_op jit(solution)/shard_map/ppermute | solution.py:56
  67.1 9.8 %collective-permute-start.7 = (bf16[128,128]{1,0:T(8,128)(2,1)S(1)}, bf16[128,128]{1,0:T(8,128)(2,1)S(1)}, u32[]{:S(2)}, u32[]{:S(2)}) collective-permute-start(bf16[128,128]{1,0:T(8,128)(2,1)S(1)} %get-tuple-element.39.rest_1_), channel_id=1, source_target_pairs={{0,20},{4,16},{8,28},{12,24},{16,4},{20,0},{24,12},{28,8},{32,52},... | collective-permute-start | bytes 98312 | tf_op jit(solution)/shard_map/ppermute | solution.py:56
  69.8 7.1 %collective-permute-start.8 = (bf16[128,128]{1,0:T(8,128)(2,1)S(1)}, bf16[128,128]{1,0:T(8,128)(2,1)S(1)}, u32[]{:S(2)}, u32[]{:S(2)}) collective-permute-start(bf16[128,128]{1,0:T(8,128)(2,1)S(1)} %get-tuple-element.40.rest_2_), channel_id=1, source_target_pairs={{0,8},{4,12},{8,0},{12,4},{16,24},{20,28},{24,16},{28,20},{32,40},... | collective-permute-start | bytes 98312 | tf_op jit(solution)/shard_map/ppermute | solution.py:56
  70.2 6.7 %collective-permute-start.9 = (bf16[128,128]{1,0:T(8,128)(2,1)S(1)}, bf16[128,128]{1,0:T(8,128)(2,1)S(1)}, u32[]{:S(2)}, u32[]{:S(2)}) collective-permute-start(bf16[128,128]{1,0:T(8,128)(2,1)S(1)} %get-tuple-element.41.rest_3_), channel_id=1, source_target_pairs={{0,40},{4,44},{8,32},{12,36},{16,56},{20,60},{24,48},{28,52},{32,8... | collective-permute-start | bytes 98312 | tf_op jit(solution)/shard_map/ppermute | solution.py:56
  81.7 2.7 %collective-permute-start.11 = (bf16[3584,128]{1,0:T(8,128)(2,1)S(1)}, bf16[3584,128]{1,0:T(8,128)(2,1)S(1)}, u32[]{:S(2)}, u32[]{:S(2)}) collective-permute-start(bf16[3584,128]{1,0:T(8,128)(2,1)S(1)} %bitcast.4), channel_id=1, source_target_pairs={{0,4},{4,0},{1,5},{5,1},{2,6},{6,2},{3,7},{7,3},{8,12},{12,8},{9,1... | collective-permute-start | bytes 2752520 | tf_op jit(solution)/shard_map/ppermute | solution.py:531

commit v7 on v6

--- a/solution.py
+++ b/solution.py
@@ -189,18 +189,20 @@
         pair_weights[pl.ds((t + 9) * 128, 128), pl.ds(128, 128)] = block
 
 
+GROUP = 16
+
+
 def weight_terms(wide, odd, turned, put):
-    for ti in range(3):
-        columns = []
-        for tj in range(3):
-            for tk in range(3):
-                columns.append(
-                    jnp.concatenate(
-                        [tap(wide, odd, n, i + ti, tj, tk) for n in range(4) for i in range(8)], axis=0
-                    )
-                )
+    for start in range(0, 27, GROUP):
+        taps = range(start, min(start + GROUP, 27))
+        columns = [
+            jnp.concatenate(
+                [tap(wide, odd, n, i + t // 9, t // 3 % 3, t % 3) for n in range(4) for i in range(8)], axis=0
+            )
+            for t in taps
+        ]
         total = jnp.dot(turned[...], jnp.concatenate(columns, axis=1), preferred_element_type=F32)
-        put(ti, [total[:, q * 128 : (q + 1) * 128] for q in range(9)])
+        put(start, [total[:, q * 128 : (q + 1) * 128] for q in range(len(taps))])
 
 
 def fetch(sems, *pairs):
@@ -292,7 +294,7 @@
     core = device & 1
 
     def put(of_core, start, blocks):
-        rows = pl.ds(start * 128, 1152)
+        rows = pl.ds(start * 128, 128 * len(blocks))
         stacked = jnp.concatenate(blocks, axis=0)
 
         @pl.when(core == of_core)
@@ -303,8 +305,8 @@
         def _():
             other_terms[rows, :] = stacked.astype(BF)
 
-    def put_second(ti, blocks):
-        put(1, 18 - 9 * ti, blocks[::-1])
+    def put_second(start, blocks):
+        put(1, 27 - start - len(blocks), blocks[::-1])
 
     weight_terms(wide_grad, odd_grad, hidden_turned, put_second)
 
@@ -318,8 +320,8 @@
 
     lax.fori_loop(0, 4 // SLOTS, backward, 0, unroll=True)
 
-    def put_first(ti, blocks):
-        put(0, 9 * ti, [block.T for block in blocks])
+    def put_first(start, blocks):
+        put(0, start, [block.T for block in blocks])
 
     weight_terms(wide, odd, grad_turned, put_first)
 

time: 86.3 us -> 85.6 us (level)
  no operation moved by 1% of the time
where the time goes in v7:
time: 85.6 us; the launch traced here: 85.2 us
  starting transfers between devices  34.1 us (40%)
  Pallas kernels  25.9 us (30%)
  waiting for transfers between devices  24.3 us (28%)
  between operations  0.91 us (1%)
    pallas_call x9, Pallas kernels, call(): pl.pallas_call(kernel, out_shape=outs, in_specs=specs, out_specs=tuple((o...  25.9 us
    ppermute x10, starting transfers between devices, exchange(): got.append(lax.ppermute(sent[way], SPACE, SWAPS[way]))  19.3 us
    all_to_all x1, waiting for transfers between devices, step(): lax.all_to_all(terms.reshape(64, CHUNK, 128), PEERS, split_axis=0, concat...  14.7 us
    all_to_all x1, starting transfers between devices, step(): lax.all_to_all(terms.reshape(64, CHUNK, 128), PEERS, split_axis=0, concat...  7.3 us
    ppermute x10, waiting for transfers between devices, exchange(): got.append(lax.ppermute(sent[way], SPACE, SWAPS[way]))  6.67 us
    all_to_all x1, starting transfers between devices, step(): lax.all_to_all(spread, PEERS, split_axis=0, concat_axis=0, tiled=True)  5.22 us
    ppermute x1, waiting for transfers between devices, step(): other = lax.ppermute(other, 'core', PARTNER)  2.05 us
  transfers between devices with their start and end apart: 14, of which 5 were waited for; matrix products, arithmetic and copies ran while one was open for 0% of the time, Pallas kernels for 11%

profile of v7, /device:TPU:1, one launch (start us, length us, event | category | flops | bytes accessed | tf_op | source)
XLA Modules:
  0.0 85.2 jit_solution(15739698889387111744)
XLA Ops:
  0.6 1.6 %shard_map.86 = (bf16[256,128]{1,0:T(8,128)(2,1)S(1)}, bf16[256,128]{1,0:T(8,128)(2,1)S(1)}, bf16[256,128]{1,0:T(8,128)(2,1)S(1)}, bf16[256,128]{1,0:T(8,128)(2,1)S(1)}, bf16[512,128]{1,0:T(8,128)(2,1)S(1)}) custom-call(bf16[1,4,512,128]{3,2,1,0:T(8,128)(2,1)} %voxels.3, bf16[1,4,512,128]{3,2,1,0:T(8,128)(2,1)} %cotangent.3, s32[1,4,6]{2,1,0:T(4,128)} %links_in.7), custom_call_target="tpu_custom_call" | custom-call | bytes 2097152 | tf_op jit(solution)/shard_map/pallas_call | solution.py:426
  2.2 4.5 %collective-permute-start.4 = (bf16[512,128]{1,0:T(8,128)(2,1)S(1)}, bf16[512,128]{1,0:T(8,128)(2,1)S(1)}, u32[]{:S(2)}, u32[]{:S(2)}) collective-permute-start(bf16[512,128]{1,0:T(8,128)(2,1)S(1)} %get-tuple-element.34), channel_id=1, source_target_pairs={{0,64},{4,68},{8,72},{12,76},{16,80},{20,84},{24,88},{28,92},{32,9... | collective-permute-start | bytes 393224 | tf_op jit(solution)/shard_map/ppermute | solution.py:56
  6.7 1.0 %collective-permute-start = (bf16[256,128]{1,0:T(8,128)(2,1)S(1)}, bf16[256,128]{1,0:T(8,128)(2,1)S(1)}, u32[]{:S(2)}, u32[]{:S(2)}) collective-permute-start(bf16[256,128]{1,0:T(8,128)(2,1)S(1)} %get-tuple-element.30), channel_id=1, source_target_pairs={{0,4},{4,0},{8,12},{12,8},{16,20},{20,16},{24,28},{28,24},{32,36},... | collective-permute-start | bytes 196616 | tf_op jit(solution)/shard_map/ppermute | solution.py:56
  7.7 2.7 %collective-permute-start.1 = (bf16[256,128]{1,0:T(8,128)(2,1)S(1)}, bf16[256,128]{1,0:T(8,128)(2,1)S(1)}, u32[]{:S(2)}, u32[]{:S(2)}) collective-permute-start(bf16[256,128]{1,0:T(8,128)(2,1)S(1)} %get-tuple-element.31), channel_id=1, source_target_pairs={{0,20},{4,16},{8,28},{12,24},{16,4},{20,0},{24,12},{28,8},{32,52},... | collective-permute-start | bytes 196616 | tf_op jit(solution)/shard_map/ppermute | solution.py:56
  10.3 0.2 collective-permute-start.2
  10.6 1.6 %collective-permute-start.3 = (bf16[256,128]{1,0:T(8,128)(2,1)S(1)}, bf16[256,128]{1,0:T(8,128)(2,1)S(1)}, u32[]{:S(2)}, u32[]{:S(2)}) collective-permute-start(bf16[256,128]{1,0:T(8,128)(2,1)S(1)} %get-tuple-element.33), channel_id=1, source_target_pairs={{0,40},{4,44},{8,32},{12,36},{16,56},{20,60},{24,48},{28,52},{32,8... | collective-permute-start | bytes 196616 | tf_op jit(solution)/shard_map/ppermute | solution.py:56
  12.2 2.2 %shard_map.85 = (f32[4,512,128]{2,1,0:T(8,128)S(1)}, f32[4,512,128]{2,1,0:T(8,128)S(1)}, bf16[4608,256]{1,0:T(8,128)(2,1)S(1)}, bf16[4608,256]{1,0:T(8,128)(2,1)S(1)}) custom-call(bf16[1,4,512,128]{3,2,1,0:T(8,128)(2,1)} %voxels.3, bf16[1,4,512,128]{3,2,1,0:T(8,128)(2,1)} %cotangent.3, s32[1,4]{1,0:T(1,128)} %occupied_in.5, bf16[27,128,128]{2,1,0:T(8,128)(2,1)} %first_in.1, ...), custom_call_target="tpu_custom_call" | custom-call | flops 1048576 | bytes 8388608 | tf_op jit(solution)/shard_map/pallas_call | solution.py:426
  14.4 0.0 collective-permute-done.g0
  14.4 0.0 collective-permute-done.1.g1
  14.4 0.0 collective-permute-done.2.g2
  14.4 1.1 %collective-permute-done.3.g3 = bf16[256,128]{1,0:T(8,128)(2,1)S(1)} collective-permute-done((bf16[256,128]{1,0:T(8,128)(2,1)S(1)}, bf16[256,128]{1,0:T(8,128)(2,1)S(1)}, u32[]{:S(2)}, u32[]{:S(2)}) %collective-permute-start.3) | collective-permute-done | bytes 65568 | tf_op jit(solution)/shard_map/ppermute | solution.py:56
  15.5 0.0 collective-permute-done.4.g4
  15.5 11.6 %shard_map.87 = (bf16[4,512,128]{2,1,0:T(8,128)(2,1)S(1)}, f32[3456,128]{1,0:T(8,128)S(1)}, bf16[3456,128]{1,0:T(8,128)(2,1)S(1)}) custom-call(f32[4,512,128]{2,1,0:T(8,128)S(1)} %get-tuple-element.26.x.masked, f32[4,512,128]{2,1,0:T(8,128)S(1)} %get-tuple-element.27.g, bf16[4608,256]{1,0:T(8,128)(2,1)S(1)} %get-tuple-element.28.first_pairs, ...), custom_call_target="tpu_custom_call" | custom-call | flops 8589934592 | bytes 8388608 | tf_op jit(solution)/shard_map/pallas_call | solution.py:426
  27.1 1.7 %collective-permute-start.5 = (bf16[3456,128]{1,0:T(8,128)(2,1)S(1)}, bf16[3456,128]{1,0:T(8,128)(2,1)S(1)}, u32[]{:S(2)}, u32[]{:S(2)}) collective-permute-start(bf16[3456,128]{1,0:T(8,128)(2,1)S(1)} %get-tuple-element.36), channel_id=1, source_target_pairs={{0,4},{4,0},{1,5},{5,1},{2,6},{6,2},{3,7},{7,3},{8,12},{12,8},{9,1... | collective-permute-start | bytes 2654216 | tf_op jit(solution)/shard_map/ppermute | solution.py:486
  28.8 2.1 %collective-permute-done.5.other = bf16[3456,128]{1,0:T(8,128)(2,1)S(1)} collective-permute-done((bf16[3456,128]{1,0:T(8,128)(2,1)S(1)}, bf16[3456,128]{1,0:T(8,128)(2,1)S(1)}, u32[]{:S(2)}, u32[]{:S(2)}) %collective-permute-start.5) | collective-permute-done | bytes 884768 | tf_op jit(solution)/shard_map/ppermute | solution.py:486
  30.9 1.0 %shard_map.88 = bf16[3584,128]{1,0:T(8,128)(2,1)} custom-call(f32[3456,128]{1,0:T(8,128)S(1)} %get-tuple-element.35.own, bf16[3456,128]{1,0:T(8,128)(2,1)S(1)} %collective-permute-done.5.other), custom_call_target="tpu_custom_call" | custom-call | bytes 4194304 | tf_op jit(solution)/shard_map/pallas_call | solution.py:426
  31.9 7.3 %all-to-all-start = ((bf16[64,56,128]{2,1,0:T(8,128)(2,1)}), bf16[64,56,128]{2,1,0:T(8,128)(2,1)S(1)}, u32[]{:S(2)}, u32[]{:S(2)}) async-start(bf16[64,56,128]{2,1,0:T(8,128)(2,1)} %bitcast), calls=%async_computation | async-start | bytes 1835008 | tf_op jit(solution)/shard_map/all_to_all | solution.py:498
  39.2 1.0 %shard_map.89 = (bf16[128,128]{1,0:T(8,128)(2,1)S(1)}, bf16[128,128]{1,0:T(8,128)(2,1)S(1)}, bf16[128,128]{1,0:T(8,128)(2,1)S(1)}, bf16[128,128]{1,0:T(8,128)(2,1)S(1)}, bf16[256,128]{1,0:T(8,128)(2,1)S(1)}) custom-call(bf16[4,512,128]{2,1,0:T(8,128)(2,1)S(1)} %get-tuple-element.37.hidden, s32[1,4,6]{2,1,0:T(4,128)} %links_in.7), custom_call_target="tpu_custom_call" | custom-call | bytes 1048576 | tf_op jit(solution)/shard_map/pallas_call | solution.py:426
  40.2 14.7 %all-to-all-done.chunks = bf16[64,56,128]{2,1,0:T(8,128)(2,1)S(1)} async-done(((bf16[64,56,128]{2,1,0:T(8,128)(2,1)}), bf16[64,56,128]{2,1,0:T(8,128)(2,1)S(1)}, u32[]{:S(2)}, u32[]{:S(2)}) %all-to-all-start) | async-done | bytes 917536 | tf_op jit(solution)/shard_map/all_to_all | solution.py:498
  54.9 1.2 %shard_map.90 = bf16[64,56,128]{2,1,0:T(8,128)(2,1)} custom-call(bf16[64,56,128]{2,1,0:T(8,128)(2,1)S(1)} %all-to-all-done.chunks, bf16[128,128]{1,0:T(8,128)(2,1)S(1)} %get-tuple-element.38.rest_0_, bf16[128,128]{1,0:T(8,128)(2,1)S(1)} %get-tuple-element.39.rest_1_, bf16[128,128]{1,0:T(8,128)(2,1)S(1)} %get-tuple-element.40.rest_2_, ...), custom_call_target="tpu_custom_call" | custom-call | bytes 2097152 | tf_op jit(solution)/shard_map/pallas_call | solution.py:426
  56.0 5.2 %all-to-all-start.1 = ((bf16[64,56,128]{2,1,0:T(8,128)(2,1)}), bf16[64,56,128]{2,1,0:T(8,128)(2,1)S(1)}, u32[]{:S(2)}, u32[]{:S(2)}) async-start(bf16[64,56,128]{2,1,0:T(8,128)(2,1)} %shard_map.90), calls=%async_computation.1 | async-start | bytes 1835008 | tf_op jit(solution)/shard_map/all_to_all | solution.py:520
  61.2 2.6 %collective-permute-start.10 = (bf16[256,128]{1,0:T(8,128)(2,1)S(1)}, bf16[256,128]{1,0:T(8,128)(2,1)S(1)}, u32[]{:S(2)}, u32[]{:S(2)}) collective-permute-start(bf16[256,128]{1,0:T(8,128)(2,1)S(1)} %get-tuple-element.42.rest_4_), channel_id=1, source_target_pairs={{0,64},{4,68},{8,72},{12,76},{16,80},{20,84},{24,88},{28,92},{32,9... | collective-permute-start | bytes 196616 | tf_op jit(solution)/shard_map/ppermute | solution.py:56
  63.8 2.6 %collective-permute-start.6 = (bf16[128,128]{1,0:T(8,128)(2,1)S(1)}, bf16[128,128]{1,0:T(8,128)(2,1)S(1)}, u32[]{:S(2)}, u32[]{:S(2)}) collective-permute-start(bf16[128,128]{1,0:T(8,128)(2,1)S(1)} %get-tuple-element.38.rest_0_), channel_id=1, source_target_pairs={{0,4},{4,0},{8,12},{12,8},{16,20},{20,16},{24,28},{28,24},{32,36},... | collective-permute-start | bytes 98312 | tf_op jit(solution)/shard_map/ppermute | solution.py:56
  66.4 2.7 %collective-permute-start.7 = (bf16[128,128]{1,0:T(8,128)(2,1)S(1)}, bf16[128,128]{1,0:T(8,128)(2,1)S(1)}, u32[]{:S(2)}, u32[]{:S(2)}) collective-permute-start(bf16[128,128]{1,0:T(8,128)(2,1)S(1)} %get-tuple-element.39.rest_1_), channel_id=1, source_target_pairs={{0,20},{4,16},{8,28},{12,24},{16,4},{20,0},{24,12},{28,8},{32,52},... | collective-permute-start | bytes 98312 | tf_op jit(solution)/shard_map/ppermute | solution.py:56
  69.1 0.4 collective-permute-start.8
  69.5 1.1 %collective-permute-start.9 = (bf16[128,128]{1,0:T(8,128)(2,1)S(1)}, bf16[128,128]{1,0:T(8,128)(2,1)S(1)}, u32[]{:S(2)}, u32[]{:S(2)}) collective-permute-start(bf16[128,128]{1,0:T(8,128)(2,1)S(1)} %get-tuple-element.41.rest_3_), channel_id=1, source_target_pairs={{0,40},{4,44},{8,32},{12,36},{16,56},{20,60},{24,48},{28,52},{32,8... | collective-permute-start | bytes 98312 | tf_op jit(solution)/shard_map/ppermute | solution.py:56
  70.6 0.0 collective-permute-done.6.g0
  70.6 5.6 %collective-permute-done.7.g1 = bf16[128,128]{1,0:T(8,128)(2,1)S(1)} collective-permute-done((bf16[128,128]{1,0:T(8,128)(2,1)S(1)}, bf16[128,128]{1,0:T(8,128)(2,1)S(1)}, u32[]{:S(2)}, u32[]{:S(2)}) %collective-permute-start.7) | collective-permute-done | bytes 32800 | tf_op jit(solution)/shard_map/ppermute | solution.py:56
  76.2 0.0 collective-permute-done.8.g2
  76.2 0.0 collective-permute-done.9.g3
  76.2 0.0 collective-permute-done.10.g4
  76.2 4.8 %shard_map.91 = bf16[1,4,512,128]{3,2,1,0:T(8,128)(2,1)} custom-call(f32[4,512,128]{2,1,0:T(8,128)S(1)} %get-tuple-element.26.x.masked, bf16[4,512,128]{2,1,0:T(8,128)(2,1)S(1)} %get-tuple-element.37.hidden, s32[1,4,6]{2,1,0:T(4,128)} %links_in.7, s32[1,4]{1,0:T(1,128)} %occupied_in.5, bf16[27,128,128]{2,1,0:T(8,128)(2,1)} %second_in.3, ...), custom_call_target="tpu_custom_call" | custom-call | flops 3221225472 | bytes 4194304 | tf_op jit(solution)/shard_map/pallas_call | solution.py:426
  81.0 0.0 all-to-all-done.1
  81.0 0.6 collective-permute-start.11
  81.6 1.3 %shard_map.92 = (f32[3456,128]{1,0:T(8,128)}, f32[3456,128]{1,0:T(8,128)}) custom-call(bf16[3584,128]{1,0:T(8,128)(2,1)S(1)} %bitcast.5), custom_call_target="tpu_custom_call" | custom-call | bytes 3145728 | tf_op jit(solution)/shard_map/pallas_call | solution.py:426
  82.9 0.8 collective-permute-done.11.other
  83.7 1.3 %shard_map.93 = (f32[3456,128]{1,0:T(8,128)}, f32[3456,128]{1,0:T(8,128)}) custom-call(bf16[3584,128]{1,0:T(8,128)(2,1)S(1)} %collective-permute-done.11.other, f32[3456,128]{1,0:T(8,128)} %get-tuple-element.45.first_in, f32[3456,128]{1,0:T(8,128)} %get-tuple-element.46.second_in), custom_call_target="tpu_custom_call", output_to_operand_aliasing={{0}: (1, {}), {1}: (2, {})} | custom-call | bytes 3145728 | tf_op jit(solution)/shard_map/pallas_call | solution.py:426
Async XLA Ops:
  2.2 13.3 %collective-permute-start.4 = (bf16[512,128]{1,0:T(8,128)(2,1)S(1)}, bf16[512,128]{1,0:T(8,128)(2,1)S(1)}, u32[]{:S(2)}, u32[]{:S(2)}) collective-permute-start(bf16[512,128]{1,0:T(8,128)(2,1)S(1)} %get-tuple-element.34), channel_id=1, source_target_pairs={{0,64},{4,68},{8,72},{12,76},{16,80},{20,84},{24,88},{28,92},{32,9... | collective-permute-start | bytes 393224 | tf_op jit(solution)/shard_map/ppermute | solution.py:56
  6.7 7.7 %collective-permute-start = (bf16[256,128]{1,0:T(8,128)(2,1)S(1)}, bf16[256,128]{1,0:T(8,128)(2,1)S(1)}, u32[]{:S(2)}, u32[]{:S(2)}) collective-permute-start(bf16[256,128]{1,0:T(8,128)(2,1)S(1)} %get-tuple-element.30), channel_id=1, source_target_pairs={{0,4},{4,0},{8,12},{12,8},{16,20},{20,16},{24,28},{28,24},{32,36},... | collective-permute-start | bytes 196616 | tf_op jit(solution)/shard_map/ppermute | solution.py:56
  7.7 6.8 %collective-permute-start.1 = (bf16[256,128]{1,0:T(8,128)(2,1)S(1)}, bf16[256,128]{1,0:T(8,128)(2,1)S(1)}, u32[]{:S(2)}, u32[]{:S(2)}) collective-permute-start(bf16[256,128]{1,0:T(8,128)(2,1)S(1)} %get-tuple-element.31), channel_id=1, source_target_pairs={{0,20},{4,16},{8,28},{12,24},{16,4},{20,0},{24,12},{28,8},{32,52},... | collective-permute-start | bytes 196616 | tf_op jit(solution)/shard_map/ppermute | solution.py:56
  10.3 4.1 %collective-permute-start.2 = (bf16[256,128]{1,0:T(8,128)(2,1)S(1)}, bf16[256,128]{1,0:T(8,128)(2,1)S(1)}, u32[]{:S(2)}, u32[]{:S(2)}) collective-permute-start(bf16[256,128]{1,0:T(8,128)(2,1)S(1)} %get-tuple-element.32), channel_id=1, source_target_pairs={{0,8},{4,12},{8,0},{12,4},{16,24},{20,28},{24,16},{28,20},{32,40},... | collective-permute-start | bytes 196616 | tf_op jit(solution)/shard_map/ppermute | solution.py:56
  10.6 4.9 %collective-permute-start.3 = (bf16[256,128]{1,0:T(8,128)(2,1)S(1)}, bf16[256,128]{1,0:T(8,128)(2,1)S(1)}, u32[]{:S(2)}, u32[]{:S(2)}) collective-permute-start(bf16[256,128]{1,0:T(8,128)(2,1)S(1)} %get-tuple-element.33), channel_id=1, source_target_pairs={{0,40},{4,44},{8,32},{12,36},{16,56},{20,60},{24,48},{28,52},{32,8... | collective-permute-start | bytes 196616 | tf_op jit(solution)/shard_map/ppermute | solution.py:56
  27.1 3.7 %collective-permute-start.5 = (bf16[3456,128]{1,0:T(8,128)(2,1)S(1)}, bf16[3456,128]{1,0:T(8,128)(2,1)S(1)}, u32[]{:S(2)}, u32[]{:S(2)}) collective-permute-start(bf16[3456,128]{1,0:T(8,128)(2,1)S(1)} %get-tuple-element.36), channel_id=1, source_target_pairs={{0,4},{4,0},{1,5},{5,1},{2,6},{6,2},{3,7},{7,3},{8,12},{12,8},{9,1... | collective-permute-start | bytes 2654216 | tf_op jit(solution)/shard_map/ppermute | solution.py:486
  31.9 23.0 %all-to-all-start = ((bf16[64,56,128]{2,1,0:T(8,128)(2,1)}), bf16[64,56,128]{2,1,0:T(8,128)(2,1)S(1)}, u32[]{:S(2)}, u32[]{:S(2)}) async-start(bf16[64,56,128]{2,1,0:T(8,128)(2,1)} %bitcast), calls=%async_computation | async-start | bytes 1835008 | tf_op jit(solution)/shard_map/all_to_all | solution.py:498
  56.0 25.0 %all-to-all-start.1 = ((bf16[64,56,128]{2,1,0:T(8,128)(2,1)}), bf16[64,56,128]{2,1,0:T(8,128)(2,1)S(1)}, u32[]{:S(2)}, u32[]{:S(2)}) async-start(bf16[64,56,128]{2,1,0:T(8,128)(2,1)} %shard_map.90), calls=%async_computation.1 | async-start | bytes 1835008 | tf_op jit(solution)/shard_map/all_to_all | solution.py:520
  61.2 14.9 %collective-permute-start.10 = (bf16[256,128]{1,0:T(8,128)(2,1)S(1)}, bf16[256,128]{1,0:T(8,128)(2,1)S(1)}, u32[]{:S(2)}, u32[]{:S(2)}) collective-permute-start(bf16[256,128]{1,0:T(8,128)(2,1)S(1)} %get-tuple-element.42.rest_4_), channel_id=1, source_target_pairs={{0,64},{4,68},{8,72},{12,76},{16,80},{20,84},{24,88},{28,92},{32,9... | collective-permute-start | bytes 196616 | tf_op jit(solution)/shard_map/ppermute | solution.py:56
  63.8 6.7 %collective-permute-start.6 = (bf16[128,128]{1,0:T(8,128)(2,1)S(1)}, bf16[128,128]{1,0:T(8,128)(2,1)S(1)}, u32[]{:S(2)}, u32[]{:S(2)}) collective-permute-start(bf16[128,128]{1,0:T(8,128)(2,1)S(1)} %get-tuple-element.38.rest_0_), channel_id=1, source_target_pairs={{0,4},{4,0},{8,12},{12,8},{16,20},{20,16},{24,28},{28,24},{32,36},... | collective-permute-start | bytes 98312 | tf_op jit(solution)/shard_map/ppermute | solution.py:56
  66.4 9.8 %collective-permute-start.7 = (bf16[128,128]{1,0:T(8,128)(2,1)S(1)}, bf16[128,128]{1,0:T(8,128)(2,1)S(1)}, u32[]{:S(2)}, u32[]{:S(2)}) collective-permute-start(bf16[128,128]{1,0:T(8,128)(2,1)S(1)} %get-tuple-element.39.rest_1_), channel_id=1, source_target_pairs={{0,20},{4,16},{8,28},{12,24},{16,4},{20,0},{24,12},{28,8},{32,52},... | collective-permute-start | bytes 98312 | tf_op jit(solution)/shard_map/ppermute | solution.py:56
  69.1 7.1 %collective-permute-start.8 = (bf16[128,128]{1,0:T(8,128)(2,1)S(1)}, bf16[128,128]{1,0:T(8,128)(2,1)S(1)}, u32[]{:S(2)}, u32[]{:S(2)}) collective-permute-start(bf16[128,128]{1,0:T(8,128)(2,1)S(1)} %get-tuple-element.40.rest_2_), channel_id=1, source_target_pairs={{0,8},{4,12},{8,0},{12,4},{16,24},{20,28},{24,16},{28,20},{32,40},... | collective-permute-start | bytes 98312 | tf_op jit(solution)/shard_map/ppermute | solution.py:56
  69.5 6.7 %collective-permute-start.9 = (bf16[128,128]{1,0:T(8,128)(2,1)S(1)}, bf16[128,128]{1,0:T(8,128)(2,1)S(1)}, u32[]{:S(2)}, u32[]{:S(2)}) collective-permute-start(bf16[128,128]{1,0:T(8,128)(2,1)S(1)} %get-tuple-element.41.rest_3_), channel_id=1, source_target_pairs={{0,40},{4,44},{8,32},{12,36},{16,56},{20,60},{24,48},{28,52},{32,8... | collective-permute-start | bytes 98312 | tf_op jit(solution)/shard_map/ppermute | solution.py:56
  81.0 2.7 %collective-permute-start.11 = (bf16[3584,128]{1,0:T(8,128)(2,1)S(1)}, bf16[3584,128]{1,0:T(8,128)(2,1)S(1)}, u32[]{:S(2)}, u32[]{:S(2)}) collective-permute-start(bf16[3584,128]{1,0:T(8,128)(2,1)S(1)} %bitcast.4), channel_id=1, source_target_pairs={{0,4},{4,0},{1,5},{5,1},{2,6},{6,2},{3,7},{7,3},{8,12},{12,8},{9,1... | collective-permute-start | bytes 2752520 | tf_op jit(solution)/shard_map/ppermute | solution.py:533

commit v8 on v7

--- a/solution.py
+++ b/solution.py
@@ -85,14 +85,11 @@
             for n in range(4):
                 link = links[0, n, 2 * axis + side]
                 remote = (link >= 0) & ((link >> 2) != device)
-                at = rank
-
-                @pl.when(remote)
-                def _():
-                    for a, x in enumerate(fields):
-                        row = pl.multiple_of((a * width + at) * 64, 64)
-                        send[pl.ds(row, 64), :] = face_of(x, n, axis, side * 7).astype(BF)
-
+                at = jnp.minimum(rank, width - 1)
+                for a, x in enumerate(fields):
+                    row = pl.ds(pl.multiple_of((a * width + at) * 64, 64), 64)
+                    face = face_of(x, n, axis, side * 7).astype(BF)
+                    send[row, :] = jnp.where(remote, face, send[row, :])
                 rank = rank + remote.astype(jnp.int32)
 
 

time: 85.6 us -> 85.5 us (level)
  no operation moved by 1% of the time
where the time goes in v8:
time: 85.5 us; the launch traced here: 85.1 us
  starting transfers between devices  34.1 us (40%)
  Pallas kernels  25.8 us (30%)
  waiting for transfers between devices  24.3 us (28%)
  between operations  0.91 us (1%)
    pallas_call x9, Pallas kernels, call(): pl.pallas_call(kernel, out_shape=outs, in_specs=specs, out_specs=tuple((o...  25.8 us
    ppermute x10, starting transfers between devices, exchange(): got.append(lax.ppermute(sent[way], SPACE, SWAPS[way]))  19.3 us
    all_to_all x1, waiting for transfers between devices, step(): lax.all_to_all(terms.reshape(64, CHUNK, 128), PEERS, split_axis=0, concat...  14.8 us
    all_to_all x1, starting transfers between devices, step(): lax.all_to_all(terms.reshape(64, CHUNK, 128), PEERS, split_axis=0, concat...  7.25 us
    ppermute x10, waiting for transfers between devices, exchange(): got.append(lax.ppermute(sent[way], SPACE, SWAPS[way]))  6.67 us
    all_to_all x1, starting transfers between devices, step(): lax.all_to_all(spread, PEERS, split_axis=0, concat_axis=0, tiled=True)  5.22 us
    ppermute x1, waiting for transfers between devices, step(): other = lax.ppermute(other, 'core', PARTNER)  2.05 us
  transfers between devices with their start and end apart: 14, of which 5 were waited for; matrix products, arithmetic and copies ran while one was open for 0% of the time, Pallas kernels for 11%

profile of v8, /device:TPU:1, one launch (start us, length us, event | category | flops | bytes accessed | tf_op | source)
XLA Modules:
  0.0 85.1 jit_solution(16224313043868523739)
XLA Ops:
  0.6 1.6 %shard_map.86 = (bf16[256,128]{1,0:T(8,128)(2,1)S(1)}, bf16[256,128]{1,0:T(8,128)(2,1)S(1)}, bf16[256,128]{1,0:T(8,128)(2,1)S(1)}, bf16[256,128]{1,0:T(8,128)(2,1)S(1)}, bf16[512,128]{1,0:T(8,128)(2,1)S(1)}) custom-call(bf16[1,4,512,128]{3,2,1,0:T(8,128)(2,1)} %voxels.3, bf16[1,4,512,128]{3,2,1,0:T(8,128)(2,1)} %cotangent.3, s32[1,4,6]{2,1,0:T(4,128)} %links_in.7), custom_call_target="tpu_custom_call" | custom-call | bytes 2097152 | tf_op jit(solution)/shard_map/pallas_call | solution.py:423
  2.2 4.5 %collective-permute-start.4 = (bf16[512,128]{1,0:T(8,128)(2,1)S(1)}, bf16[512,128]{1,0:T(8,128)(2,1)S(1)}, u32[]{:S(2)}, u32[]{:S(2)}) collective-permute-start(bf16[512,128]{1,0:T(8,128)(2,1)S(1)} %get-tuple-element.34), channel_id=1, source_target_pairs={{0,64},{4,68},{8,72},{12,76},{16,80},{20,84},{24,88},{28,92},{32,9... | collective-permute-start | bytes 393224 | tf_op jit(solution)/shard_map/ppermute | solution.py:56
  6.7 1.0 %collective-permute-start = (bf16[256,128]{1,0:T(8,128)(2,1)S(1)}, bf16[256,128]{1,0:T(8,128)(2,1)S(1)}, u32[]{:S(2)}, u32[]{:S(2)}) collective-permute-start(bf16[256,128]{1,0:T(8,128)(2,1)S(1)} %get-tuple-element.30), channel_id=1, source_target_pairs={{0,4},{4,0},{8,12},{12,8},{16,20},{20,16},{24,28},{28,24},{32,36},... | collective-permute-start | bytes 196616 | tf_op jit(solution)/shard_map/ppermute | solution.py:56
  7.7 2.6 %collective-permute-start.1 = (bf16[256,128]{1,0:T(8,128)(2,1)S(1)}, bf16[256,128]{1,0:T(8,128)(2,1)S(1)}, u32[]{:S(2)}, u32[]{:S(2)}) collective-permute-start(bf16[256,128]{1,0:T(8,128)(2,1)S(1)} %get-tuple-element.31), channel_id=1, source_target_pairs={{0,20},{4,16},{8,28},{12,24},{16,4},{20,0},{24,12},{28,8},{32,52},... | collective-permute-start | bytes 196616 | tf_op jit(solution)/shard_map/ppermute | solution.py:56
  10.3 0.3 collective-permute-start.2
  10.6 1.6 %collective-permute-start.3 = (bf16[256,128]{1,0:T(8,128)(2,1)S(1)}, bf16[256,128]{1,0:T(8,128)(2,1)S(1)}, u32[]{:S(2)}, u32[]{:S(2)}) collective-permute-start(bf16[256,128]{1,0:T(8,128)(2,1)S(1)} %get-tuple-element.33), channel_id=1, source_target_pairs={{0,40},{4,44},{8,32},{12,36},{16,56},{20,60},{24,48},{28,52},{32,8... | collective-permute-start | bytes 196616 | tf_op jit(solution)/shard_map/ppermute | solution.py:56
  12.2 2.2 %shard_map.85 = (f32[4,512,128]{2,1,0:T(8,128)S(1)}, f32[4,512,128]{2,1,0:T(8,128)S(1)}, bf16[4608,256]{1,0:T(8,128)(2,1)S(1)}, bf16[4608,256]{1,0:T(8,128)(2,1)S(1)}) custom-call(bf16[1,4,512,128]{3,2,1,0:T(8,128)(2,1)} %voxels.3, bf16[1,4,512,128]{3,2,1,0:T(8,128)(2,1)} %cotangent.3, s32[1,4]{1,0:T(1,128)} %occupied_in.5, bf16[27,128,128]{2,1,0:T(8,128)(2,1)} %first_in.1, ...), custom_call_target="tpu_custom_call" | custom-call | flops 1048576 | bytes 8388608 | tf_op jit(solution)/shard_map/pallas_call | solution.py:423
  14.4 0.0 collective-permute-done.g0
  14.4 0.0 collective-permute-done.1.g1
  14.5 0.0 collective-permute-done.2.g2
  14.5 1.1 %collective-permute-done.3.g3 = bf16[256,128]{1,0:T(8,128)(2,1)S(1)} collective-permute-done((bf16[256,128]{1,0:T(8,128)(2,1)S(1)}, bf16[256,128]{1,0:T(8,128)(2,1)S(1)}, u32[]{:S(2)}, u32[]{:S(2)}) %collective-permute-start.3) | collective-permute-done | bytes 65568 | tf_op jit(solution)/shard_map/ppermute | solution.py:56
  15.5 0.0 collective-permute-done.4.g4
  15.5 11.6 %shard_map.87 = (bf16[4,512,128]{2,1,0:T(8,128)(2,1)S(1)}, f32[3456,128]{1,0:T(8,128)S(1)}, bf16[3456,128]{1,0:T(8,128)(2,1)S(1)}) custom-call(f32[4,512,128]{2,1,0:T(8,128)S(1)} %get-tuple-element.26.x.masked, f32[4,512,128]{2,1,0:T(8,128)S(1)} %get-tuple-element.27.g, bf16[4608,256]{1,0:T(8,128)(2,1)S(1)} %get-tuple-element.28.first_pairs, ...), custom_call_target="tpu_custom_call" | custom-call | flops 8589934592 | bytes 8388608 | tf_op jit(solution)/shard_map/pallas_call | solution.py:423
  27.2 1.7 %collective-permute-start.5 = (bf16[3456,128]{1,0:T(8,128)(2,1)S(1)}, bf16[3456,128]{1,0:T(8,128)(2,1)S(1)}, u32[]{:S(2)}, u32[]{:S(2)}) collective-permute-start(bf16[3456,128]{1,0:T(8,128)(2,1)S(1)} %get-tuple-element.36), channel_id=1, source_target_pairs={{0,4},{4,0},{1,5},{5,1},{2,6},{6,2},{3,7},{7,3},{8,12},{12,8},{9,1... | collective-permute-start | bytes 2654216 | tf_op jit(solution)/shard_map/ppermute | solution.py:483
  28.8 2.1 %collective-permute-done.5.other = bf16[3456,128]{1,0:T(8,128)(2,1)S(1)} collective-permute-done((bf16[3456,128]{1,0:T(8,128)(2,1)S(1)}, bf16[3456,128]{1,0:T(8,128)(2,1)S(1)}, u32[]{:S(2)}, u32[]{:S(2)}) %collective-permute-start.5) | collective-permute-done | bytes 884768 | tf_op jit(solution)/shard_map/ppermute | solution.py:483
  30.9 1.0 %shard_map.88 = bf16[3584,128]{1,0:T(8,128)(2,1)} custom-call(f32[3456,128]{1,0:T(8,128)S(1)} %get-tuple-element.35.own, bf16[3456,128]{1,0:T(8,128)(2,1)S(1)} %collective-permute-done.5.other), custom_call_target="tpu_custom_call" | custom-call | bytes 4194304 | tf_op jit(solution)/shard_map/pallas_call | solution.py:423
  31.9 7.3 %all-to-all-start = ((bf16[64,56,128]{2,1,0:T(8,128)(2,1)}), bf16[64,56,128]{2,1,0:T(8,128)(2,1)S(1)}, u32[]{:S(2)}, u32[]{:S(2)}) async-start(bf16[64,56,128]{2,1,0:T(8,128)(2,1)} %bitcast), calls=%async_computation | async-start | bytes 1835008 | tf_op jit(solution)/shard_map/all_to_all | solution.py:495
  39.1 0.9 %shard_map.89 = (bf16[128,128]{1,0:T(8,128)(2,1)S(1)}, bf16[128,128]{1,0:T(8,128)(2,1)S(1)}, bf16[128,128]{1,0:T(8,128)(2,1)S(1)}, bf16[128,128]{1,0:T(8,128)(2,1)S(1)}, bf16[256,128]{1,0:T(8,128)(2,1)S(1)}) custom-call(bf16[4,512,128]{2,1,0:T(8,128)(2,1)S(1)} %get-tuple-element.37.hidden, s32[1,4,6]{2,1,0:T(4,128)} %links_in.7), custom_call_target="tpu_custom_call" | custom-call | bytes 1048576 | tf_op jit(solution)/shard_map/pallas_call | solution.py:423
  40.0 14.8 %all-to-all-done.chunks = bf16[64,56,128]{2,1,0:T(8,128)(2,1)S(1)} async-done(((bf16[64,56,128]{2,1,0:T(8,128)(2,1)}), bf16[64,56,128]{2,1,0:T(8,128)(2,1)S(1)}, u32[]{:S(2)}, u32[]{:S(2)}) %all-to-all-start) | async-done | bytes 917536 | tf_op jit(solution)/shard_map/all_to_all | solution.py:495
  54.8 1.2 %shard_map.90 = bf16[64,56,128]{2,1,0:T(8,128)(2,1)} custom-call(bf16[64,56,128]{2,1,0:T(8,128)(2,1)S(1)} %all-to-all-done.chunks, bf16[128,128]{1,0:T(8,128)(2,1)S(1)} %get-tuple-element.38.rest_0_, bf16[128,128]{1,0:T(8,128)(2,1)S(1)} %get-tuple-element.39.rest_1_, bf16[128,128]{1,0:T(8,128)(2,1)S(1)} %get-tuple-element.40.rest_2_, ...), custom_call_target="tpu_custom_call" | custom-call | bytes 2097152 | tf_op jit(solution)/shard_map/pallas_call | solution.py:423
  56.0 5.2 %all-to-all-start.1 = ((bf16[64,56,128]{2,1,0:T(8,128)(2,1)}), bf16[64,56,128]{2,1,0:T(8,128)(2,1)S(1)}, u32[]{:S(2)}, u32[]{:S(2)}) async-start(bf16[64,56,128]{2,1,0:T(8,128)(2,1)} %shard_map.90), calls=%async_computation.1 | async-start | bytes 1835008 | tf_op jit(solution)/shard_map/all_to_all | solution.py:517
  61.2 2.6 %collective-permute-start.10 = (bf16[256,128]{1,0:T(8,128)(2,1)S(1)}, bf16[256,128]{1,0:T(8,128)(2,1)S(1)}, u32[]{:S(2)}, u32[]{:S(2)}) collective-permute-start(bf16[256,128]{1,0:T(8,128)(2,1)S(1)} %get-tuple-element.42.rest_4_), channel_id=1, source_target_pairs={{0,64},{4,68},{8,72},{12,76},{16,80},{20,84},{24,88},{28,92},{32,9... | collective-permute-start | bytes 196616 | tf_op jit(solution)/shard_map/ppermute | solution.py:56
  63.8 2.6 %collective-permute-start.6 = (bf16[128,128]{1,0:T(8,128)(2,1)S(1)}, bf16[128,128]{1,0:T(8,128)(2,1)S(1)}, u32[]{:S(2)}, u32[]{:S(2)}) collective-permute-start(bf16[128,128]{1,0:T(8,128)(2,1)S(1)} %get-tuple-element.38.rest_0_), channel_id=1, source_target_pairs={{0,4},{4,0},{8,12},{12,8},{16,20},{20,16},{24,28},{28,24},{32,36},... | collective-permute-start | bytes 98312 | tf_op jit(solution)/shard_map/ppermute | solution.py:56
  66.4 2.7 %collective-permute-start.7 = (bf16[128,128]{1,0:T(8,128)(2,1)S(1)}, bf16[128,128]{1,0:T(8,128)(2,1)S(1)}, u32[]{:S(2)}, u32[]{:S(2)}) collective-permute-start(bf16[128,128]{1,0:T(8,128)(2,1)S(1)} %get-tuple-element.39.rest_1_), channel_id=1, source_target_pairs={{0,20},{4,16},{8,28},{12,24},{16,4},{20,0},{24,12},{28,8},{32,52},... | collective-permute-start | bytes 98312 | tf_op jit(solution)/shard_map/ppermute | solution.py:56
  69.1 0.4 collective-permute-start.8
  69.5 1.1 %collective-permute-start.9 = (bf16[128,128]{1,0:T(8,128)(2,1)S(1)}, bf16[128,128]{1,0:T(8,128)(2,1)S(1)}, u32[]{:S(2)}, u32[]{:S(2)}) collective-permute-start(bf16[128,128]{1,0:T(8,128)(2,1)S(1)} %get-tuple-element.41.rest_3_), channel_id=1, source_target_pairs={{0,40},{4,44},{8,32},{12,36},{16,56},{20,60},{24,48},{28,52},{32,8... | collective-permute-start | bytes 98312 | tf_op jit(solution)/shard_map/ppermute | solution.py:56
  70.6 0.0 collective-permute-done.6.g0
  70.6 5.6 %collective-permute-done.7.g1 = bf16[128,128]{1,0:T(8,128)(2,1)S(1)} collective-permute-done((bf16[128,128]{1,0:T(8,128)(2,1)S(1)}, bf16[128,128]{1,0:T(8,128)(2,1)S(1)}, u32[]{:S(2)}, u32[]{:S(2)}) %collective-permute-start.7) | collective-permute-done | bytes 32800 | tf_op jit(solution)/shard_map/ppermute | solution.py:56
  76.2 0.0 collective-permute-done.8.g2
  76.2 0.0 collective-permute-done.9.g3
  76.2 0.0 collective-permute-done.10.g4
  76.2 4.8 %shard_map.91 = bf16[1,4,512,128]{3,2,1,0:T(8,128)(2,1)} custom-call(f32[4,512,128]{2,1,0:T(8,128)S(1)} %get-tuple-element.26.x.masked, bf16[4,512,128]{2,1,0:T(8,128)(2,1)S(1)} %get-tuple-element.37.hidden, s32[1,4,6]{2,1,0:T(4,128)} %links_in.7, s32[1,4]{1,0:T(1,128)} %occupied_in.5, bf16[27,128,128]{2,1,0:T(8,128)(2,1)} %second_in.3, ...), custom_call_target="tpu_custom_call" | custom-call | flops 3221225472 | bytes 4194304 | tf_op jit(solution)/shard_map/pallas_call | solution.py:423
  81.0 0.0 all-to-all-done.1
  81.0 0.6 collective-permute-start.11
  81.6 1.3 %shard_map.92 = (f32[3456,128]{1,0:T(8,128)}, f32[3456,128]{1,0:T(8,128)}) custom-call(bf16[3584,128]{1,0:T(8,128)(2,1)S(1)} %bitcast.5), custom_call_target="tpu_custom_call" | custom-call | bytes 3145728 | tf_op jit(solution)/shard_map/pallas_call | solution.py:423
  82.9 0.8 collective-permute-done.11.other
  83.7 1.3 %shard_map.93 = (f32[3456,128]{1,0:T(8,128)}, f32[3456,128]{1,0:T(8,128)}) custom-call(bf16[3584,128]{1,0:T(8,128)(2,1)S(1)} %collective-permute-done.11.other, f32[3456,128]{1,0:T(8,128)} %get-tuple-element.45.first_in, f32[3456,128]{1,0:T(8,128)} %get-tuple-element.46.second_in), custom_call_target="tpu_custom_call", output_to_operand_aliasing={{0}: (1, {}), {1}: (2, {})} | custom-call | bytes 3145728 | tf_op jit(solution)/shard_map/pallas_call | solution.py:423
Async XLA Ops:
  2.2 13.3 %collective-permute-start.4 = (bf16[512,128]{1,0:T(8,128)(2,1)S(1)}, bf16[512,128]{1,0:T(8,128)(2,1)S(1)}, u32[]{:S(2)}, u32[]{:S(2)}) collective-permute-start(bf16[512,128]{1,0:T(8,128)(2,1)S(1)} %get-tuple-element.34), channel_id=1, source_target_pairs={{0,64},{4,68},{8,72},{12,76},{16,80},{20,84},{24,88},{28,92},{32,9... | collective-permute-start | bytes 393224 | tf_op jit(solution)/shard_map/ppermute | solution.py:56
  6.7 7.7 %collective-permute-start = (bf16[256,128]{1,0:T(8,128)(2,1)S(1)}, bf16[256,128]{1,0:T(8,128)(2,1)S(1)}, u32[]{:S(2)}, u32[]{:S(2)}) collective-permute-start(bf16[256,128]{1,0:T(8,128)(2,1)S(1)} %get-tuple-element.30), channel_id=1, source_target_pairs={{0,4},{4,0},{8,12},{12,8},{16,20},{20,16},{24,28},{28,24},{32,36},... | collective-permute-start | bytes 196616 | tf_op jit(solution)/shard_map/ppermute | solution.py:56
  7.7 6.8 %collective-permute-start.1 = (bf16[256,128]{1,0:T(8,128)(2,1)S(1)}, bf16[256,128]{1,0:T(8,128)(2,1)S(1)}, u32[]{:S(2)}, u32[]{:S(2)}) collective-permute-start(bf16[256,128]{1,0:T(8,128)(2,1)S(1)} %get-tuple-element.31), channel_id=1, source_target_pairs={{0,20},{4,16},{8,28},{12,24},{16,4},{20,0},{24,12},{28,8},{32,52},... | collective-permute-start | bytes 196616 | tf_op jit(solution)/shard_map/ppermute | solution.py:56
  10.3 4.1 %collective-permute-start.2 = (bf16[256,128]{1,0:T(8,128)(2,1)S(1)}, bf16[256,128]{1,0:T(8,128)(2,1)S(1)}, u32[]{:S(2)}, u32[]{:S(2)}) collective-permute-start(bf16[256,128]{1,0:T(8,128)(2,1)S(1)} %get-tuple-element.32), channel_id=1, source_target_pairs={{0,8},{4,12},{8,0},{12,4},{16,24},{20,28},{24,16},{28,20},{32,40},... | collective-permute-start | bytes 196616 | tf_op jit(solution)/shard_map/ppermute | solution.py:56
  10.6 4.9 %collective-permute-start.3 = (bf16[256,128]{1,0:T(8,128)(2,1)S(1)}, bf16[256,128]{1,0:T(8,128)(2,1)S(1)}, u32[]{:S(2)}, u32[]{:S(2)}) collective-permute-start(bf16[256,128]{1,0:T(8,128)(2,1)S(1)} %get-tuple-element.33), channel_id=1, source_target_pairs={{0,40},{4,44},{8,32},{12,36},{16,56},{20,60},{24,48},{28,52},{32,8... | collective-permute-start | bytes 196616 | tf_op jit(solution)/shard_map/ppermute | solution.py:56
  27.2 3.7 %collective-permute-start.5 = (bf16[3456,128]{1,0:T(8,128)(2,1)S(1)}, bf16[3456,128]{1,0:T(8,128)(2,1)S(1)}, u32[]{:S(2)}, u32[]{:S(2)}) collective-permute-start(bf16[3456,128]{1,0:T(8,128)(2,1)S(1)} %get-tuple-element.36), channel_id=1, source_target_pairs={{0,4},{4,0},{1,5},{5,1},{2,6},{6,2},{3,7},{7,3},{8,12},{12,8},{9,1... | collective-permute-start | bytes 2654216 | tf_op jit(solution)/shard_map/ppermute | solution.py:483
  31.9 22.9 %all-to-all-start = ((bf16[64,56,128]{2,1,0:T(8,128)(2,1)}), bf16[64,56,128]{2,1,0:T(8,128)(2,1)S(1)}, u32[]{:S(2)}, u32[]{:S(2)}) async-start(bf16[64,56,128]{2,1,0:T(8,128)(2,1)} %bitcast), calls=%async_computation | async-start | bytes 1835008 | tf_op jit(solution)/shard_map/all_to_all | solution.py:495
  56.0 25.0 %all-to-all-start.1 = ((bf16[64,56,128]{2,1,0:T(8,128)(2,1)}), bf16[64,56,128]{2,1,0:T(8,128)(2,1)S(1)}, u32[]{:S(2)}, u32[]{:S(2)}) async-start(bf16[64,56,128]{2,1,0:T(8,128)(2,1)} %shard_map.90), calls=%async_computation.1 | async-start | bytes 1835008 | tf_op jit(solution)/shard_map/all_to_all | solution.py:517
  61.2 14.9 %collective-permute-start.10 = (bf16[256,128]{1,0:T(8,128)(2,1)S(1)}, bf16[256,128]{1,0:T(8,128)(2,1)S(1)}, u32[]{:S(2)}, u32[]{:S(2)}) collective-permute-start(bf16[256,128]{1,0:T(8,128)(2,1)S(1)} %get-tuple-element.42.rest_4_), channel_id=1, source_target_pairs={{0,64},{4,68},{8,72},{12,76},{16,80},{20,84},{24,88},{28,92},{32,9... | collective-permute-start | bytes 196616 | tf_op jit(solution)/shard_map/ppermute | solution.py:56
  63.8 6.7 %collective-permute-start.6 = (bf16[128,128]{1,0:T(8,128)(2,1)S(1)}, bf16[128,128]{1,0:T(8,128)(2,1)S(1)}, u32[]{:S(2)}, u32[]{:S(2)}) collective-permute-start(bf16[128,128]{1,0:T(8,128)(2,1)S(1)} %get-tuple-element.38.rest_0_), channel_id=1, source_target_pairs={{0,4},{4,0},{8,12},{12,8},{16,20},{20,16},{24,28},{28,24},{32,36},... | collective-permute-start | bytes 98312 | tf_op jit(solution)/shard_map/ppermute | solution.py:56
  66.4 9.8 %collective-permute-start.7 = (bf16[128,128]{1,0:T(8,128)(2,1)S(1)}, bf16[128,128]{1,0:T(8,128)(2,1)S(1)}, u32[]{:S(2)}, u32[]{:S(2)}) collective-permute-start(bf16[128,128]{1,0:T(8,128)(2,1)S(1)} %get-tuple-element.39.rest_1_), channel_id=1, source_target_pairs={{0,20},{4,16},{8,28},{12,24},{16,4},{20,0},{24,12},{28,8},{32,52},... | collective-permute-start | bytes 98312 | tf_op jit(solution)/shard_map/ppermute | solution.py:56
  69.1 7.1 %collective-permute-start.8 = (bf16[128,128]{1,0:T(8,128)(2,1)S(1)}, bf16[128,128]{1,0:T(8,128)(2,1)S(1)}, u32[]{:S(2)}, u32[]{:S(2)}) collective-permute-start(bf16[128,128]{1,0:T(8,128)(2,1)S(1)} %get-tuple-element.40.rest_2_), channel_id=1, source_target_pairs={{0,8},{4,12},{8,0},{12,4},{16,24},{20,28},{24,16},{28,20},{32,40},... | collective-permute-start | bytes 98312 | tf_op jit(solution)/shard_map/ppermute | solution.py:56
  69.5 6.7 %collective-permute-start.9 = (bf16[128,128]{1,0:T(8,128)(2,1)S(1)}, bf16[128,128]{1,0:T(8,128)(2,1)S(1)}, u32[]{:S(2)}, u32[]{:S(2)}) collective-permute-start(bf16[128,128]{1,0:T(8,128)(2,1)S(1)} %get-tuple-element.41.rest_3_), channel_id=1, source_target_pairs={{0,40},{4,44},{8,32},{12,36},{16,56},{20,60},{24,48},{28,52},{32,8... | collective-permute-start | bytes 98312 | tf_op jit(solution)/shard_map/ppermute | solution.py:56
  81.0 2.7 %collective-permute-start.11 = (bf16[3584,128]{1,0:T(8,128)(2,1)S(1)}, bf16[3584,128]{1,0:T(8,128)(2,1)S(1)}, u32[]{:S(2)}, u32[]{:S(2)}) collective-permute-start(bf16[3584,128]{1,0:T(8,128)(2,1)S(1)} %bitcast.4), channel_id=1, source_target_pairs={{0,4},{4,0},{1,5},{5,1},{2,6},{6,2},{3,7},{7,3},{8,12},{12,8},{9,1... | collective-permute-start | bytes 2752520 | tf_op jit(solution)/shard_map/ppermute | solution.py:530
